TPU v7x, 32 devices: a whole 2x2x4 slice. The times are simulated.
32 devices in a mesh: section: 2 (over x), seq: 16 (over z, y, core).
Axes of the slice: x: 2, y: 2, z: 4, core: 2. Of those that a mesh axis runs over, the one named last changes fastest.
Arguments:
- queries: bfloat16 [2, 2048, 3072], P('section', 'seq'), may hold values from -60 to 60
- packed_key_value: bfloat16 [2, 2048, 1024], P('section', 'seq'), may hold values from -6 to 6
- incoming: bfloat16 [2, 2048, 3072], P('section', 'seq'), may hold values from -6 to 6
- loss_grad: bfloat16 [2048, 3072], P('seq'), may hold values from -6 to 6
- global_blocks: int32 [2, 2], P('section'), may hold values from 0 to 31
- random_blocks: int32 [2, 32, 4, 3], P('section'), may hold values from 0 to 31, as said below
Outputs:
- d_queries: bfloat16 [2, 2048, 3072], P('section', 'seq')
- d_key_value: bfloat16 [2, 2048, 1024], P('section', 'seq')
Inputs may be any that keep to these rules, and one draw needn't show every extreme that they name: `random_blocks`: the random blocks of a query block lie among the blocks held by the seq index that holds the query block and the indices just before and after it.
All inputs are finite; a program needn't handle non-finite values.
Results may differ from a plain program's by a relative error of at most 0.006.
Values may be sent and summed in bfloat16 or wider, within the bound.
No kernel may reach another device: no remote copies, remote signals or barrier semaphores. Data moves between devices by JAX's collectives and lax.ppermute only.
A program may use at most 64 MiB of HBM per device.

v0:
```python
import math

import jax
import jax.numpy as jnp
from jax import lax
from jax.sharding import PartitionSpec as P

HQ = 24
KEY_HEADS = 4
HEAD_SIZE = 128
BLOCK_TOKENS = 64
GLOBAL_BLOCKS = 2
RANDOM_BLOCKS = 3
GROUP_HEADS = 6


def from_behind(shard, axis, by):
    peers = lax.axis_size(axis)
    pairs = [(i, i + by) for i in range(peers) if 0 <= i + by < peers]
    return lax.ppermute(shard, axis, pairs)


def with_halo(shard, sides, width):
    for axis, dim in sides:
        peers, length = (lax.axis_size(axis), shard.shape[dim])
        up = [(i, (i + 1) % peers) for i in range(peers - 1)]
        down = [(j, i) for i, j in up]
        last = lax.slice_in_dim(shard, length - width, length, axis=dim)
        first = lax.slice_in_dim(shard, 0, width, axis=dim)
        before = lax.ppermute(last, axis, up)
        after = lax.ppermute(first, axis, down)
        shard = jnp.concatenate([before, shard, after], axis=dim)
    return shard


def body(queries, packed_key_value, incoming, loss_grad, global_blocks, random_blocks):
    score_scale = 1.0 / math.sqrt(HEAD_SIZE)
    tok_rows = queries.shape[1]
    local_block_count = tok_rows // BLOCK_TOKENS
    width_kv = packed_key_value.shape[2]
    position = lax.axis_index("seq")
    seq_count = lax.axis_size("seq")
    every_block = local_block_count * seq_count
    shifted = from_behind(incoming, "section", -1)
    is_last = lax.axis_index("section") == lax.axis_size("section") - 1
    output_gradient = jnp.where(is_last, loss_grad, shifted[0])
    pairs_own = packed_key_value[0]
    extended = with_halo(pairs_own, (("seq", 0),), tok_rows)
    global_block_index = global_blocks[0]
    random_table = random_blocks[0]
    owners_of = global_block_index // local_block_count
    local_slot = global_block_index % local_block_count
    own_blocks = pairs_own.reshape(local_block_count, BLOCK_TOKENS, width_kv)
    pick_mask = (
        (owners_of[:, None] == position)
        & (local_slot[:, None] == jnp.arange(local_block_count, dtype=jnp.int32)[None, :])
    ).astype(jnp.float32)
    owned_rows = jnp.einsum(
        "gn,nkc->gkc", pick_mask, own_blocks.astype(jnp.float32), precision=lax.Precision.HIGHEST
    )
    glob_rows = lax.psum(owned_rows, "seq").astype(jnp.bfloat16)
    candidate_blocks = jnp.concatenate(
        [extended.reshape(3 * local_block_count, BLOCK_TOKENS, width_kv), glob_rows], 0
    )
    candidate_count = 3 * local_block_count + GLOBAL_BLOCKS
    candidate_groups = candidate_blocks.reshape(
        candidate_count, BLOCK_TOKENS, 2, KEY_HEADS, HEAD_SIZE
    ).transpose(3, 0, 1, 2, 4)
    block_ids = jnp.arange(local_block_count, dtype=jnp.int32)
    offsets = jnp.arange(-1, 2, dtype=jnp.int32)[None, :]
    global_ids = position * local_block_count + block_ids[:, None] + offsets
    usable = jnp.concatenate(
        [
            (global_ids >= 0) & (global_ids < every_block),
            jnp.ones((local_block_count, GLOBAL_BLOCKS + RANDOM_BLOCKS), dtype=bool),
        ],
        1,
    )
    key_mask = jnp.repeat(usable, BLOCK_TOKENS, axis=1)
    window_blocks = local_block_count + block_ids[:, None] + offsets
    global_slot_rows = 3 * local_block_count + jnp.arange(GLOBAL_BLOCKS, dtype=jnp.int32)
    own_random = lax.dynamic_slice_in_dim(
        random_table, position * local_block_count, local_block_count, 0
    )
    random_block_index = jnp.transpose(own_random, (1, 0, 2)) - (position - 1) * local_block_count
    key_block_index = jnp.concatenate(
        [
            jnp.broadcast_to(window_blocks[None], (KEY_HEADS, local_block_count, 3)),
            jnp.broadcast_to(
                global_slot_rows[None, None, :], (KEY_HEADS, local_block_count, GLOBAL_BLOCKS)
            ),
            random_block_index,
        ],
        2,
    )
    query_group_rows = (
        queries[0]
        .reshape(local_block_count, BLOCK_TOKENS, KEY_HEADS, GROUP_HEADS, HEAD_SIZE)
        .transpose(2, 0, 1, 3, 4)
    )
    gradient_group_rows = output_gradient.reshape(
        local_block_count, BLOCK_TOKENS, KEY_HEADS, GROUP_HEADS, HEAD_SIZE
    ).transpose(2, 0, 1, 3, 4)
    cand_range = jnp.arange(candidate_count, dtype=jnp.int32)

    def one_group(group_args):
        index_g, query_grouped, gradient_grouped, pairs_g = group_args
        selected = pairs_g[index_g]
        key_row_block = selected[:, :, :, 0].reshape(local_block_count, -1, HEAD_SIZE)
        value_row_block = selected[:, :, :, 1].reshape(local_block_count, -1, HEAD_SIZE)
        logit_scores = (
            jnp.einsum(
                "elmi,eti->emlt", query_grouped, key_row_block, preferred_element_type=jnp.float32
            )
            * score_scale
        )
        logit_scores = jnp.where(key_mask[:, None, None, :], logit_scores, -1e30)
        row_max = jnp.max(logit_scores, axis=-1, keepdims=True)
        weights_raw = jnp.exp(logit_scores - row_max)
        row_total = jnp.sum(weights_raw, axis=-1, keepdims=True)
        probs = weights_raw / row_total
        probability_lowbits = probs.astype(jnp.bfloat16)
        probability_gradient = jnp.einsum(
            "elmi,eti->emlt", gradient_grouped, value_row_block, preferred_element_type=jnp.float32
        )
        row_delta = jnp.sum(probs * probability_gradient, axis=-1, keepdims=True)
        score_gradient = (probs * (probability_gradient - row_delta) * score_scale).astype(
            jnp.bfloat16
        )
        query_gradient = jnp.einsum(
            "yzmu,yup->ymzp", score_gradient, key_row_block, preferred_element_type=jnp.float32
        )
        key_gradient = jnp.einsum(
            "xapt,xpag->xtg", score_gradient, query_grouped, preferred_element_type=jnp.float32
        )
        value_gradient = jnp.einsum(
            "xapt,xpag->xtg",
            probability_lowbits,
            gradient_grouped,
            preferred_element_type=jnp.float32,
        )
        paired = jnp.stack([key_gradient, value_gradient], 2).reshape(
            -1, BLOCK_TOKENS * 2 * HEAD_SIZE
        )
        onehot = (index_g.reshape(-1)[:, None] == cand_range[None, :]).astype(jnp.float32)
        summed = jnp.dot(onehot.T, paired, precision=lax.Precision.HIGHEST)
        stats_g = jnp.stack([row_max[..., 0], row_total[..., 0], row_delta[..., 0]], 0)
        return (query_gradient, summed, stats_g)

    grad_query_all, reduced_total, stats_all = lax.map(
        one_group, (key_block_index, query_group_rows, gradient_group_rows, candidate_groups)
    )
    d_queries = (
        grad_query_all.transpose(1, 2, 0, 3, 4)
        .reshape(tok_rows, HQ * HEAD_SIZE)
        .astype(jnp.bfloat16)
    )
    cand_grads = (
        reduced_total.reshape(KEY_HEADS, candidate_count, BLOCK_TOKENS, 2, HEAD_SIZE)
        .transpose(1, 2, 3, 0, 4)
        .reshape(candidate_count, BLOCK_TOKENS, width_kv)
    )
    glob_grads = cand_grads[3 * local_block_count :]
    shard_grads = cand_grads[: 3 * local_block_count].reshape(3 * tok_rows, width_kv)
    returned = with_halo(shard_grads, (("seq", 0),), tok_rows)
    own_grad = (
        returned[2 * tok_rows : 3 * tok_rows] + returned[:tok_rows] + returned[4 * tok_rows :]
    )
    global_sum = lax.psum(glob_grads, "seq")
    own_grad = own_grad + jnp.einsum(
        "gn,gkc->nkc", pick_mask, global_sum, precision=lax.Precision.HIGHEST
    ).reshape(tok_rows, width_kv)
    return (d_queries[None], own_grad.astype(jnp.bfloat16)[None])


def solution(mesh):
    in_specs = (
        P("section", "seq", None),
        P("section", "seq", None),
        P("section", "seq", None),
        P("seq", None),
        P("section", None),
        P("section", None, None, None),
    )
    out_specs = (P("section", "seq", None), P("section", "seq", None))
    return jax.shard_map(body, mesh=mesh, in_specs=in_specs, out_specs=out_specs, check_vma=False)
```

profile of v0, /device:TPU:11, one launch (start us, length us, event | category | flops | bytes accessed | tf_op | source)
XLA Modules:
  0.0 296.2 jit_solution(2747808551489926258)
XLA Ops:
  7.2 2.7 collective-permute-start.1
  10.0 3.0 %collective-permute-start = (bf16[128,1024]{1,0:T(8,128)(2,1)}, bf16[128,1024]{1,0:T(8,128)(2,1)}, u32[]{:S(2)}, u32[]{:S(2)}) collective-permute-start(bf16[128,1024]{1,0:T(8,128)(2,1)} %bitcast.211), channel_id=1, source_target_pairs={{0,1},{1,2},{2,3},{3,4},{4,5},{5,6},{6,7},{7,8},{8,9},{9,10},{10,1... | collective-permute-start | bytes 786440 | tf_op jit(solution)/shard_map/ppermute | solution.py:30
  13.0 2.2 collective-permute-start.2
  16.6 1.5 fusion.57
  18.1 52.1 %all-reduce.5 = bf16[2,64,1024]{2,0,1:T(2,128)(2,1)S(1)} all-reduce(f32[2,64,1024]{2,0,1:T(2,128)S(1)} %fusion.57), channel_id=1, replica_groups=mesh['section'=2,'seq'=16] {'seq'}, use_global_device_ids=true, to_apply=%region_0.1 | all-reduce | flops 131072 | bytes 786432 | tf_op jit(solution)/shard_map/psum | solution.py:61
  78.1 96.2 %while.13 = (s32[]{:T(128)}, bf16[4,2,64,6,128]{4,2,3,1,0:T(8,128)(2,1)}, f32[4,8,16384]{2,1,0:T(8,128)}, bf16[4,8,64,2,128]{4,2,3,1,0:T(8,128)(2,1)}, s32[4,2,8...) while((s32[]{:T(128)}, ...), condition=%wide.region_5.6_spmd.clone, body=%wide.region_1.5_spmd.clone.sunk | while | flops 638457280 | bytes 29743888 | solution.py:150
  80.6 2.6 fusion.104
  83.2 6.3 %fusion.105 = bf16[4,2,64,6,128]{4,2,3,1,0:T(8,128)(2,1)} fusion(bf16[4,2,64,6,128]{4,2,3,1,0:T(8,128)(2,1)} %get-tuple-element.193, s32[]{:T(128)S(6)} %copy.79, bf16[2,512,128,1]{2,1,3,0:T(8,128)(2,1)S(1)} %bitcast.203, f32[2,512,64,6]{1,2,3,0:T(8,128)S(1)} %fusion.103, f32[2,6,64,512]{3,2,1,0:T(8,128)} %get-tuple-element.180, ...), kind=kOutput, calls=%fused_computation.20.clone.1 | convolution fusion | flops 103417088 | bytes 6963204 | tf_op jit(solution)/shard_map/while/body/eval_jaxpr/yzmu,yup->ymzp/dot_general | solution.py:130
  89.6 2.7 convolution_bitcast_fusion.6
  92.3 6.8 %convolution_bitcast_fusion.7 = f32[2,512,1,128]{3,1,0,2:T(8,128)S(1)} fusion(f32[2,512,64,6]{1,2,3,0:T(8,128)S(1)} %fusion.103, bf16[4,2,64,6,128]{4,2,3,1,0:T(8,128)(2,1)} %get-tuple-element.206, s32[]{:T(128)S(6)} %copy.79, f32[2,6,64,512]{3,2,1,0:T(8,128)} %get-tuple-element.180, f32[2,6,64]{2,1,0:T(8,128)S(1)} %get-tuple-element.181), kind=kOutput, calls=%fused_computation.18.clone.1 | convolution fusion | flops 103417088 | bytes 7028740 | tf_op jit(solution)/shard_map/while/body/eval_jaxpr/xapt,xpag->xtg/dot_general | solution.py:133
  104.6 2.6 fusion.104
  107.2 6.4 %fusion.105 = bf16[4,2,64,6,128]{4,2,3,1,0:T(8,128)(2,1)} fusion(bf16[4,2,64,6,128]{4,2,3,1,0:T(8,128)(2,1)} %get-tuple-element.193, s32[]{:T(128)S(6)} %copy.79, bf16[2,512,128,1]{2,1,3,0:T(8,128)(2,1)S(1)} %bitcast.203, f32[2,512,64,6]{1,2,3,0:T(8,128)S(1)} %fusion.103, f32[2,6,64,512]{3,2,1,0:T(8,128)} %get-tuple-element.180, ...), kind=kOutput, calls=%fused_computation.20.clone.1 | convolution fusion | flops 103417088 | bytes 6963204 | tf_op jit(solution)/shard_map/while/body/eval_jaxpr/yzmu,yup->ymzp/dot_general | solution.py:130
  113.6 2.7 convolution_bitcast_fusion.6
  116.3 6.8 %convolution_bitcast_fusion.7 = f32[2,512,1,128]{3,1,0,2:T(8,128)S(1)} fusion(f32[2,512,64,6]{1,2,3,0:T(8,128)S(1)} %fusion.103, bf16[4,2,64,6,128]{4,2,3,1,0:T(8,128)(2,1)} %get-tuple-element.206, s32[]{:T(128)S(6)} %copy.79, f32[2,6,64,512]{3,2,1,0:T(8,128)} %get-tuple-element.180, f32[2,6,64]{2,1,0:T(8,128)S(1)} %get-tuple-element.181), kind=kOutput, calls=%fused_computation.18.clone.1 | convolution fusion | flops 103417088 | bytes 7028740 | tf_op jit(solution)/shard_map/while/body/eval_jaxpr/xapt,xpag->xtg/dot_general | solution.py:133
  124.9 1.4 fusion.106
  128.6 2.7 fusion.104
  131.2 6.3 %fusion.105 = bf16[4,2,64,6,128]{4,2,3,1,0:T(8,128)(2,1)} fusion(bf16[4,2,64,6,128]{4,2,3,1,0:T(8,128)(2,1)} %get-tuple-element.193, s32[]{:T(128)S(6)} %copy.79, bf16[2,512,128,1]{2,1,3,0:T(8,128)(2,1)S(1)} %bitcast.203, f32[2,512,64,6]{1,2,3,0:T(8,128)S(1)} %fusion.103, f32[2,6,64,512]{3,2,1,0:T(8,128)} %get-tuple-element.180, ...), kind=kOutput, calls=%fused_computation.20.clone.1 | convolution fusion | flops 103417088 | bytes 6963204 | tf_op jit(solution)/shard_map/while/body/eval_jaxpr/yzmu,yup->ymzp/dot_general | solution.py:130
  137.6 2.7 convolution_bitcast_fusion.6
  140.3 6.8 %convolution_bitcast_fusion.7 = f32[2,512,1,128]{3,1,0,2:T(8,128)S(1)} fusion(f32[2,512,64,6]{1,2,3,0:T(8,128)S(1)} %fusion.103, bf16[4,2,64,6,128]{4,2,3,1,0:T(8,128)(2,1)} %get-tuple-element.206, s32[]{:T(128)S(6)} %copy.79, f32[2,6,64,512]{3,2,1,0:T(8,128)} %get-tuple-element.180, f32[2,6,64]{2,1,0:T(8,128)S(1)} %get-tuple-element.181), kind=kOutput, calls=%fused_computation.18.clone.1 | convolution fusion | flops 103417088 | bytes 7028740 | tf_op jit(solution)/shard_map/while/body/eval_jaxpr/xapt,xpag->xtg/dot_general | solution.py:133
  148.9 1.4 fusion.106
  152.6 2.6 fusion.104
  155.3 6.3 %fusion.105 = bf16[4,2,64,6,128]{4,2,3,1,0:T(8,128)(2,1)} fusion(bf16[4,2,64,6,128]{4,2,3,1,0:T(8,128)(2,1)} %get-tuple-element.193, s32[]{:T(128)S(6)} %copy.79, bf16[2,512,128,1]{2,1,3,0:T(8,128)(2,1)S(1)} %bitcast.203, f32[2,512,64,6]{1,2,3,0:T(8,128)S(1)} %fusion.103, f32[2,6,64,512]{3,2,1,0:T(8,128)} %get-tuple-element.180, ...), kind=kOutput, calls=%fused_computation.20.clone.1 | convolution fusion | flops 103417088 | bytes 6963204 | tf_op jit(solution)/shard_map/while/body/eval_jaxpr/yzmu,yup->ymzp/dot_general | solution.py:130
  161.6 2.7 convolution_bitcast_fusion.6
  164.3 6.8 %convolution_bitcast_fusion.7 = f32[2,512,1,128]{3,1,0,2:T(8,128)S(1)} fusion(f32[2,512,64,6]{1,2,3,0:T(8,128)S(1)} %fusion.103, bf16[4,2,64,6,128]{4,2,3,1,0:T(8,128)(2,1)} %get-tuple-element.206, s32[]{:T(128)S(6)} %copy.79, f32[2,6,64,512]{3,2,1,0:T(8,128)} %get-tuple-element.180, f32[2,6,64]{2,1,0:T(8,128)S(1)} %get-tuple-element.181), kind=kOutput, calls=%fused_computation.18.clone.1 | convolution fusion | flops 103417088 | bytes 7028740 | tf_op jit(solution)/shard_map/while/body/eval_jaxpr/xapt,xpag->xtg/dot_general | solution.py:133
  172.9 1.4 fusion.106
  174.3 2.9 copy.70
  177.9 7.1 %collective-permute-start.4 = (f32[128,1024]{1,0:T(8,128)S(1)}, f32[128,1024]{1,0:T(8,128)}, u32[]{:S(2)}, u32[]{:S(2)}) collective-permute-start(f32[128,1024]{1,0:T(8,128)S(1)} %slice.40), channel_id=1, source_target_pairs={{1,0},{2,1},{3,2},{4,3},{5,4},{6,5},{7,6},{8,7},{9,8},{10,9},{11,1... | collective-permute-start | bytes 1572872 | tf_op jit(solution)/shard_map/ppermute | solution.py:31
  185.2 2.1 collective-permute-start.3
  189.2 1.7 convert_element_type.34
  191.2 93.8 %all-reduce.4.cloned.1.call-done = f32[2,64,1024]{2,0,1:T(2,128)} async-done(((f32[2,64,1024]{2,0,1:T(2,128)}), f32[2,64,1024]{2,0,1:T(2,128)}) %all-reduce.4.cloned.1.call-update) | async-done | bytes 524304 | tf_op jit(solution)/shard_map/psum | solution.py:169
  285.0 2.1 fusion.60
  287.3 2.1 fusion.56
  (110 shorter events, 29.9 us)
Async XLA Ops:
  7.2 63.0 %copy-start = (s32[1,32,4,3]{1,2,3,0:T(4,128)S(1)}, s32[1,32,4,3]{1,2,3,0:T(4,128)}, u32[]{:S(2)}) copy-start(s32[1,32,4,3]{1,2,3,0:T(4,128)} %param.13) | copy-start | bytes 4612
  7.2 64.0 %copy-start.1 = (bf16[1,128,3072]{2,1,0:T(8,128)(2,1)S(1)}, bf16[1,128,3072]{2,1,0:T(8,128)(2,1)}, u32[]{:S(2)}) copy-start(bf16[1,128,3072]{2,1,0:T(8,128)(2,1)} %param.8) | copy-start | bytes 2359300
  7.2 277.8 %all-reduce.4.cloned.1.call-start = ((), (), s32[]{:S(2)}) async-start(), calls=%async_computation | async-start | bytes 1048576 | tf_op jit(solution)/shard_map/psum | solution.py:169
  7.2 66.2 %collective-permute-start.1 = (bf16[128,1024]{1,0:T(8,128)(2,1)}, bf16[128,1024]{1,0:T(8,128)(2,1)S(1)}, u32[]{:S(2)}, u32[]{:S(2)}) collective-permute-start(bf16[128,1024]{1,0:T(8,128)(2,1)} %bitcast.210), channel_id=1, source_target_pairs={{1,0},{2,1},{3,2},{4,3},{5,4},{6,5},{7,6},{8,7},{9,8},{10,9},{11,1... | collective-permute-start | bytes 786440 | tf_op jit(solution)/shard_map/ppermute | solution.py:31
  10.0 63.4 %collective-permute-start = (bf16[128,1024]{1,0:T(8,128)(2,1)}, bf16[128,1024]{1,0:T(8,128)(2,1)}, u32[]{:S(2)}, u32[]{:S(2)}) collective-permute-start(bf16[128,1024]{1,0:T(8,128)(2,1)} %bitcast.211), channel_id=1, source_target_pairs={{0,1},{1,2},{2,3},{3,4},{4,5},{5,6},{6,7},{7,8},{8,9},{9,10},{10,1... | collective-permute-start | bytes 786440 | tf_op jit(solution)/shard_map/ppermute | solution.py:30
  13.0 63.7 %collective-permute-start.2 = (bf16[1,128,3072]{2,1,0:T(8,128)(2,1)}, bf16[1,128,3072]{2,1,0:T(8,128)(2,1)S(1)}, u32[]{:S(2)}, u32[]{:S(2)}) collective-permute-start(bf16[1,128,3072]{2,1,0:T(8,128)(2,1)} %param.10), channel_id=1, source_target_pairs={{16,0},{17,1},{18,2},{19,3},{20,4},{21,5},{22,6},{23,7},{24,8},{25... | collective-permute-start | bytes 2359304 | tf_op jit(solution)/shard_map/ppermute | solution.py:20
  71.1 2.3 copy-start.4
  75.0 1.7 copy-start.2
  177.9 109.4 %collective-permute-start.4 = (f32[128,1024]{1,0:T(8,128)S(1)}, f32[128,1024]{1,0:T(8,128)}, u32[]{:S(2)}, u32[]{:S(2)}) collective-permute-start(f32[128,1024]{1,0:T(8,128)S(1)} %slice.40), channel_id=1, source_target_pairs={{1,0},{2,1},{3,2},{4,3},{5,4},{6,5},{7,6},{8,7},{9,8},{10,9},{11,1... | collective-permute-start | bytes 1572872 | tf_op jit(solution)/shard_map/ppermute | solution.py:31
  185.0 3.6 %copy-start.3 = (bf16[4,2,64,6,128]{4,2,3,1,0:T(8,128)(2,1)S(1)}, bf16[4,2,64,6,128]{4,2,3,1,0:T(8,128)(2,1)}, u32[]{:S(2)}) copy-start(bf16[4,2,64,6,128]{4,2,3,1,0:T(8,128)(2,1)} %get-tuple-element.50) | copy-start | bytes 2359300
  185.2 102.0 %collective-permute-start.3 = (f32[128,1024]{1,0:T(8,128)S(1)}, f32[128,1024]{1,0:T(8,128)}, u32[]{:S(2)}, u32[]{:S(2)}) collective-permute-start(f32[128,1024]{1,0:T(8,128)S(1)} %slice.38), channel_id=1, source_target_pairs={{0,1},{1,2},{2,3},{3,4},{4,5},{5,6},{6,7},{7,8},{8,9},{9,10},{10,1... | collective-permute-start | bytes 1572872 | tf_op jit(solution)/shard_map/ppermute | solution.py:30
Sparse Core Ops, SparseCore 0:
  188.7 96.2 all-reduce.3
where the time goes:
time: 299 us; the launch traced here: 296 us
  waiting for transfers between devices  93.9 us (31%)
  matrix products  84.4 us (28%)
  blocking collectives  52.1 us (17%)
  local copies, waits for them, and re-layouts  28.2 us (9%)
  starting transfers between devices  17.2 us (6%)
  between operations  14.3 us (5%)
  other arithmetic  5.56 us (2%)
    psum x1, waiting for transfers between devices, body(): global_sum = lax.psum(glob_grads, 'seq')  93.8 us
    psum x1, blocking collectives, body(): glob_rows = lax.psum(owned_rows, 'seq').astype(jnp.bfloat16)  52.1 us
    dot_general x4, matrix products, one_group(): jnp.einsum('xapt,xpag->xtg', score_gradient, query_grouped, preferred_ele...  27.1 us
    dot_general x4, matrix products, one_group(): jnp.einsum('yzmu,yup->ymzp', score_gradient, key_row_block, preferred_ele...  25.4 us
    dot_general x4, matrix products, one_group(): jnp.einsum('xapt,xpag->xtg', probability_lowbits, gradient_grouped, prefe...  10.9 us
    sub x4, matrix products, one_group(): weights_raw = jnp.exp(logit_scores - row_max)  10.6 us
    ppermute x2, starting transfers between devices, with_halo(): after = lax.ppermute(first, axis, down)  9.81 us
  transfers between devices with their start and end apart: 6, of which 1 were waited for; matrix products, arithmetic and copies ran while one was open for 5% of the time, Pallas kernels for 0%

commit v1 on v0

v1 whole, which is shorter than its diff:
```python
import functools
import math

import jax
import jax.numpy as jnp
from jax import lax
from jax.experimental import pallas as pl
from jax.experimental.pallas import tpu as pltpu
from jax.sharding import PartitionSpec as P

HQ = 24
KEY_HEADS = 4
HEAD_SIZE = 128
BLOCK_TOKENS = 64
GLOBAL_BLOCKS = 2
GROUP_HEADS = 6
SCALE = 1.0 / math.sqrt(HEAD_SIZE)
LOG2E = math.log2(math.e)
NEG = -1e30
NT = (((1,), (1,)), ((), ()))
NN = (((1,), (0,)), ((), ()))
TN = (((0,), (0,)), ((), ()))


def dot(a, b, dims):
    return lax.dot_general(a, b, dims, preferred_element_type=jnp.float32)


def exchange(x, pairs):
    return lax.ppermute(x, "seq", pairs)


def attention_kernel(
    flag_ref,
    bias_ref,
    q_ref,
    shifted_ref,
    loss_ref,
    own_k, own_v, on_k, on_v, off_k, off_v, glob_k, glob_v,
    dq_ref,
    g_own,
    g_on,
    g_off,
    g_glob,
):
    g = pl.program_id(0)
    toks = q_ref.shape[0]
    nb = toks // BLOCK_TOKENS
    rows_e = GROUP_HEADS * BLOCK_TOKENS
    ncand = bias_ref.shape[1] // KEY_HEADS

    def rows_of(ref):
        parts = [
            ref[e * BLOCK_TOKENS : (e + 1) * BLOCK_TOKENS, h * HEAD_SIZE : (h + 1) * HEAD_SIZE]
            for e in range(nb)
            for h in range(GROUP_HEADS)
        ]
        return jnp.concatenate(parts, 0)

    qg = rows_of(q_ref)
    dog = jnp.where(flag_ref[0] == 1, rows_of(loss_ref), rows_of(shifted_ref))
    keys = jnp.concatenate([own_k[...], on_k[...], off_k[...], glob_k[...]], 0)
    vals = jnp.concatenate([own_v[...], on_v[...], off_v[...], glob_v[...]], 0)
    dq_cols = []
    p_cols = []
    ds_cols = []
    for e in range(nb):
        q_e = qg[e * rows_e : (e + 1) * rows_e]
        do_e = dog[e * rows_e : (e + 1) * rows_e]
        s = dot(keys, q_e, NT)
        dp = dot(vals, do_e, NT)
        t = jnp.concatenate(
            [
                s[j * BLOCK_TOKENS : (j + 1) * BLOCK_TOKENS] * (SCALE * LOG2E)
                + bias_ref[e, g * ncand + j]
                for j in range(ncand)
            ],
            0,
        )
        m = jnp.max(t, axis=0, keepdims=True)
        w = jnp.exp2(t - m)
        inv = 1.0 / jnp.sum(w, axis=0, keepdims=True)
        p = w * inv
        delta = jnp.sum(p * dp, axis=0, keepdims=True)
        p_cols.append(p.astype(jnp.bfloat16))
        ds_cols.append((p * (dp - delta) * SCALE).astype(jnp.bfloat16))
    p_half = jnp.concatenate(p_cols, 1)
    ds_half = jnp.concatenate(ds_cols, 1)
    dq = dot(keys, ds_half, TN).T
    for e in range(nb):
        for h in range(GROUP_HEADS):
            r = e * rows_e + h * BLOCK_TOKENS
            dq_ref[e * BLOCK_TOKENS : (e + 1) * BLOCK_TOKENS, h * HEAD_SIZE : (h + 1) * HEAD_SIZE] = (
                dq[r : r + BLOCK_TOKENS].astype(dq_ref.dtype)
            )
    for i, grad in enumerate((dot(ds_half, qg, NN), dot(p_half, dog, NN))):
        g_own[i] = grad[:toks]
        g_on[i] = grad[toks : 2 * toks].astype(g_on.dtype)
        g_off[i] = grad[2 * toks : 3 * toks].astype(g_off.dtype)
        for b in range(GLOBAL_BLOCKS):
            r = 3 * toks + b * BLOCK_TOKENS
            g_glob[b, i] = grad[r : r + BLOCK_TOKENS].astype(g_glob.dtype)


def attention(flag, bias, queries, shifted, loss, own, on, off, glob):
    toks = queries.shape[0]
    bf = jnp.bfloat16
    wide = pl.BlockSpec((toks, GROUP_HEADS * HEAD_SIZE), lambda g: (0, g))
    k_of = pl.BlockSpec((toks, HEAD_SIZE), lambda g: (0, g))
    v_of = pl.BlockSpec((toks, HEAD_SIZE), lambda g: (0, g + KEY_HEADS))
    glob_rows = GLOBAL_BLOCKS * BLOCK_TOKENS
    gk_of = pl.BlockSpec((glob_rows, HEAD_SIZE), lambda g: (0, g))
    gv_of = pl.BlockSpec((glob_rows, HEAD_SIZE), lambda g: (0, g + KEY_HEADS))
    smem = pl.BlockSpec(memory_space=pltpu.SMEM)
    width = KEY_HEADS * HEAD_SIZE
    pair = pl.BlockSpec((2, toks, HEAD_SIZE), lambda g: (0, 0, g))
    quad = pl.BlockSpec((GLOBAL_BLOCKS, 2, BLOCK_TOKENS, HEAD_SIZE), lambda g: (0, 0, 0, g))
    return pl.pallas_call(
        attention_kernel,
        grid=(KEY_HEADS,),
        in_specs=[smem, smem, wide, wide, wide, k_of, v_of, k_of, v_of, k_of, v_of, gk_of, gv_of],
        out_specs=[wide, pair, pair, pair, quad],
        out_shape=[
            jax.ShapeDtypeStruct((toks, HQ * HEAD_SIZE), bf),
            jax.ShapeDtypeStruct((2, toks, width), jnp.float32),
            jax.ShapeDtypeStruct((2, toks, width), bf),
            jax.ShapeDtypeStruct((2, toks, width), bf),
            jax.ShapeDtypeStruct((GLOBAL_BLOCKS, 2, BLOCK_TOKENS, width), bf),
        ],
        compiler_params=pltpu.CompilerParams(vmem_limit_bytes=40 << 20),
        name="attention",
    )(flag, bias, queries, shifted, loss, own, own, on, on, off, off, glob, glob)


def finish_kernel(where_ref, g_own, r_on, r_off, r_glob, out_ref):
    toks = g_own.shape[1]
    nb = toks // BLOCK_TOKENS
    width = g_own.shape[2]
    for i in range(2):
        for s in range(nb):
            rows = slice(s * BLOCK_TOKENS, (s + 1) * BLOCK_TOKENS)
            total = (
                g_own[i, rows] + r_on[i, rows].astype(jnp.float32) + r_off[i, rows].astype(jnp.float32)
            )
            for b in range(GLOBAL_BLOCKS):
                total = total + jnp.where(
                    where_ref[b] == s, r_glob[b, i].astype(jnp.float32), 0.0
                )
            out_ref[rows, i * width : (i + 1) * width] = total.astype(out_ref.dtype)


def finish(where, g_own, r_on, r_off, r_glob):
    toks, width = g_own.shape[1:]
    vmem = pl.BlockSpec(memory_space=pltpu.VMEM)
    return pl.pallas_call(
        finish_kernel,
        in_specs=[pl.BlockSpec(memory_space=pltpu.SMEM)] + [vmem] * 4,
        out_specs=vmem,
        out_shape=jax.ShapeDtypeStruct((toks, 2 * width), jnp.bfloat16),
        name="finish",
    )(where, g_own, r_on, r_off, r_glob)


def body(queries, packed_key_value, incoming, loss_grad, global_blocks, random_blocks):
    toks = queries.shape[1]
    nb = toks // BLOCK_TOKENS
    sections = lax.axis_size("section")
    peers = lax.axis_size("seq")
    bits = peers.bit_length() - 1
    assert peers == 1 << bits and bits >= 1
    pos = lax.axis_index("seq")
    core = pos % 2
    is_last = lax.axis_index("section") == sections - 1

    twin = [(i, i ^ 1) for i in range(peers)]
    side = [(i, i + 1) for i in range(1, peers - 1, 2)]
    side = side + [(j, i) for i, j in side]
    orders = (list(range(1, bits)), list(range(2, bits)) + [1])
    hops = [
        [(i, i ^ (1 << orders[i % 2][r])) for i in range(peers)] for r in range(bits - 1)
    ]

    shifted = lax.ppermute(incoming[0], "section", [(i, i - 1) for i in range(1, sections)])
    own = packed_key_value[0]
    on = exchange(own, twin)
    off = exchange(own, side)

    glob_ids = global_blocks[0]
    owner = glob_ids // nb
    slot = glob_ids % nb
    mine_owner = jnp.where(core == 0, owner[0], owner[1])
    mine_slot = jnp.where(core == 0, slot[0], slot[1])
    row = mine_slot * BLOCK_TOKENS
    from_own = lax.dynamic_slice_in_dim(own, row, BLOCK_TOKENS, 0)
    from_on = lax.dynamic_slice_in_dim(on, row, BLOCK_TOKENS, 0)
    held = jnp.where(mine_owner == pos, from_own, jnp.where(mine_owner == pos + 1 - 2 * core, from_on, 0))
    for hop in hops:
        held = held + exchange(held, hop)
    other = exchange(held, twin)
    glob = jnp.where(core == 0, jnp.concatenate([held, other], 0), jnp.concatenate([other, held], 0))

    on_pos = pos + 1 - 2 * core
    off_pos = pos - 1 + 2 * core
    step = jnp.arange(nb, dtype=jnp.int32)
    cand_ids = jnp.concatenate([pos * nb + step, on_pos * nb + step, off_pos * nb + step])
    block_ids = pos * nb + step
    own_random = lax.dynamic_slice_in_dim(random_blocks[0], pos * nb, nb, 0)
    listed = jnp.sum(
        (own_random[:, :, None, :] == cand_ids[None, None, :, None]).astype(jnp.float32), -1
    )
    inside = (cand_ids >= 0) & (cand_ids < peers * nb)
    window = (jnp.abs(cand_ids[None, :] - block_ids[:, None]) <= 1) & inside[None, :]
    times = listed + window[:, None, :].astype(jnp.float32)
    bias = jnp.where(times > 0, jnp.log2(jnp.maximum(times, 1.0)), NEG)
    bias = jnp.concatenate([bias, jnp.zeros((nb, KEY_HEADS, GLOBAL_BLOCKS), jnp.float32)], 2)
    bias = bias.reshape(nb, -1)
    flag = is_last.astype(jnp.int32).reshape(1)

    dq, g_own, g_on, g_off, g_glob = attention(
        flag, bias, queries[0], shifted, loss_grad, own, on, off, glob
    )

    keep = jnp.where(core == 0, g_glob[0], g_glob[1])
    give = jnp.where(core == 0, g_glob[1], g_glob[0])
    total = keep.astype(jnp.float32) + exchange(give, twin).astype(jnp.float32)
    for hop in hops:
        total = total + exchange(total.astype(jnp.bfloat16), hop).astype(jnp.float32)
    half = total.astype(jnp.bfloat16)
    half_other = exchange(half, twin)
    r_glob = jnp.where(core == 0, jnp.stack([half, half_other]), jnp.stack([half_other, half]))
    r_on = exchange(g_on, twin)
    r_off = exchange(g_off, side)
    where = jnp.where(owner == pos, slot, -1).astype(jnp.int32)
    out = finish(where, g_own, r_on, r_off, r_glob)
    return (dq[None], out[None])


def solution(mesh):
    in_specs = (
        P("section", "seq", None),
        P("section", "seq", None),
        P("section", "seq", None),
        P("seq", None),
        P("section", None),
        P("section", None, None, None),
    )
    out_specs = (P("section", "seq", None), P("section", "seq", None))
    return jax.shard_map(body, mesh=mesh, in_specs=in_specs, out_specs=out_specs, check_vma=False)
```

time: 299 us -> 69.9 us (0.23)
  matrix products: 84.4 us -> 0 us
  waiting for transfers between devices: 93.9 us -> 25.5 us
  blocking collectives: 52.1 us -> 0 us
  local copies, waits for them, and re-layouts: 28.2 us -> 2.26 us
  Pallas kernels: 0 us -> 10.9 us
  between operations: 14.3 us -> 3.43 us
  starting transfers between devices: 17.2 us -> 24.6 us
    psum x1 -> x0, waiting for transfers between devices: 93.8 us -> none  [body(): global_sum = lax.psum(glob_grads, 'seq')]
    dot_general x22 -> x0, matrix products: 73.8 us -> none  [the longest x4 27.1 us: one_group(): jnp.einsum('xapt,xpag->xtg', score_gradient, query_grouped, preferred_ele...]
    psum x1 -> x0, blocking collectives: 52.1 us -> none  [body(): glob_rows = lax.psum(owned_rows, 'seq').astype(jnp.bfloat16)]
    ppermute x5 -> x14, waiting for transfers between devices: 0.01 us -> 25.5 us  [the longest x13 25.5 us: exchange(): return lax.ppermute(x, 'seq', pairs)]
    pallas_call x0 -> x2, Pallas kernels: none -> 10.9 us  [the longest x1 8.7 us: attention(): pl.pallas_call(attention_kernel, grid=(KEY_HEADS,), in_specs=[smem, smem,...]
    sub x4 -> x0, matrix products: 10.6 us -> none  [one_group(): weights_raw = jnp.exp(logit_scores - row_max)]
    ppermute x5 -> x14, starting transfers between devices: 17.2 us -> 24.6 us  [the longest x13 22.4 us: exchange(): return lax.ppermute(x, 'seq', pairs)]
    reshape x6 -> x1, local copies, waits for them, and re-layouts: 7.25 us -> 0.08 us  [body(): bias = bias.reshape(nb, -1)]
  transfers between devices with their start and end apart: 6 -> 14, of which waited for: 1 -> 9; matrix products, arithmetic and copies ran while one was open for 5% -> 5% of each run, Pallas kernels for 0% -> 0%
where the time goes in v1:
time: 69.9 us; the launch traced here: 69.6 us
  waiting for transfers between devices  25.5 us (36%)
  starting transfers between devices  24.6 us (35%)
  Pallas kernels  10.9 us (16%)
  between operations  3.43 us (5%)
  other arithmetic  3.02 us (4%)
  local copies, waits for them, and re-layouts  2.26 us (3%)
    ppermute x13, waiting for transfers between devices, exchange(): return lax.ppermute(x, 'seq', pairs)  25.5 us
    ppermute x13, starting transfers between devices, exchange(): return lax.ppermute(x, 'seq', pairs)  22.4 us
    pallas_call x1, Pallas kernels, attention(): pl.pallas_call(attention_kernel, grid=(KEY_HEADS,), in_specs=[smem, smem,...  8.7 us
    ppermute x1, starting transfers between devices, body(): lax.ppermute(incoming[0], 'section', [(i, i - 1) for i in range(1, sectio...  2.21 us
    pallas_call x1, Pallas kernels, finish(): pl.pallas_call(finish_kernel, in_specs=[pl.BlockSpec(memory_space=pltpu.S...  2.16 us
  transfers between devices with their start and end apart: 14, of which 9 were waited for; matrix products, arithmetic and copies ran while one was open for 5% of the time, Pallas kernels for 0%

profile of v1, /device:TPU:11, one launch (start us, length us, event | category | flops | bytes accessed | tf_op | source)
XLA Modules:
  0.0 69.6 jit_solution(15390063994754408841)
XLA Ops:
  0.6 3.7 %collective-permute-start.2 = (bf16[128,1024]{1,0:T(8,128)(2,1)}, bf16[128,1024]{1,0:T(8,128)(2,1)S(1)}, u32[]{:S(2)}, u32[]{:S(2)}) collective-permute-start(bf16[128,1024]{1,0:T(8,128)(2,1)} %bitcast.45), channel_id=1, source_target_pairs={{1,2},{3,4},{5,6},{7,8},{9,10},{11,12},{13,14},{2,1},{4,3},{6,5},{... | collective-permute-start | bytes 786440 | tf_op jit(solution)/shard_map/ppermute | solution.py:30
  4.4 2.2 %collective-permute-start = (bf16[128,3072]{1,0:T(8,128)(2,1)}, bf16[128,3072]{1,0:T(8,128)(2,1)S(1)}, u32[]{:S(2)}, u32[]{:S(2)}) collective-permute-start(bf16[128,3072]{1,0:T(8,128)(2,1)} %bitcast.53), channel_id=1, source_target_pairs={{16,0},{17,1},{18,2},{19,3},{20,4},{21,5},{22,6},{23,7},{24,8},{25... | collective-permute-start | bytes 2359304 | tf_op jit(solution)/shard_map/ppermute | solution.py:183
  6.7 0.6 copy-done.7
  7.3 0.6 compare_select_fusion
  7.9 0.6 fusion.3
  11.1 1.0 %bitcast_select_fusion = bf16[64,1024]{1,0:T(8,128)(2,1)S(1)} fusion(bf16[128,1024]{1,0:T(8,128)(2,1)S(1)} %collective-permute-done.1.on_k.on_v, s32[]{:T(128)S(6)} %select_n.96, bf16[1,128,1024]{2,1,0:T(8,128)(2,1)} %param.7, pred[]{:T(512)S(6)} %eq.49, pred[]{:T(512)S(6)} %eq.48), kind=kLoop, calls=%fused_computation.8 | loop fusion | flops 131072 | bytes 393222 | tf_op jit(solution)/shard_map/jit(_where)/select_n | solution.py:196
  12.2 0.2 collective-permute-start.3
  12.5 3.9 %collective-permute-done.3 = bf16[64,1024]{1,0:T(8,128)(2,1)S(1)} collective-permute-done((bf16[64,1024]{1,0:T(8,128)(2,1)S(1)}, bf16[64,1024]{1,0:T(8,128)(2,1)S(1)}, u32[]{:S(2)}, u32[]{:S(2)}) %collective-permute-start.3) | collective-permute-done | bytes 131104 | tf_op jit(solution)/shard_map/ppermute | solution.py:30
  16.4 2.4 %collective-permute-start.4 = (bf16[64,1024]{1,0:T(8,128)(2,1)S(1)}, bf16[64,1024]{1,0:T(8,128)(2,1)S(1)}, u32[]{:S(2)}, u32[]{:S(2)}) collective-permute-start(bf16[64,1024]{1,0:T(8,128)(2,1)S(1)} %add.104), channel_id=1, source_target_pairs={{0,4},{1,9},{2,6},{3,11},{4,0},{5,13},{6,2},{7,15},{8,12},{9,1},{1... | collective-permute-start | bytes 393224 | tf_op jit(solution)/shard_map/ppermute | solution.py:30
  18.8 3.1 %collective-permute-done.4 = bf16[64,1024]{1,0:T(8,128)(2,1)S(1)} collective-permute-done((bf16[64,1024]{1,0:T(8,128)(2,1)S(1)}, bf16[64,1024]{1,0:T(8,128)(2,1)S(1)}, u32[]{:S(2)}, u32[]{:S(2)}) %collective-permute-start.4) | collective-permute-done | bytes 131104 | tf_op jit(solution)/shard_map/ppermute | solution.py:30
  22.0 0.6 collective-permute-start.5
  22.7 0.1 copy.11
  22.8 0.1 convert_reduce_fusion
  22.9 3.0 %collective-permute-done.5 = bf16[64,1024]{1,0:T(8,128)(2,1)S(1)} collective-permute-done((bf16[64,1024]{1,0:T(8,128)(2,1)S(1)}, bf16[64,1024]{1,0:T(8,128)(2,1)S(1)}, u32[]{:S(2)}, u32[]{:S(2)}) %collective-permute-start.5) | collective-permute-done | bytes 131104 | tf_op jit(solution)/shard_map/ppermute | solution.py:30
  25.9 4.1 %collective-permute-start.6 = (bf16[64,1024]{1,0:T(8,128)(2,1)S(1)}, bf16[64,1024]{1,0:T(8,128)(2,1)S(1)}, u32[]{:S(2)}, u32[]{:S(2)}) collective-permute-start(bf16[64,1024]{1,0:T(8,128)(2,1)S(1)} %add.106), channel_id=1, source_target_pairs={{0,1},{1,0},{2,3},{3,2},{4,5},{5,4},{6,7},{7,6},{8,9},{9,8},{10,11... | collective-permute-start | bytes 393224 | tf_op jit(solution)/shard_map/ppermute | solution.py:30
  30.2 0.9 %collective-permute-done.6 = bf16[64,1024]{1,0:T(8,128)(2,1)S(1)} collective-permute-done((bf16[64,1024]{1,0:T(8,128)(2,1)S(1)}, bf16[64,1024]{1,0:T(8,128)(2,1)S(1)}, u32[]{:S(2)}, u32[]{:S(2)}) %collective-permute-start.6) | collective-permute-done | bytes 131104 | tf_op jit(solution)/shard_map/ppermute | solution.py:30
  31.2 8.7 %attention.1 = (bf16[128,3072]{1,0:T(8,128)(2,1)}, f32[2,128,512]{2,1,0:T(8,128)S(1)}, bf16[2,128,512]{2,1,0:T(8,128)(2,1)S(1)}, bf16[2,128,512]{2,1,0:T(8,128)(2,1)S(1)}, bf16[2,2,64,512]{3,2,1,0:T(8,128)(2,1)S(1)}) custom-call(s32[1]{0:T(128)} %bitcast.flag_ref, f32[2,32]{1,0:T(2,128)S(1)} %reshape.101.bias_ref, bf16[128,3072]{1,0:T(8,128)(2,1)S(1)} %bitcast.49, ...), custom_call_target="tpu_custom_call" | custom-call | tf_op jit(solution)/shard_map/attention/pallas_call | solution.py:118
  39.9 0.4 collective-permute-start.9
  40.3 1.0 %collective-permute-done.9 = bf16[2,64,512]{2,1,0:T(8,128)(2,1)S(1)} collective-permute-done((bf16[2,64,512]{2,1,0:T(8,128)(2,1)S(1)}, bf16[2,64,512]{2,1,0:T(8,128)(2,1)S(1)}, u32[]{:S(2)}, u32[]{:S(2)}) %collective-permute-start.9) | collective-permute-done | bytes 131104 | tf_op jit(solution)/shard_map/ppermute | solution.py:30
  41.4 4.1 %collective-permute-done.10 = bf16[2,64,512]{2,1,0:T(8,128)(2,1)S(1)} collective-permute-done((bf16[2,64,512]{2,1,0:T(8,128)(2,1)S(1)}, bf16[2,64,512]{2,1,0:T(8,128)(2,1)S(1)}, u32[]{:S(2)}, u32[]{:S(2)}) %collective-permute-start.10) | collective-permute-done | bytes 131104 | tf_op jit(solution)/shard_map/ppermute | solution.py:30
  45.6 3.1 %collective-permute-start.11 = (bf16[2,64,512]{2,1,0:T(8,128)(2,1)S(1)}, bf16[2,64,512]{2,1,0:T(8,128)(2,1)S(1)}, u32[]{:S(2)}, u32[]{:S(2)}) collective-permute-start(bf16[2,64,512]{2,1,0:T(8,128)(2,1)S(1)} %fusion.2), channel_id=1, source_target_pairs={{0,4},{1,9},{2,6},{3,11},{4,0},{5,13},{6,2},{7,15},{8,12},{9,1},{1... | collective-permute-start | bytes 393224 | tf_op jit(solution)/shard_map/ppermute | solution.py:30
  48.7 2.9 %collective-permute-done.11 = bf16[2,64,512]{2,1,0:T(8,128)(2,1)S(1)} collective-permute-done((bf16[2,64,512]{2,1,0:T(8,128)(2,1)S(1)}, bf16[2,64,512]{2,1,0:T(8,128)(2,1)S(1)}, u32[]{:S(2)}, u32[]{:S(2)}) %collective-permute-start.11) | collective-permute-done | bytes 131104 | tf_op jit(solution)/shard_map/ppermute | solution.py:30
  51.6 0.3 collective-permute-start.12
  51.9 4.4 %collective-permute-start.7 = (bf16[2,128,512]{2,1,0:T(8,128)(2,1)S(1)}, bf16[2,128,512]{2,1,0:T(8,128)(2,1)S(1)}, u32[]{:S(2)}, u32[]{:S(2)}) collective-permute-start(bf16[2,128,512]{2,1,0:T(8,128)(2,1)S(1)} %get-tuple-element.9), channel_id=1, source_target_pairs={{0,1},{1,0},{2,3},{3,2},{4,5},{5,4},{6,7},{7,6},{8,9},{9,8},{10,11... | collective-permute-start | bytes 786440 | tf_op jit(solution)/shard_map/ppermute | solution.py:30
  56.3 2.1 %collective-permute-start.8 = (bf16[2,128,512]{2,1,0:T(8,128)(2,1)S(1)}, bf16[2,128,512]{2,1,0:T(8,128)(2,1)S(1)}, u32[]{:S(2)}, u32[]{:S(2)}) collective-permute-start(bf16[2,128,512]{2,1,0:T(8,128)(2,1)S(1)} %get-tuple-element.10), channel_id=1, source_target_pairs={{1,2},{3,4},{5,6},{7,8},{9,10},{11,12},{13,14},{2,1},{4,3},{6,5},{... | collective-permute-start | bytes 786440 | tf_op jit(solution)/shard_map/ppermute | solution.py:30
  58.4 0.1 add_convert_fusion
  58.5 0.9 %collective-permute-start.13 = (bf16[2,64,512]{2,1,0:T(8,128)(2,1)S(1)}, bf16[2,64,512]{2,1,0:T(8,128)(2,1)S(1)}, u32[]{:S(2)}, u32[]{:S(2)}) collective-permute-start(bf16[2,64,512]{2,1,0:T(8,128)(2,1)S(1)} %add_convert_fusion), channel_id=1, source_target_pairs={{0,1},{1,0},{2,3},{3,2},{4,5},{5,4},{6,7},{7,6},{8,9},{9,8},{10,11... | collective-permute-start | bytes 393224 | tf_op jit(solution)/shard_map/ppermute | solution.py:30
  59.4 1.0 %collective-permute-done.13 = bf16[2,64,512]{2,1,0:T(8,128)(2,1)S(1)} collective-permute-done((bf16[2,64,512]{2,1,0:T(8,128)(2,1)S(1)}, bf16[2,64,512]{2,1,0:T(8,128)(2,1)S(1)}, u32[]{:S(2)}, u32[]{:S(2)}) %collective-permute-start.13) | collective-permute-done | bytes 131104 | tf_op jit(solution)/shard_map/ppermute | solution.py:30
  60.4 0.7 %maximum_select_fusion.1.r_glob = bf16[2,2,64,512]{3,2,1,0:T(8,128)(2,1)} fusion(bf16[1,2,64,512]{3,2,1,0:T(8,128)(2,1)S(1)} %bitcast.52, bf16[1,2,64,512]{3,2,1,0:T(8,128)(2,1)S(1)} %bitcast.50, pred[]{:T(512)S(6)} %eq.47), kind=kLoop, calls=%fused_computation.1 | loop fusion | flops 393216 | bytes 524289 | tf_op jit(solution)/shard_map/jit(_where)/select_n | solution.py:230
  61.1 5.7 %collective-permute-done.8.r_off = bf16[2,128,512]{2,1,0:T(8,128)(2,1)S(1)} collective-permute-done((bf16[2,128,512]{2,1,0:T(8,128)(2,1)S(1)}, bf16[2,128,512]{2,1,0:T(8,128)(2,1)S(1)}, u32[]{:S(2)}, u32[]{:S(2)}) %collective-permute-start.8) | collective-permute-done | bytes 262176 | tf_op jit(solution)/shard_map/ppermute | solution.py:30
  66.8 0.7 %copy-done.6 = bf16[2,128,512]{2,1,0:T(8,128)(2,1)} copy-done((bf16[2,128,512]{2,1,0:T(8,128)(2,1)}, bf16[2,128,512]{2,1,0:T(8,128)(2,1)S(1)}, u32[]{:S(2)}) %copy-start.6) | copy-done | bytes 262168
  67.5 2.2 %finish.1 = bf16[128,1024]{1,0:T(8,128)(2,1)} custom-call(s32[2]{0:T(128)} %get-tuple-element.14.where_ref, f32[2,128,512]{2,1,0:T(8,128)} %copy-done.4, bf16[2,128,512]{2,1,0:T(8,128)(2,1)} %copy-done.5, bf16[2,128,512]{2,1,0:T(8,128)(2,1)} %copy-done.6, bf16[2,2,64,512]{3,2,1,0:T(8,128)(2,1)} %maximum_select_fusion.1.r_glob), custom_call_target="tpu_custom_call" | custom-call | tf_op jit(solution)/shard_map/finish/pallas_call | solution.py:155
  (37 shorter events, 0.9 us)
Async XLA Ops:
  0.6 22.0 %copy-start = (s32[1,32,4,3]{1,2,3,0:T(4,128)S(1)}, s32[1,32,4,3]{1,2,3,0:T(4,128)}, u32[]{:S(2)}) copy-start(s32[1,32,4,3]{1,2,3,0:T(4,128)} %param.11) | copy-start | bytes 4612
  0.6 30.5 %collective-permute-start.2 = (bf16[128,1024]{1,0:T(8,128)(2,1)}, bf16[128,1024]{1,0:T(8,128)(2,1)S(1)}, u32[]{:S(2)}, u32[]{:S(2)}) collective-permute-start(bf16[128,1024]{1,0:T(8,128)(2,1)} %bitcast.45), channel_id=1, source_target_pairs={{1,2},{3,4},{5,6},{7,8},{9,10},{11,12},{13,14},{2,1},{4,3},{6,5},{... | collective-permute-start | bytes 786440 | tf_op jit(solution)/shard_map/ppermute | solution.py:30
  4.4 6.7 %collective-permute-start.1 = (bf16[128,1024]{1,0:T(8,128)(2,1)}, bf16[128,1024]{1,0:T(8,128)(2,1)S(1)}, u32[]{:S(2)}, u32[]{:S(2)}) collective-permute-start(bf16[128,1024]{1,0:T(8,128)(2,1)} %bitcast.46), channel_id=1, source_target_pairs={{0,1},{1,0},{2,3},{3,2},{4,5},{5,4},{6,7},{7,6},{8,9},{9,8},{10,11... | collective-permute-start | bytes 786440 | tf_op jit(solution)/shard_map/ppermute | solution.py:30
  4.4 26.7 %collective-permute-start = (bf16[128,3072]{1,0:T(8,128)(2,1)}, bf16[128,3072]{1,0:T(8,128)(2,1)S(1)}, u32[]{:S(2)}, u32[]{:S(2)}) collective-permute-start(bf16[128,3072]{1,0:T(8,128)(2,1)} %bitcast.53), channel_id=1, source_target_pairs={{16,0},{17,1},{18,2},{19,3},{20,4},{21,5},{22,6},{23,7},{24,8},{25... | collective-permute-start | bytes 2359304 | tf_op jit(solution)/shard_map/ppermute | solution.py:183
  6.7 0.7 copy-start.7
  11.1 20.0 %copy-start.3 = (bf16[128,3072]{1,0:T(8,128)(2,1)S(1)}, bf16[128,3072]{1,0:T(8,128)(2,1)}, u32[]{:S(2)}) copy-start(bf16[128,3072]{1,0:T(8,128)(2,1)} %loss_ref.1) | copy-start | bytes 2359300
  12.2 4.2 %collective-permute-start.3 = (bf16[64,1024]{1,0:T(8,128)(2,1)S(1)}, bf16[64,1024]{1,0:T(8,128)(2,1)S(1)}, u32[]{:S(2)}, u32[]{:S(2)}) collective-permute-start(bf16[64,1024]{1,0:T(8,128)(2,1)S(1)} %bitcast_select_fusion), channel_id=1, source_target_pairs={{0,2},{1,5},{2,0},{3,7},{4,6},{5,1},{6,4},{7,3},{8,10},{9,13},{10,... | collective-permute-start | bytes 393224 | tf_op jit(solution)/shard_map/ppermute | solution.py:30
  16.4 14.8 %copy-start.2 = (bf16[1,128,3072]{2,1,0:T(8,128)(2,1)S(1)}, bf16[1,128,3072]{2,1,0:T(8,128)(2,1)}, u32[]{:S(2)}) copy-start(bf16[1,128,3072]{2,1,0:T(8,128)(2,1)} %param.6) | copy-start | bytes 2359300
  16.4 5.6 %collective-permute-start.4 = (bf16[64,1024]{1,0:T(8,128)(2,1)S(1)}, bf16[64,1024]{1,0:T(8,128)(2,1)S(1)}, u32[]{:S(2)}, u32[]{:S(2)}) collective-permute-start(bf16[64,1024]{1,0:T(8,128)(2,1)S(1)} %add.104), channel_id=1, source_target_pairs={{0,4},{1,9},{2,6},{3,11},{4,0},{5,13},{6,2},{7,15},{8,12},{9,1},{1... | collective-permute-start | bytes 393224 | tf_op jit(solution)/shard_map/ppermute | solution.py:30
  22.0 3.9 %collective-permute-start.5 = (bf16[64,1024]{1,0:T(8,128)(2,1)S(1)}, bf16[64,1024]{1,0:T(8,128)(2,1)S(1)}, u32[]{:S(2)}, u32[]{:S(2)}) collective-permute-start(bf16[64,1024]{1,0:T(8,128)(2,1)S(1)} %add.105), channel_id=1, source_target_pairs={{0,8},{1,3},{2,10},{3,1},{4,12},{5,7},{6,14},{7,5},{8,0},{9,11},{1... | collective-permute-start | bytes 393224 | tf_op jit(solution)/shard_map/ppermute | solution.py:30
  25.9 5.1 %collective-permute-start.6 = (bf16[64,1024]{1,0:T(8,128)(2,1)S(1)}, bf16[64,1024]{1,0:T(8,128)(2,1)S(1)}, u32[]{:S(2)}, u32[]{:S(2)}) collective-permute-start(bf16[64,1024]{1,0:T(8,128)(2,1)S(1)} %add.106), channel_id=1, source_target_pairs={{0,1},{1,0},{2,3},{3,2},{4,5},{5,4},{6,7},{7,6},{8,9},{9,8},{10,11... | collective-permute-start | bytes 393224 | tf_op jit(solution)/shard_map/ppermute | solution.py:30
  30.2 1.0 %copy-start.1 = (bf16[1,128,1024]{2,1,0:T(8,128)(2,1)S(1)}, bf16[1,128,1024]{2,1,0:T(8,128)(2,1)}, u32[]{:S(2)}) copy-start(bf16[1,128,1024]{2,1,0:T(8,128)(2,1)} %param.7) | copy-start | bytes 786436
  39.9 1.5 %copy-start.4 = (f32[2,128,512]{2,1,0:T(8,128)}, f32[2,128,512]{2,1,0:T(8,128)S(1)}, u32[]{:S(2)}) copy-start(f32[2,128,512]{2,1,0:T(8,128)S(1)} %get-tuple-element.8.g_own) | copy-start | bytes 1572868
  39.9 1.4 %collective-permute-start.9 = (bf16[2,64,512]{2,1,0:T(8,128)(2,1)S(1)}, bf16[2,64,512]{2,1,0:T(8,128)(2,1)S(1)}, u32[]{:S(2)}, u32[]{:S(2)}) collective-permute-start(bf16[2,64,512]{2,1,0:T(8,128)(2,1)S(1)} %select_bitcast_fusion), channel_id=1, source_target_pairs={{0,1},{1,0},{2,3},{3,2},{4,5},{5,4},{6,7},{7,6},{8,9},{9,8},{10,11... | collective-permute-start | bytes 393224 | tf_op jit(solution)/shard_map/ppermute | solution.py:30
  41.4 4.2 %collective-permute-start.10 = (bf16[2,64,512]{2,1,0:T(8,128)(2,1)S(1)}, bf16[2,64,512]{2,1,0:T(8,128)(2,1)S(1)}, u32[]{:S(2)}, u32[]{:S(2)}) collective-permute-start(bf16[2,64,512]{2,1,0:T(8,128)(2,1)S(1)} %get-tuple-element.12), channel_id=1, source_target_pairs={{0,2},{1,5},{2,0},{3,7},{4,6},{5,1},{6,4},{7,3},{8,10},{9,13},{10,... | collective-permute-start | bytes 393224 | tf_op jit(solution)/shard_map/ppermute | solution.py:30
  45.6 5.9 %collective-permute-start.11 = (bf16[2,64,512]{2,1,0:T(8,128)(2,1)S(1)}, bf16[2,64,512]{2,1,0:T(8,128)(2,1)S(1)}, u32[]{:S(2)}, u32[]{:S(2)}) collective-permute-start(bf16[2,64,512]{2,1,0:T(8,128)(2,1)S(1)} %fusion.2), channel_id=1, source_target_pairs={{0,4},{1,9},{2,6},{3,11},{4,0},{5,13},{6,2},{7,15},{8,12},{9,1},{1... | collective-permute-start | bytes 393224 | tf_op jit(solution)/shard_map/ppermute | solution.py:30
  51.6 6.8 %collective-permute-start.12 = (bf16[2,64,512]{2,1,0:T(8,128)(2,1)S(1)}, bf16[2,64,512]{2,1,0:T(8,128)(2,1)S(1)}, u32[]{:S(2)}, u32[]{:S(2)}) collective-permute-start(bf16[2,64,512]{2,1,0:T(8,128)(2,1)S(1)} %fusion.1), channel_id=1, source_target_pairs={{0,8},{1,3},{2,10},{3,1},{4,12},{5,7},{6,14},{7,5},{8,0},{9,11},{1... | collective-permute-start | bytes 393224 | tf_op jit(solution)/shard_map/ppermute | solution.py:30
  51.9 9.2 %collective-permute-start.7 = (bf16[2,128,512]{2,1,0:T(8,128)(2,1)S(1)}, bf16[2,128,512]{2,1,0:T(8,128)(2,1)S(1)}, u32[]{:S(2)}, u32[]{:S(2)}) collective-permute-start(bf16[2,128,512]{2,1,0:T(8,128)(2,1)S(1)} %get-tuple-element.9), channel_id=1, source_target_pairs={{0,1},{1,0},{2,3},{3,2},{4,5},{5,4},{6,7},{7,6},{8,9},{9,8},{10,11... | collective-permute-start | bytes 786440 | tf_op jit(solution)/shard_map/ppermute | solution.py:30
  56.3 10.5 %collective-permute-start.8 = (bf16[2,128,512]{2,1,0:T(8,128)(2,1)S(1)}, bf16[2,128,512]{2,1,0:T(8,128)(2,1)S(1)}, u32[]{:S(2)}, u32[]{:S(2)}) collective-permute-start(bf16[2,128,512]{2,1,0:T(8,128)(2,1)S(1)} %get-tuple-element.10), channel_id=1, source_target_pairs={{1,2},{3,4},{5,6},{7,8},{9,10},{11,12},{13,14},{2,1},{4,3},{6,5},{... | collective-permute-start | bytes 786440 | tf_op jit(solution)/shard_map/ppermute | solution.py:30
  58.5 1.9 %collective-permute-start.13 = (bf16[2,64,512]{2,1,0:T(8,128)(2,1)S(1)}, bf16[2,64,512]{2,1,0:T(8,128)(2,1)S(1)}, u32[]{:S(2)}, u32[]{:S(2)}) collective-permute-start(bf16[2,64,512]{2,1,0:T(8,128)(2,1)S(1)} %add_convert_fusion), channel_id=1, source_target_pairs={{0,1},{1,0},{2,3},{3,2},{4,5},{5,4},{6,7},{7,6},{8,9},{9,8},{10,11... | collective-permute-start | bytes 393224 | tf_op jit(solution)/shard_map/ppermute | solution.py:30
  61.1 5.7 %copy-start.5 = (bf16[2,128,512]{2,1,0:T(8,128)(2,1)}, bf16[2,128,512]{2,1,0:T(8,128)(2,1)S(1)}, u32[]{:S(2)}) copy-start(bf16[2,128,512]{2,1,0:T(8,128)(2,1)S(1)} %collective-permute-done.7.r_on) | copy-start | bytes 786436
  66.8 0.7 %copy-start.6 = (bf16[2,128,512]{2,1,0:T(8,128)(2,1)}, bf16[2,128,512]{2,1,0:T(8,128)(2,1)S(1)}, u32[]{:S(2)}) copy-start(bf16[2,128,512]{2,1,0:T(8,128)(2,1)S(1)} %collective-permute-done.8.r_off) | copy-start | bytes 786436

commit v2 on v1

v2 whole, which is shorter than its diff:
```python
import functools
import math

import jax
import jax.numpy as jnp
from jax import lax
from jax.experimental import pallas as pl
from jax.experimental.pallas import tpu as pltpu
from jax.sharding import PartitionSpec as P

HQ = 24
KEY_HEADS = 4
HEAD_SIZE = 128
BLOCK_TOKENS = 64
GLOBAL_BLOCKS = 2
GROUP_HEADS = 6
SCALE = 1.0 / math.sqrt(HEAD_SIZE)
LOG2E = math.log2(math.e)
NEG = -1e30
WIDTH = KEY_HEADS * HEAD_SIZE
ROWS_E = GROUP_HEADS * BLOCK_TOKENS
GLOB_ROWS = GLOBAL_BLOCKS * BLOCK_TOKENS
NT = (((1,), (1,)), ((), ()))
NN = (((1,), (0,)), ((), ()))
TN = (((0,), (0,)), ((), ()))
F32 = jnp.float32
BF = jnp.bfloat16
VMEM = pl.BlockSpec(memory_space=pltpu.VMEM)
SMEM = pl.BlockSpec(memory_space=pltpu.SMEM)


def dot(a, b, dims):
    return lax.dot_general(a, b, dims, preferred_element_type=F32)


def call(kernel, name, ins, outs, args, flops):
    return pl.pallas_call(
        kernel,
        in_specs=ins,
        out_specs=[VMEM] * len(outs),
        out_shape=outs,
        compiler_params=pltpu.CompilerParams(vmem_limit_bytes=24 << 20),
        cost_estimate=pl.CostEstimate(flops=flops, bytes_accessed=flops // 500, transcendentals=0),
        name=name,
    )(*args)


def shape(*dims, dtype=F32):
    return jax.ShapeDtypeStruct(dims, dtype)


def group_rows(ref, g):
    toks = ref.shape[0]
    parts = []
    for e in range(toks // BLOCK_TOKENS):
        for h in range(GROUP_HEADS):
            c = (g * GROUP_HEADS + h) * HEAD_SIZE
            parts.append(ref[e * BLOCK_TOKENS : (e + 1) * BLOCK_TOKENS, c : c + HEAD_SIZE])
    return jnp.concatenate(parts, 0)


def stacked(refs, c):
    return jnp.concatenate([ref[:, c : c + HEAD_SIZE] for ref in refs], 0)


def at_last_section():
    return lax.axis_index("section") == lax.axis_size("section") - 1


def pick_kernel(ids_ref, own_ref, on_ref, out_ref):
    nb = own_ref.shape[0] // BLOCK_TOKENS
    pos = lax.axis_index("seq")
    core = lax.rem(pos, 2)
    block = ids_ref[0, core]
    owner = lax.div(block, nb)
    row = pl.multiple_of(lax.rem(block, nb) * BLOCK_TOKENS, BLOCK_TOKENS)
    twin = pos + 1 - 2 * core
    mine = owner == pos
    theirs = owner == twin

    @pl.when(mine)
    def _():
        out_ref[...] = own_ref[pl.ds(row, BLOCK_TOKENS), :]

    @pl.when(theirs)
    def _():
        out_ref[...] = on_ref[pl.ds(row, BLOCK_TOKENS), :]

    @pl.when(jnp.logical_not(mine | theirs))
    def _():
        out_ref[...] = jnp.zeros_like(out_ref)


def local_kernel(bias_ref, q_ref, own_ref, on_ref, off_ref, w_ref, stat_ref):
    toks = q_ref.shape[0]
    nb = toks // BLOCK_TOKENS
    ncand = 3 * nb
    for g in range(KEY_HEADS):
        keys = stacked((own_ref, on_ref, off_ref), g * HEAD_SIZE)
        s = dot(keys, group_rows(q_ref, g), NT)
        for e in range(nb):
            cols = slice(e * ROWS_E, (e + 1) * ROWS_E)
            t = jnp.concatenate(
                [
                    s[j * BLOCK_TOKENS : (j + 1) * BLOCK_TOKENS, cols] * (SCALE * LOG2E)
                    + bias_ref[e, g * ncand + j]
                    for j in range(ncand)
                ],
                0,
            )
            m = jnp.max(t, axis=0, keepdims=True)
            w = jnp.exp2(t - m)
            w_ref[g, :, cols] = w
            stat_ref[g, 0:1, cols] = m
            stat_ref[g, 1:2, cols] = jnp.sum(w, axis=0, keepdims=True)


def global_kernel(
    q_ref, shifted_ref, loss_ref, own_ref, on_ref, off_ref, held_ref, other_ref, w_ref, stat_ref,
    dp_ref, ds_ref, out_stat_ref, keep_ref, give_ref, do_ref,
):
    last = at_last_section()

    @pl.when(last)
    def _():
        do_ref[...] = loss_ref[...]

    @pl.when(jnp.logical_not(last))
    def _():
        do_ref[...] = shifted_ref[...]

    for g in range(KEY_HEADS):
        kc = g * HEAD_SIZE
        vc = WIDTH + kc
        qg = group_rows(q_ref, g)
        dog = group_rows(do_ref, g)
        t = dot(stacked((held_ref, other_ref), kc), qg, NT) * (SCALE * LOG2E)
        dpg = dot(stacked((held_ref, other_ref), vc), dog, NT)
        dpl = dot(stacked((own_ref, on_ref, off_ref), vc), dog, NT)
        dp_ref[g] = dpl
        partial_delta = jnp.sum(w_ref[g] * dpl, axis=0, keepdims=True)
        m_local = stat_ref[g, 0:1, :]
        m = jnp.maximum(m_local, jnp.max(t, axis=0, keepdims=True))
        shrink = jnp.exp2(m_local - m)
        w = jnp.exp2(t - m)
        total = shrink * stat_ref[g, 1:2, :] + jnp.sum(w, axis=0, keepdims=True)
        inv = 1.0 / total
        p = w * inv
        local_factor = shrink * inv
        delta = local_factor * partial_delta + jnp.sum(p * dpg, axis=0, keepdims=True)
        ds = (p * (dpg - delta) * SCALE).astype(BF)
        ds_ref[g] = ds
        out_stat_ref[g, 0:1, :] = local_factor
        out_stat_ref[g, 1:2, :] = delta
        cols = slice(kc, kc + HEAD_SIZE)
        for i, grad in enumerate((dot(ds, qg, NN), dot(p.astype(BF), dog, NN))):
            keep_ref[i, :, cols] = grad[:BLOCK_TOKENS]
            give_ref[i, :, cols] = grad[BLOCK_TOKENS:].astype(BF)


def rest_kernel(
    q_ref, do_ref, own_ref, on_ref, off_ref, held_ref, other_ref, w_ref, dp_ref, ds_ref, stat_ref,
    dq_ref, g_own, g_on, g_off,
):
    toks = q_ref.shape[0]
    for g in range(KEY_HEADS):
        kc = g * HEAD_SIZE
        keys = stacked((own_ref, on_ref, off_ref, held_ref, other_ref), kc)
        p = w_ref[g] * stat_ref[g, 0:1, :]
        ds = (p * (dp_ref[g] - stat_ref[g, 1:2, :]) * SCALE).astype(BF)
        ds_all = jnp.concatenate([ds, ds_ref[g]], 0)
        dq = dot(keys, ds_all, TN).T
        for e in range(toks // BLOCK_TOKENS):
            for h in range(GROUP_HEADS):
                r = e * ROWS_E + h * BLOCK_TOKENS
                c = (g * GROUP_HEADS + h) * HEAD_SIZE
                dq_ref[e * BLOCK_TOKENS : (e + 1) * BLOCK_TOKENS, c : c + HEAD_SIZE] = (
                    dq[r : r + BLOCK_TOKENS].astype(BF)
                )
        cols = slice(kc, kc + HEAD_SIZE)
        grads = (dot(ds, group_rows(q_ref, g), NN), dot(p.astype(BF), group_rows(do_ref, g), NN))
        for i, grad in enumerate(grads):
            g_own[i, :, cols] = grad[:toks]
            g_on[i, :, cols] = grad[toks : 2 * toks].astype(BF)
            g_off[i, :, cols] = grad[2 * toks :].astype(BF)


def finish_kernel(ids_ref, g_own, r_on, r_off, half_ref, half_other_ref, out_ref):
    toks = g_own.shape[1]
    nb = toks // BLOCK_TOKENS
    pos = lax.axis_index("seq")
    core = lax.rem(pos, 2)
    places = []
    for which in (core, 1 - core):
        block = ids_ref[0, which]
        places.append(jnp.where(lax.div(block, nb) == pos, lax.rem(block, nb), -1))
    for i in range(2):
        for s in range(nb):
            rows = slice(s * BLOCK_TOKENS, (s + 1) * BLOCK_TOKENS)
            total = g_own[i, rows] + r_on[i, rows].astype(F32) + r_off[i, rows].astype(F32)
            for place, ref in zip(places, (half_ref, half_other_ref)):
                total = total + jnp.where(place == s, ref[i].astype(F32), 0.0)
            out_ref[rows, i * WIDTH : (i + 1) * WIDTH] = total.astype(BF)


def list_bias(random_table, pos, peers, nb):
    core = pos % 2
    step = jnp.arange(nb, dtype=jnp.int32)
    holders = (pos, pos + 1 - 2 * core, pos - 1 + 2 * core)
    cand_ids = jnp.concatenate([h * nb + step for h in holders])
    block_ids = pos * nb + step
    own_random = lax.dynamic_slice_in_dim(random_table, pos * nb, nb, 0)
    listed = jnp.sum((own_random[:, :, None, :] == cand_ids[None, None, :, None]).astype(F32), -1)
    inside = (cand_ids >= 0) & (cand_ids < peers * nb)
    window = (jnp.abs(cand_ids[None, :] - block_ids[:, None]) <= 1) & inside[None, :]
    times = listed + window[:, None, :].astype(F32)
    bias = jnp.where(times > 0, jnp.log2(jnp.maximum(times, 1.0)), NEG)
    return bias.reshape(nb, -1)


def body(queries, packed_key_value, incoming, loss_grad, global_blocks, random_blocks):
    toks = queries.shape[1]
    nb = toks // BLOCK_TOKENS
    rows = nb * ROWS_E
    sections = lax.axis_size("section")
    peers = lax.axis_size("seq")
    bits = peers.bit_length() - 1
    assert peers == 1 << bits and bits >= 1
    pos = lax.axis_index("seq")

    twin = [(i, i ^ 1) for i in range(peers)]
    side = [(i, i + 1) for i in range(1, peers - 1, 2)]
    side = side + [(j, i) for i, j in side]
    orders = (list(range(1, bits)), list(range(2, bits)) + [1])
    hops = [
        [(i, i ^ (1 << orders[i % 2][r])) for i in range(peers)] for r in range(bits - 1)
    ]
    exchange = lambda x, pairs: lax.ppermute(x, "seq", pairs)

    q = queries[0]
    own = packed_key_value[0]
    on = exchange(own, twin)
    shifted = lax.ppermute(incoming[0], "section", [(i, i - 1) for i in range(1, sections)])
    (held,) = call(
        pick_kernel, "pick", [SMEM, VMEM, VMEM], [shape(BLOCK_TOKENS, own.shape[1], dtype=BF)],
        (global_blocks, own, on), 10**6,
    )
    off = exchange(own, side)
    for hop in hops:
        held = held + exchange(held, hop)
    other = exchange(held, twin)

    bias = list_bias(random_blocks[0], pos, peers, nb)
    near = (own, on, off)
    w, stats = call(
        local_kernel, "local", [SMEM] + [VMEM] * 4,
        [shape(KEY_HEADS, 3 * toks, rows), shape(KEY_HEADS, 8, rows)],
        (bias, q) + near, 3 * 10**9,
    )
    dp, ds, stats, keep, give, d_out = call(
        global_kernel, "globals", [VMEM] * 10,
        [
            shape(KEY_HEADS, 3 * toks, rows),
            shape(KEY_HEADS, GLOB_ROWS, rows, dtype=BF),
            shape(KEY_HEADS, 8, rows),
            shape(2, BLOCK_TOKENS, WIDTH),
            shape(2, BLOCK_TOKENS, WIDTH, dtype=BF),
            shape(*q.shape, dtype=BF),
        ],
        (q, shifted, loss_grad) + near + (held, other, w, stats), 3 * 10**9,
    )
    total = keep + exchange(give, twin).astype(F32)
    dq, g_own, g_on, g_off = call(
        rest_kernel, "rest", [VMEM] * 11,
        [
            shape(*q.shape, dtype=BF),
            shape(2, toks, WIDTH),
            shape(2, toks, WIDTH, dtype=BF),
            shape(2, toks, WIDTH, dtype=BF),
        ],
        (q, d_out) + near + (held, other, w, dp, ds, stats), 5 * 10**9,
    )
    r_on = exchange(g_on, twin)
    r_off = exchange(g_off, side)
    for hop in hops:
        total = total + exchange(total.astype(BF), hop).astype(F32)
    half = total.astype(BF)
    half_other = exchange(half, twin)
    (out,) = call(
        finish_kernel, "finish", [SMEM] + [VMEM] * 5, [shape(*own.shape, dtype=BF)],
        (global_blocks, g_own, r_on, r_off, half, half_other), 10**6,
    )
    return (dq[None], out[None])


def solution(mesh):
    in_specs = (
        P("section", "seq", None),
        P("section", "seq", None),
        P("section", "seq", None),
        P("seq", None),
        P("section", None),
        P("section", None, None, None),
    )
    out_specs = (P("section", "seq", None), P("section", "seq", None))
    return jax.shard_map(body, mesh=mesh, in_specs=in_specs, out_specs=out_specs, check_vma=False)
```

time: 69.9 us -> 65.2 us (0.933)
  between operations: 3.43 us -> 0.83 us
  other arithmetic: 3.02 us -> 0.61 us
  local copies, waits for them, and re-layouts: 2.26 us -> 3.97 us
  starting transfers between devices: 24.6 us -> 23.3 us
  Pallas kernels: 10.9 us -> 9.83 us
  waiting for transfers between devices: 25.5 us -> 26.4 us
    select_n x6 -> x1, other arithmetic: 2.4 us -> 0.01 us  [list_bias(): bias = jnp.where(times > 0, jnp.log2(jnp.maximum(times, 1.0)), NEG)]
    unnamed x16 -> x14, local copies, waits for them, and re-layouts: 1.39 us -> 3.71 us
    ppermute x13, starting transfers between devices: 22.4 us -> 21.1 us  [body(): exchange = lambda x, pairs: lax.ppermute(x, 'seq', pairs)]
    pallas_call x2 -> x5, Pallas kernels: 10.9 us -> 9.83 us  [call(): pl.pallas_call(kernel, in_specs=ins, out_specs=[VMEM] * len(outs), out_sh...]
    ppermute x13, waiting for transfers between devices: 25.5 us -> 26.4 us  [body(): exchange = lambda x, pairs: lax.ppermute(x, 'seq', pairs)]
  transfers between devices with their start and end apart: 14 -> 14, of which waited for: 9 -> 7; matrix products, arithmetic and copies ran while one was open for 5% -> 1% of each run, Pallas kernels for 0% -> 9%
where the time goes in v2:
time: 65.2 us; the launch traced here: 64.9 us
  waiting for transfers between devices  26.4 us (40%)
  starting transfers between devices  23.3 us (36%)
  Pallas kernels  9.83 us (15%)
  local copies, waits for them, and re-layouts  3.97 us (6%)
  between operations  0.83 us (1%)
    ppermute x13, waiting for transfers between devices, body(): exchange = lambda x, pairs: lax.ppermute(x, 'seq', pairs)  26.4 us
    ppermute x13, starting transfers between devices, body(): exchange = lambda x, pairs: lax.ppermute(x, 'seq', pairs)  21.1 us
    pallas_call x5, Pallas kernels, call(): pl.pallas_call(kernel, in_specs=ins, out_specs=[VMEM] * len(outs), out_sh...  9.83 us
    unnamed x14, local copies, waits for them, and re-layouts  3.71 us
    ppermute x1, starting transfers between devices, body(): lax.ppermute(incoming[0], 'section', [(i, i - 1) for i in range(1, sectio...  2.21 us
  transfers between devices with their start and end apart: 14, of which 7 were waited for; matrix products, arithmetic and copies ran while one was open for 1% of the time, Pallas kernels for 9%

profile of v2, /device:TPU:11, one launch (start us, length us, event | category | flops | bytes accessed | tf_op | source)
XLA Modules:
  0.0 64.9 jit_solution(16939787425590023575)
XLA Ops:
  0.6 0.7 %collective-permute-start.1 = (bf16[128,1024]{1,0:T(8,128)(2,1)}, bf16[128,1024]{1,0:T(8,128)(2,1)S(1)}, u32[]{:S(2)}, u32[]{:S(2)}) collective-permute-start(bf16[128,1024]{1,0:T(8,128)(2,1)} %bitcast.7), channel_id=1, source_target_pairs={{0,1},{1,0},{2,3},{3,2},{4,5},{5,4},{6,7},{7,6},{8,9},{9,8},{10,11... | collective-permute-start | bytes 786440 | tf_op jit(solution)/shard_map/ppermute | solution.py:238
  1.4 3.1 %collective-permute-start.2 = (bf16[128,1024]{1,0:T(8,128)(2,1)}, bf16[128,1024]{1,0:T(8,128)(2,1)S(1)}, u32[]{:S(2)}, u32[]{:S(2)}) collective-permute-start(bf16[128,1024]{1,0:T(8,128)(2,1)} %bitcast.8), channel_id=1, source_target_pairs={{1,2},{3,4},{5,6},{7,8},{9,10},{11,12},{13,14},{2,1},{4,3},{6,5},{... | collective-permute-start | bytes 786440 | tf_op jit(solution)/shard_map/ppermute | solution.py:238
  4.4 2.2 %collective-permute-start = (bf16[128,3072]{1,0:T(8,128)(2,1)}, bf16[128,3072]{1,0:T(8,128)(2,1)S(1)}, u32[]{:S(2)}, u32[]{:S(2)}) collective-permute-start(bf16[128,3072]{1,0:T(8,128)(2,1)} %bitcast.17), channel_id=1, source_target_pairs={{16,0},{17,1},{18,2},{19,3},{20,4},{21,5},{22,6},{23,7},{24,8},{25... | collective-permute-start | bytes 2359304 | tf_op jit(solution)/shard_map/ppermute | solution.py:243
  6.7 0.1 compare_and_fusion
  6.8 0.9 %copy-done.1 = bf16[1,128,1024]{2,1,0:T(8,128)(2,1)S(1)} copy-done((bf16[1,128,1024]{2,1,0:T(8,128)(2,1)S(1)}, bf16[1,128,1024]{2,1,0:T(8,128)(2,1)}, u32[]{:S(2)}) %copy-start.1) | copy-done | bytes 262168
  7.7 0.7 %copy-done.3 = s32[1,2]{1,0:T(1,128)S(1)} copy-done((s32[1,2]{1,0:T(1,128)S(1)}, s32[1,2]{1,0:T(1,128)}, u32[]{:S(2)}) %copy-start.3) | copy-done | bytes 32
  8.4 0.6 pick.1
  9.0 0.2 collective-permute-start.3
  9.3 3.9 %collective-permute-done.3 = bf16[64,1024]{1,0:T(8,128)(2,1)S(1)} collective-permute-done((bf16[64,1024]{1,0:T(8,128)(2,1)S(1)}, bf16[64,1024]{1,0:T(8,128)(2,1)S(1)}, u32[]{:S(2)}, u32[]{:S(2)}) %collective-permute-start.3) | collective-permute-done | bytes 131104 | tf_op jit(solution)/shard_map/ppermute | solution.py:238
  13.2 2.4 %collective-permute-start.4 = (bf16[64,1024]{1,0:T(8,128)(2,1)S(1)}, bf16[64,1024]{1,0:T(8,128)(2,1)S(1)}, u32[]{:S(2)}, u32[]{:S(2)}) collective-permute-start(bf16[64,1024]{1,0:T(8,128)(2,1)S(1)} %add.78), channel_id=1, source_target_pairs={{0,4},{1,9},{2,6},{3,11},{4,0},{5,13},{6,2},{7,15},{8,12},{9,1},{1... | collective-permute-start | bytes 393224 | tf_op jit(solution)/shard_map/ppermute | solution.py:238
  15.7 0.1 copy.11
  15.8 0.1 convert_reduce_fusion
  15.8 2.9 %collective-permute-done.4 = bf16[64,1024]{1,0:T(8,128)(2,1)S(1)} collective-permute-done((bf16[64,1024]{1,0:T(8,128)(2,1)S(1)}, bf16[64,1024]{1,0:T(8,128)(2,1)S(1)}, u32[]{:S(2)}, u32[]{:S(2)}) %collective-permute-start.4) | collective-permute-done | bytes 131104 | tf_op jit(solution)/shard_map/ppermute | solution.py:238
  18.8 0.8 %collective-permute-start.5 = (bf16[64,1024]{1,0:T(8,128)(2,1)S(1)}, bf16[64,1024]{1,0:T(8,128)(2,1)S(1)}, u32[]{:S(2)}, u32[]{:S(2)}) collective-permute-start(bf16[64,1024]{1,0:T(8,128)(2,1)S(1)} %add.79), channel_id=1, source_target_pairs={{0,8},{1,3},{2,10},{3,1},{4,12},{5,7},{6,14},{7,5},{8,0},{9,11},{1... | collective-permute-start | bytes 393224 | tf_op jit(solution)/shard_map/ppermute | solution.py:238
  19.7 0.1 reshape.96.bias_ref
  19.7 3.0 %collective-permute-done.5 = bf16[64,1024]{1,0:T(8,128)(2,1)S(1)} collective-permute-done((bf16[64,1024]{1,0:T(8,128)(2,1)S(1)}, bf16[64,1024]{1,0:T(8,128)(2,1)S(1)}, u32[]{:S(2)}, u32[]{:S(2)}) %collective-permute-start.5) | collective-permute-done | bytes 131104 | tf_op jit(solution)/shard_map/ppermute | solution.py:238
  22.7 4.0 %collective-permute-start.6 = (bf16[64,1024]{1,0:T(8,128)(2,1)S(1)}, bf16[64,1024]{1,0:T(8,128)(2,1)S(1)}, u32[]{:S(2)}, u32[]{:S(2)}) collective-permute-start(bf16[64,1024]{1,0:T(8,128)(2,1)S(1)} %add.80.held_ref), channel_id=1, source_target_pairs={{0,1},{1,0},{2,3},{3,2},{4,5},{5,4},{6,7},{7,6},{8,9},{9,8},{10,11... | collective-permute-start | bytes 393224 | tf_op jit(solution)/shard_map/ppermute | solution.py:238
  26.8 0.9 %copy-done.2 = bf16[1,128,1024]{2,1,0:T(8,128)(2,1)S(1)} copy-done((bf16[1,128,1024]{2,1,0:T(8,128)(2,1)S(1)}, bf16[1,128,1024]{2,1,0:T(8,128)(2,1)}, u32[]{:S(2)}) %copy-start.2) | copy-done | bytes 262168
  27.7 1.1 %copy-done.6 = bf16[1,128,3072]{2,1,0:T(8,128)(2,1)S(1)} copy-done((bf16[1,128,3072]{2,1,0:T(8,128)(2,1)S(1)}, bf16[1,128,3072]{2,1,0:T(8,128)(2,1)}, u32[]{:S(2)}) %copy-start.6) | copy-done | bytes 786456
  28.9 2.1 %local.1 = (f32[4,384,768]{2,1,0:T(8,128)S(1)}, f32[4,8,768]{2,1,0:T(8,128)S(1)}) custom-call(f32[2,24]{1,0:T(2,128)S(1)} %reshape.96.bias_ref, bf16[128,3072]{1,0:T(8,128)(2,1)S(1)} %bitcast.13, bf16[128,1024]{1,0:T(8,128)(2,1)S(1)} %bitcast.10, bf16[128,1024]{1,0:T(8,128)(2,1)S(1)} %collective-permute-done.1.on_ref, ...), custom_call_target="tpu_custom_call" | custom-call | flops 3000000000 | bytes 6000000 | tf_op jit(solution)/shard_map/local/pallas_call | solution.py:37
  31.0 2.9 %globals.1 = (f32[4,384,768]{2,1,0:T(8,128)S(1)}, bf16[4,128,768]{2,1,0:T(8,128)(2,1)S(1)}, f32[4,8,768]{2,1,0:T(8,128)S(1)}, f32[2,64,512]{2,1,0:T(8,128)S(1)},...) custom-call(bf16[128,3072]{1,0:T(8,128)(2,1)S(1)} %bitcast.14, ...), custom_call_target="tpu_custom_call" | custom-call | flops 3000000000 | bytes 6000000 | tf_op jit(solution)/shard_map/globals/pallas_call | solution.py:37
  33.9 0.1 collective-permute-start.9
  33.9 1.3 %collective-permute-done.9 = bf16[2,64,512]{2,1,0:T(8,128)(2,1)S(1)} collective-permute-done((bf16[2,64,512]{2,1,0:T(8,128)(2,1)S(1)}, bf16[2,64,512]{2,1,0:T(8,128)(2,1)S(1)}, u32[]{:S(2)}, u32[]{:S(2)}) %collective-permute-start.9) | collective-permute-done | bytes 131104 | tf_op jit(solution)/shard_map/ppermute | solution.py:238
  35.4 4.1 %collective-permute-done.10 = bf16[2,64,512]{2,1,0:T(8,128)(2,1)S(1)} collective-permute-done((bf16[2,64,512]{2,1,0:T(8,128)(2,1)S(1)}, bf16[2,64,512]{2,1,0:T(8,128)(2,1)S(1)}, u32[]{:S(2)}, u32[]{:S(2)}) %collective-permute-start.10) | collective-permute-done | bytes 131104 | tf_op jit(solution)/shard_map/ppermute | solution.py:238
  39.5 3.1 %collective-permute-start.11 = (bf16[2,64,512]{2,1,0:T(8,128)(2,1)S(1)}, bf16[2,64,512]{2,1,0:T(8,128)(2,1)S(1)}, u32[]{:S(2)}, u32[]{:S(2)}) collective-permute-start(bf16[2,64,512]{2,1,0:T(8,128)(2,1)S(1)} %fusion.2), channel_id=1, source_target_pairs={{0,4},{1,9},{2,6},{3,11},{4,0},{5,13},{6,2},{7,15},{8,12},{9,1},{1... | collective-permute-start | bytes 393224 | tf_op jit(solution)/shard_map/ppermute | solution.py:238
  42.6 2.9 %collective-permute-done.11 = bf16[2,64,512]{2,1,0:T(8,128)(2,1)S(1)} collective-permute-done((bf16[2,64,512]{2,1,0:T(8,128)(2,1)S(1)}, bf16[2,64,512]{2,1,0:T(8,128)(2,1)S(1)}, u32[]{:S(2)}, u32[]{:S(2)}) %collective-permute-start.11) | collective-permute-done | bytes 131104 | tf_op jit(solution)/shard_map/ppermute | solution.py:238
  45.7 2.9 %rest.1 = (bf16[128,3072]{1,0:T(8,128)(2,1)}, f32[2,128,512]{2,1,0:T(8,128)S(1)}, bf16[2,128,512]{2,1,0:T(8,128)(2,1)S(1)}, bf16[2,128,512]{2,1,0:T(8,128)(2,1)S(1)}) custom-call(bf16[128,3072]{1,0:T(8,128)(2,1)S(1)} %bitcast.15, bf16[128,3072]{1,0:T(8,128)(2,1)S(1)} %get-tuple-element.16.do_ref, bf16[128,1024]{1,0:T(8,128)(2,1)S(1)} %bitcast.12, ...), custom_call_target="tpu_custom_call" | custom-call | flops 5000000000 | bytes 10000000 | tf_op jit(solution)/shard_map/rest/pallas_call | solution.py:37
  48.6 4.4 %collective-permute-start.7 = (bf16[2,128,512]{2,1,0:T(8,128)(2,1)S(1)}, bf16[2,128,512]{2,1,0:T(8,128)(2,1)S(1)}, u32[]{:S(2)}, u32[]{:S(2)}) collective-permute-start(bf16[2,128,512]{2,1,0:T(8,128)(2,1)S(1)} %get-tuple-element.22), channel_id=1, source_target_pairs={{0,1},{1,0},{2,3},{3,2},{4,5},{5,4},{6,7},{7,6},{8,9},{9,8},{10,11... | collective-permute-start | bytes 786440 | tf_op jit(solution)/shard_map/ppermute | solution.py:238
  53.0 2.0 %collective-permute-start.8 = (bf16[2,128,512]{2,1,0:T(8,128)(2,1)S(1)}, bf16[2,128,512]{2,1,0:T(8,128)(2,1)S(1)}, u32[]{:S(2)}, u32[]{:S(2)}) collective-permute-start(bf16[2,128,512]{2,1,0:T(8,128)(2,1)S(1)} %get-tuple-element.23), channel_id=1, source_target_pairs={{1,2},{3,4},{5,6},{7,8},{9,10},{11,12},{13,14},{2,1},{4,3},{6,5},{... | collective-permute-start | bytes 786440 | tf_op jit(solution)/shard_map/ppermute | solution.py:238
  55.0 0.1 add_convert_fusion.half_ref
  55.2 8.3 %collective-permute-done.8.r_off = bf16[2,128,512]{2,1,0:T(8,128)(2,1)S(1)} collective-permute-done((bf16[2,128,512]{2,1,0:T(8,128)(2,1)S(1)}, bf16[2,128,512]{2,1,0:T(8,128)(2,1)S(1)}, u32[]{:S(2)}, u32[]{:S(2)}) %collective-permute-start.8) | collective-permute-done | bytes 262176 | tf_op jit(solution)/shard_map/ppermute | solution.py:238
  63.5 1.4 %finish.1 = bf16[128,1024]{1,0:T(8,128)(2,1)} custom-call(s32[1,2]{1,0:T(1,128)S(1)} %copy-done.4, f32[2,128,512]{2,1,0:T(8,128)S(1)} %get-tuple-element.21.g_own, bf16[2,128,512]{2,1,0:T(8,128)(2,1)S(1)} %collective-permute-done.7.r_on, bf16[2,128,512]{2,1,0:T(8,128)(2,1)S(1)} %collective-permute-done.8.r_off, ...), custom_call_target="tpu_custom_call" | custom-call | flops 1000000 | bytes 2000 | tf_op jit(solution)/shard_map/finish/pallas_call | solution.py:37
  (31 shorter events, 0.7 us)
Async XLA Ops:
  0.6 14.9 %copy-start = (s32[1,32,4,3]{1,2,3,0:T(4,128)S(1)}, s32[1,32,4,3]{1,2,3,0:T(4,128)}, u32[]{:S(2)}) copy-start(s32[1,32,4,3]{1,2,3,0:T(4,128)} %param.11) | copy-start | bytes 4612
  0.6 6.1 %collective-permute-start.1 = (bf16[128,1024]{1,0:T(8,128)(2,1)}, bf16[128,1024]{1,0:T(8,128)(2,1)S(1)}, u32[]{:S(2)}, u32[]{:S(2)}) collective-permute-start(bf16[128,1024]{1,0:T(8,128)(2,1)} %bitcast.7), channel_id=1, source_target_pairs={{0,1},{1,0},{2,3},{3,2},{4,5},{5,4},{6,7},{7,6},{8,9},{9,8},{10,11... | collective-permute-start | bytes 786440 | tf_op jit(solution)/shard_map/ppermute | solution.py:238
  1.4 25.4 %collective-permute-start.2 = (bf16[128,1024]{1,0:T(8,128)(2,1)}, bf16[128,1024]{1,0:T(8,128)(2,1)S(1)}, u32[]{:S(2)}, u32[]{:S(2)}) collective-permute-start(bf16[128,1024]{1,0:T(8,128)(2,1)} %bitcast.8), channel_id=1, source_target_pairs={{1,2},{3,4},{5,6},{7,8},{9,10},{11,12},{13,14},{2,1},{4,3},{6,5},{... | collective-permute-start | bytes 786440 | tf_op jit(solution)/shard_map/ppermute | solution.py:238
  4.4 26.5 %collective-permute-start = (bf16[128,3072]{1,0:T(8,128)(2,1)}, bf16[128,3072]{1,0:T(8,128)(2,1)S(1)}, u32[]{:S(2)}, u32[]{:S(2)}) collective-permute-start(bf16[128,3072]{1,0:T(8,128)(2,1)} %bitcast.17), channel_id=1, source_target_pairs={{16,0},{17,1},{18,2},{19,3},{20,4},{21,5},{22,6},{23,7},{24,8},{25... | collective-permute-start | bytes 2359304 | tf_op jit(solution)/shard_map/ppermute | solution.py:243
  6.8 1.0 %copy-start.1 = (bf16[1,128,1024]{2,1,0:T(8,128)(2,1)S(1)}, bf16[1,128,1024]{2,1,0:T(8,128)(2,1)}, u32[]{:S(2)}) copy-start(bf16[1,128,1024]{2,1,0:T(8,128)(2,1)} %param.7) | copy-start | bytes 786436
  7.7 0.7 %copy-start.3 = (s32[1,2]{1,0:T(1,128)S(1)}, s32[1,2]{1,0:T(1,128)}, u32[]{:S(2)}) copy-start(s32[1,2]{1,0:T(1,128)} %ids_ref.3) | copy-start | bytes 28
  9.0 4.2 %collective-permute-start.3 = (bf16[64,1024]{1,0:T(8,128)(2,1)S(1)}, bf16[64,1024]{1,0:T(8,128)(2,1)S(1)}, u32[]{:S(2)}, u32[]{:S(2)}) collective-permute-start(bf16[64,1024]{1,0:T(8,128)(2,1)S(1)} %pick.1), channel_id=1, source_target_pairs={{0,2},{1,5},{2,0},{3,7},{4,6},{5,1},{6,4},{7,3},{8,10},{9,13},{10,... | collective-permute-start | bytes 393224 | tf_op jit(solution)/shard_map/ppermute | solution.py:238
  13.2 5.6 %collective-permute-start.4 = (bf16[64,1024]{1,0:T(8,128)(2,1)S(1)}, bf16[64,1024]{1,0:T(8,128)(2,1)S(1)}, u32[]{:S(2)}, u32[]{:S(2)}) collective-permute-start(bf16[64,1024]{1,0:T(8,128)(2,1)S(1)} %add.78), channel_id=1, source_target_pairs={{0,4},{1,9},{2,6},{3,11},{4,0},{5,13},{6,2},{7,15},{8,12},{9,1},{1... | collective-permute-start | bytes 393224 | tf_op jit(solution)/shard_map/ppermute | solution.py:238
  18.8 3.9 %collective-permute-start.5 = (bf16[64,1024]{1,0:T(8,128)(2,1)S(1)}, bf16[64,1024]{1,0:T(8,128)(2,1)S(1)}, u32[]{:S(2)}, u32[]{:S(2)}) collective-permute-start(bf16[64,1024]{1,0:T(8,128)(2,1)S(1)} %add.79), channel_id=1, source_target_pairs={{0,8},{1,3},{2,10},{3,1},{4,12},{5,7},{6,14},{7,5},{8,0},{9,11},{1... | collective-permute-start | bytes 393224 | tf_op jit(solution)/shard_map/ppermute | solution.py:238
  22.7 8.2 %collective-permute-start.6 = (bf16[64,1024]{1,0:T(8,128)(2,1)S(1)}, bf16[64,1024]{1,0:T(8,128)(2,1)S(1)}, u32[]{:S(2)}, u32[]{:S(2)}) collective-permute-start(bf16[64,1024]{1,0:T(8,128)(2,1)S(1)} %add.80.held_ref), channel_id=1, source_target_pairs={{0,1},{1,0},{2,3},{3,2},{4,5},{5,4},{6,7},{7,6},{8,9},{9,8},{10,11... | collective-permute-start | bytes 393224 | tf_op jit(solution)/shard_map/ppermute | solution.py:238
  26.8 1.0 %copy-start.2 = (bf16[1,128,1024]{2,1,0:T(8,128)(2,1)S(1)}, bf16[1,128,1024]{2,1,0:T(8,128)(2,1)}, u32[]{:S(2)}) copy-start(bf16[1,128,1024]{2,1,0:T(8,128)(2,1)} %param.7) | copy-start | bytes 786436
  27.7 1.1 %copy-start.6 = (bf16[1,128,3072]{2,1,0:T(8,128)(2,1)S(1)}, bf16[1,128,3072]{2,1,0:T(8,128)(2,1)}, u32[]{:S(2)}) copy-start(bf16[1,128,3072]{2,1,0:T(8,128)(2,1)} %param.6) | copy-start | bytes 2359300
  28.9 2.1 %copy-start.5 = (bf16[128,3072]{1,0:T(8,128)(2,1)S(1)}, bf16[128,3072]{1,0:T(8,128)(2,1)}, u32[]{:S(2)}) copy-start(bf16[128,3072]{1,0:T(8,128)(2,1)} %loss_ref.1) | copy-start | bytes 2359300
  33.9 1.4 %collective-permute-start.9 = (bf16[2,64,512]{2,1,0:T(8,128)(2,1)S(1)}, bf16[2,64,512]{2,1,0:T(8,128)(2,1)S(1)}, u32[]{:S(2)}, u32[]{:S(2)}) collective-permute-start(bf16[2,64,512]{2,1,0:T(8,128)(2,1)S(1)} %get-tuple-element.25), channel_id=1, source_target_pairs={{0,1},{1,0},{2,3},{3,2},{4,5},{5,4},{6,7},{7,6},{8,9},{9,8},{10,11... | collective-permute-start | bytes 393224 | tf_op jit(solution)/shard_map/ppermute | solution.py:238
  35.3 4.2 %collective-permute-start.10 = (bf16[2,64,512]{2,1,0:T(8,128)(2,1)S(1)}, bf16[2,64,512]{2,1,0:T(8,128)(2,1)S(1)}, u32[]{:S(2)}, u32[]{:S(2)}) collective-permute-start(bf16[2,64,512]{2,1,0:T(8,128)(2,1)S(1)} %fusion), channel_id=1, source_target_pairs={{0,2},{1,5},{2,0},{3,7},{4,6},{5,1},{6,4},{7,3},{8,10},{9,13},{10,... | collective-permute-start | bytes 393224 | tf_op jit(solution)/shard_map/ppermute | solution.py:238
  39.5 6.0 %collective-permute-start.11 = (bf16[2,64,512]{2,1,0:T(8,128)(2,1)S(1)}, bf16[2,64,512]{2,1,0:T(8,128)(2,1)S(1)}, u32[]{:S(2)}, u32[]{:S(2)}) collective-permute-start(bf16[2,64,512]{2,1,0:T(8,128)(2,1)S(1)} %fusion.2), channel_id=1, source_target_pairs={{0,4},{1,9},{2,6},{3,11},{4,0},{5,13},{6,2},{7,15},{8,12},{9,1},{1... | collective-permute-start | bytes 393224 | tf_op jit(solution)/shard_map/ppermute | solution.py:238
  45.6 9.4 %collective-permute-start.12 = (bf16[2,64,512]{2,1,0:T(8,128)(2,1)S(1)}, bf16[2,64,512]{2,1,0:T(8,128)(2,1)S(1)}, u32[]{:S(2)}, u32[]{:S(2)}) collective-permute-start(bf16[2,64,512]{2,1,0:T(8,128)(2,1)S(1)} %fusion.1), channel_id=1, source_target_pairs={{0,8},{1,3},{2,10},{3,1},{4,12},{5,7},{6,14},{7,5},{8,0},{9,11},{1... | collective-permute-start | bytes 393224 | tf_op jit(solution)/shard_map/ppermute | solution.py:238
  45.7 17.8 %copy-start.4 = (s32[1,2]{1,0:T(1,128)S(1)}, s32[1,2]{1,0:T(1,128)}, u32[]{:S(2)}) copy-start(s32[1,2]{1,0:T(1,128)} %ids_ref.3) | copy-start | bytes 28
  48.6 6.6 %collective-permute-start.7 = (bf16[2,128,512]{2,1,0:T(8,128)(2,1)S(1)}, bf16[2,128,512]{2,1,0:T(8,128)(2,1)S(1)}, u32[]{:S(2)}, u32[]{:S(2)}) collective-permute-start(bf16[2,128,512]{2,1,0:T(8,128)(2,1)S(1)} %get-tuple-element.22), channel_id=1, source_target_pairs={{0,1},{1,0},{2,3},{3,2},{4,5},{5,4},{6,7},{7,6},{8,9},{9,8},{10,11... | collective-permute-start | bytes 786440 | tf_op jit(solution)/shard_map/ppermute | solution.py:238
  53.0 10.5 %collective-permute-start.8 = (bf16[2,128,512]{2,1,0:T(8,128)(2,1)S(1)}, bf16[2,128,512]{2,1,0:T(8,128)(2,1)S(1)}, u32[]{:S(2)}, u32[]{:S(2)}) collective-permute-start(bf16[2,128,512]{2,1,0:T(8,128)(2,1)S(1)} %get-tuple-element.23), channel_id=1, source_target_pairs={{1,2},{3,4},{5,6},{7,8},{9,10},{11,12},{13,14},{2,1},{4,3},{6,5},{... | collective-permute-start | bytes 786440 | tf_op jit(solution)/shard_map/ppermute | solution.py:238
  55.1 8.4 %collective-permute-start.13 = (bf16[2,64,512]{2,1,0:T(8,128)(2,1)S(1)}, bf16[2,64,512]{2,1,0:T(8,128)(2,1)S(1)}, u32[]{:S(2)}, u32[]{:S(2)}) collective-permute-start(bf16[2,64,512]{2,1,0:T(8,128)(2,1)S(1)} %add_convert_fusion.half_ref), channel_id=1, source_target_pairs={{0,1},{1,0},{2,3},{3,2},{4,5},{5,4},{6,7},{7,6},{8,9},{9,8},{10,11... | collective-permute-start | bytes 393224 | tf_op jit(solution)/shard_map/ppermute | solution.py:238

commit v3 on v2

--- a/solution.py
+++ b/solution.py
@@ -1,4 +1,3 @@
-import functools
 import math
 
 import jax
@@ -8,7 +7,7 @@
 from jax.experimental.pallas import tpu as pltpu
 from jax.sharding import PartitionSpec as P
 
-HQ = 24
+
 KEY_HEADS = 4
 HEAD_SIZE = 128
 BLOCK_TOKENS = 64
@@ -25,6 +24,7 @@
 TN = (((0,), (0,)), ((), ()))
 F32 = jnp.float32
 BF = jnp.bfloat16
+HBM = pl.BlockSpec(memory_space=pltpu.HBM)
 VMEM = pl.BlockSpec(memory_space=pltpu.VMEM)
 SMEM = pl.BlockSpec(memory_space=pltpu.SMEM)
 
@@ -33,15 +33,15 @@
     return lax.dot_general(a, b, dims, preferred_element_type=F32)
 
 
-def call(kernel, name, ins, outs, args, flops):
+def call(kernel, ins, outs, args, flops, scratch=()):
     return pl.pallas_call(
         kernel,
         in_specs=ins,
         out_specs=[VMEM] * len(outs),
         out_shape=outs,
+        scratch_shapes=scratch,
         compiler_params=pltpu.CompilerParams(vmem_limit_bytes=24 << 20),
         cost_estimate=pl.CostEstimate(flops=flops, bytes_accessed=flops // 500, transcendentals=0),
-        name=name,
     )(*args)
 
 
@@ -67,20 +67,30 @@
     return lax.axis_index("section") == lax.axis_size("section") - 1
 
 
-def pick_kernel(ids_ref, own_ref, on_ref, out_ref):
-    nb = own_ref.shape[0] // BLOCK_TOKENS
+def load_kernel(a_ref, b_ref, c_ref, a_out, b_out, c_out, sems):
+    copies = [
+        pltpu.make_async_copy(src, dst, sems.at[i])
+        for i, (src, dst) in enumerate(((a_ref, a_out), (b_ref, b_out), (c_ref, c_out)))
+    ]
+    for copy in copies:
+        copy.start()
+    for copy in copies:
+        copy.wait()
+
+
+def pick_kernel(table_ref, own_ref, on_ref, out_ref, sem):
     pos = lax.axis_index("seq")
     core = lax.rem(pos, 2)
-    block = ids_ref[0, core]
-    owner = lax.div(block, nb)
-    row = pl.multiple_of(lax.rem(block, nb) * BLOCK_TOKENS, BLOCK_TOKENS)
-    twin = pos + 1 - 2 * core
+    owner = table_ref[0, core]
+    row = pl.multiple_of(table_ref[1, core] * BLOCK_TOKENS, BLOCK_TOKENS)
     mine = owner == pos
-    theirs = owner == twin
+    theirs = owner == pos + 1 - 2 * core
 
     @pl.when(mine)
     def _():
-        out_ref[...] = own_ref[pl.ds(row, BLOCK_TOKENS), :]
+        copy = pltpu.make_async_copy(own_ref.at[pl.ds(row, BLOCK_TOKENS)], out_ref, sem)
+        copy.start()
+        copy.wait()
 
     @pl.when(theirs)
     def _():
@@ -158,18 +168,31 @@
             give_ref[i, :, cols] = grad[BLOCK_TOKENS:].astype(BF)
 
 
-def rest_kernel(
-    q_ref, do_ref, own_ref, on_ref, off_ref, held_ref, other_ref, w_ref, dp_ref, ds_ref, stat_ref,
-    dq_ref, g_own, g_on, g_off,
-):
+def local_ds(w_ref, dp_ref, stat_ref, g):
+    p = w_ref[g] * stat_ref[g, 0:1, :]
+    return p, (p * (dp_ref[g] - stat_ref[g, 1:2, :]) * SCALE).astype(BF)
+
+
+def pairs_kernel(q_ref, do_ref, w_ref, dp_ref, stat_ref, g_own, g_on, g_off, ds_ref):
     toks = q_ref.shape[0]
     for g in range(KEY_HEADS):
-        kc = g * HEAD_SIZE
-        keys = stacked((own_ref, on_ref, off_ref, held_ref, other_ref), kc)
-        p = w_ref[g] * stat_ref[g, 0:1, :]
-        ds = (p * (dp_ref[g] - stat_ref[g, 1:2, :]) * SCALE).astype(BF)
-        ds_all = jnp.concatenate([ds, ds_ref[g]], 0)
-        dq = dot(keys, ds_all, TN).T
+        p, ds = local_ds(w_ref, dp_ref, stat_ref, g)
+        ds_ref[g] = ds
+        cols = slice(g * HEAD_SIZE, (g + 1) * HEAD_SIZE)
+        grads = (dot(ds, group_rows(q_ref, g), NN), dot(p.astype(BF), group_rows(do_ref, g), NN))
+        for i, grad in enumerate(grads):
+            g_own[i, :, cols] = grad[:toks]
+            g_on[i, :, cols] = grad[toks : 2 * toks].astype(BF)
+            g_off[i, :, cols] = grad[2 * toks :].astype(BF)
+
+
+def queries_kernel(
+    own_ref, on_ref, off_ref, held_ref, other_ref, ds_local_ref, ds_global_ref, dq_ref
+):
+    toks = dq_ref.shape[0]
+    for g in range(KEY_HEADS):
+        keys = stacked((own_ref, on_ref, off_ref, held_ref, other_ref), g * HEAD_SIZE)
+        dq = dot(keys, jnp.concatenate([ds_local_ref[g], ds_global_ref[g]], 0), TN).T
         for e in range(toks // BLOCK_TOKENS):
             for h in range(GROUP_HEADS):
                 r = e * ROWS_E + h * BLOCK_TOKENS
@@ -177,23 +200,13 @@
                 dq_ref[e * BLOCK_TOKENS : (e + 1) * BLOCK_TOKENS, c : c + HEAD_SIZE] = (
                     dq[r : r + BLOCK_TOKENS].astype(BF)
                 )
-        cols = slice(kc, kc + HEAD_SIZE)
-        grads = (dot(ds, group_rows(q_ref, g), NN), dot(p.astype(BF), group_rows(do_ref, g), NN))
-        for i, grad in enumerate(grads):
-            g_own[i, :, cols] = grad[:toks]
-            g_on[i, :, cols] = grad[toks : 2 * toks].astype(BF)
-            g_off[i, :, cols] = grad[2 * toks :].astype(BF)
-
-
-def finish_kernel(ids_ref, g_own, r_on, r_off, half_ref, half_other_ref, out_ref):
+
+
+def finish_kernel(place_ref, g_own, r_on, r_off, half_ref, half_other_ref, out_ref):
     toks = g_own.shape[1]
     nb = toks // BLOCK_TOKENS
-    pos = lax.axis_index("seq")
-    core = lax.rem(pos, 2)
-    places = []
-    for which in (core, 1 - core):
-        block = ids_ref[0, which]
-        places.append(jnp.where(lax.div(block, nb) == pos, lax.rem(block, nb), -1))
+    core = lax.rem(lax.axis_index("seq"), 2)
+    places = (place_ref[core], place_ref[1 - core])
     for i in range(2):
         for s in range(nb):
             rows = slice(s * BLOCK_TOKENS, (s + 1) * BLOCK_TOKENS)
@@ -235,17 +248,26 @@
     hops = [
         [(i, i ^ (1 << orders[i % 2][r])) for i in range(peers)] for r in range(bits - 1)
     ]
-    exchange = lambda x, pairs: lax.ppermute(x, "seq", pairs)
+
+    def exchange(x, pairs, axis="seq"):
+        return lax.ppermute(x, axis, pairs)
 
     q = queries[0]
     own = packed_key_value[0]
     on = exchange(own, twin)
-    shifted = lax.ppermute(incoming[0], "section", [(i, i - 1) for i in range(1, sections)])
+    shifted = exchange(incoming[0], [(i, i - 1) for i in range(1, sections)], "section")
+    table = jnp.concatenate([global_blocks // nb, global_blocks % nb], 0)
     (held,) = call(
-        pick_kernel, "pick", [SMEM, VMEM, VMEM], [shape(BLOCK_TOKENS, own.shape[1], dtype=BF)],
-        (global_blocks, own, on), 10**6,
+        pick_kernel, [SMEM, HBM, VMEM],
+        [shape(BLOCK_TOKENS, own.shape[1], dtype=BF)],
+        (table, own, on), 10**6, [pltpu.SemaphoreType.DMA],
     )
     off = exchange(own, side)
+    own, q, loss_grad = call(
+        load_kernel, [HBM] * 3,
+        [shape(*x.shape, dtype=BF) for x in (own, q, loss_grad)],
+        (own, q, loss_grad), 10**7, [pltpu.SemaphoreType.DMA((3,))],
+    )
     for hop in hops:
         held = held + exchange(held, hop)
     other = exchange(held, twin)
@@ -253,12 +275,12 @@
     bias = list_bias(random_blocks[0], pos, peers, nb)
     near = (own, on, off)
     w, stats = call(
-        local_kernel, "local", [SMEM] + [VMEM] * 4,
+        local_kernel, [SMEM] + [VMEM] * 4,
         [shape(KEY_HEADS, 3 * toks, rows), shape(KEY_HEADS, 8, rows)],
         (bias, q) + near, 3 * 10**9,
     )
     dp, ds, stats, keep, give, d_out = call(
-        global_kernel, "globals", [VMEM] * 10,
+        global_kernel, [VMEM] * 10,
         [
             shape(KEY_HEADS, 3 * toks, rows),
             shape(KEY_HEADS, GLOB_ROWS, rows, dtype=BF),
@@ -270,16 +292,21 @@
         (q, shifted, loss_grad) + near + (held, other, w, stats), 3 * 10**9,
     )
     total = keep + exchange(give, twin).astype(F32)
-    dq, g_own, g_on, g_off = call(
-        rest_kernel, "rest", [VMEM] * 11,
+    g_own, g_on, g_off, ds_local = call(
+        pairs_kernel, [VMEM] * 5,
         [
-            shape(*q.shape, dtype=BF),
             shape(2, toks, WIDTH),
             shape(2, toks, WIDTH, dtype=BF),
             shape(2, toks, WIDTH, dtype=BF),
+            shape(KEY_HEADS, 3 * toks, rows, dtype=BF),
         ],
-        (q, d_out) + near + (held, other, w, dp, ds, stats), 5 * 10**9,
-    )
+        (q, d_out, w, dp, stats), 3 * 10**9,
+    )
+    (dq,) = call(
+        queries_kernel, [VMEM] * 7, [shape(*q.shape, dtype=BF)],
+        near + (held, other, ds_local, ds), 2 * 10**9,
+    )
+    place = jnp.where(table[0] == pos, table[1], -1)
     r_on = exchange(g_on, twin)
     r_off = exchange(g_off, side)
     for hop in hops:
@@ -287,8 +314,8 @@
     half = total.astype(BF)
     half_other = exchange(half, twin)
     (out,) = call(
-        finish_kernel, "finish", [SMEM] + [VMEM] * 5, [shape(*own.shape, dtype=BF)],
-        (global_blocks, g_own, r_on, r_off, half, half_other), 10**6,
+        finish_kernel, [SMEM] + [VMEM] * 5, [shape(*own.shape, dtype=BF)],
+        (place, g_own, r_on, r_off, half, half_other), 10**6,
     )
     return (dq[None], out[None])
 

time: 65.2 us -> 61.9 us (0.949)
  waiting for transfers between devices: 26.4 us -> 21.8 us
    ppermute x14, waiting for transfers between devices: 26.4 us -> 21.8 us  [exchange(): return lax.ppermute(x, axis, pairs)]
    select_n x0 -> x1, other arithmetic: none -> 0.67 us  [body(): place = jnp.where(table[0] == pos, table[1], -1)]
    unnamed x14 -> x10, local copies, waits for them, and re-layouts: 3.71 us -> 4.18 us
    pallas_call x5 -> x7, Pallas kernels: 9.83 us -> 10.2 us  [call(): pl.pallas_call(kernel, in_specs=ins, out_specs=[VMEM] * len(outs), out_sh...]
  transfers between devices with their start and end apart: 14 -> 14, of which waited for: 7 -> 6; matrix products, arithmetic and copies ran while one was open for 1% -> 2% of each run, Pallas kernels for 9% -> 10%
where the time goes in v3:
time: 61.9 us; the launch traced here: 61.6 us
  starting transfers between devices  23.1 us (37%)
  waiting for transfers between devices  21.8 us (35%)
  Pallas kernels  10.2 us (16%)
  local copies, waits for them, and re-layouts  4.45 us (7%)
  other arithmetic  1.26 us (2%)
  between operations  0.82 us (1%)
    ppermute x14, starting transfers between devices, exchange(): return lax.ppermute(x, axis, pairs)  23.1 us
    ppermute x14, waiting for transfers between devices, exchange(): return lax.ppermute(x, axis, pairs)  21.8 us
    pallas_call x7, Pallas kernels, call(): pl.pallas_call(kernel, in_specs=ins, out_specs=[VMEM] * len(outs), out_sh...  10.2 us
    unnamed x10, local copies, waits for them, and re-layouts  4.18 us
  transfers between devices with their start and end apart: 14, of which 6 were waited for; matrix products, arithmetic and copies ran while one was open for 2% of the time, Pallas kernels for 10%

profile of v3, /device:TPU:11, one launch (start us, length us, event | category | flops | bytes accessed | tf_op | source)
XLA Modules:
  0.0 61.6 jit_solution(2029807367531333226)
XLA Ops:
  0.6 0.7 %collective-permute-start = (bf16[128,1024]{1,0:T(8,128)(2,1)}, bf16[128,1024]{1,0:T(8,128)(2,1)S(1)}, u32[]{:S(2)}, u32[]{:S(2)}) collective-permute-start(bf16[128,1024]{1,0:T(8,128)(2,1)} %bitcast.9), channel_id=1, source_target_pairs={{0,1},{1,0},{2,3},{3,2},{4,5},{5,4},{6,7},{7,6},{8,9},{9,8},{10,11... | collective-permute-start | bytes 786440 | tf_op jit(solution)/shard_map/ppermute | solution.py:253
  1.4 3.1 %collective-permute-start.1 = (bf16[128,1024]{1,0:T(8,128)(2,1)}, bf16[128,1024]{1,0:T(8,128)(2,1)S(1)}, u32[]{:S(2)}, u32[]{:S(2)}) collective-permute-start(bf16[128,1024]{1,0:T(8,128)(2,1)} %bitcast.10), channel_id=1, source_target_pairs={{1,2},{3,4},{5,6},{7,8},{9,10},{11,12},{13,14},{2,1},{4,3},{6,5},{... | collective-permute-start | bytes 786440 | tf_op jit(solution)/shard_map/ppermute | solution.py:253
  4.4 2.2 %collective-permute-start.6 = (bf16[128,3072]{1,0:T(8,128)(2,1)}, bf16[128,3072]{1,0:T(8,128)(2,1)S(1)}, u32[]{:S(2)}, u32[]{:S(2)}) collective-permute-start(bf16[128,3072]{1,0:T(8,128)(2,1)} %bitcast.15), channel_id=1, source_target_pairs={{16,0},{17,1},{18,2},{19,3},{20,4},{21,5},{22,6},{23,7},{24,8},{25... | collective-permute-start | bytes 2359304 | tf_op jit(solution)/shard_map/ppermute | solution.py:253
  6.7 0.7 %fusion.2 = (s32[2]{0:T(128)S(1)}, s32[1,2]{1,0:T(1,128)S(1)}, s32[1,2]{1,0:T(1,128)S(1)}) fusion(s32[]{:T(128)S(6)} %axis_index.12, s32[1,2]{1,0:T(1,128)} %param.10), kind=kLoop, calls=%fused_computation.18 | loop fusion | flops 42 | bytes 36 | tf_op jit(solution)/shard_map/jit(_where)/select_n | solution.py:309
  7.5 0.9 %copy-done.1 = bf16[1,128,1024]{2,1,0:T(8,128)(2,1)S(1)} copy-done((bf16[1,128,1024]{2,1,0:T(8,128)(2,1)S(1)}, bf16[1,128,1024]{2,1,0:T(8,128)(2,1)}, u32[]{:S(2)}) %copy-start.1) | copy-done | bytes 262168
  8.4 0.6 shard_map.78
  9.0 0.2 collective-permute-start.2
  9.3 3.9 %collective-permute-done.2 = bf16[64,1024]{1,0:T(8,128)(2,1)S(1)} collective-permute-done((bf16[64,1024]{1,0:T(8,128)(2,1)S(1)}, bf16[64,1024]{1,0:T(8,128)(2,1)S(1)}, u32[]{:S(2)}, u32[]{:S(2)}) %collective-permute-start.2) | collective-permute-done | bytes 131104 | tf_op jit(solution)/shard_map/ppermute | solution.py:253
  13.2 2.4 %collective-permute-start.3 = (bf16[64,1024]{1,0:T(8,128)(2,1)S(1)}, bf16[64,1024]{1,0:T(8,128)(2,1)S(1)}, u32[]{:S(2)}, u32[]{:S(2)}) collective-permute-start(bf16[64,1024]{1,0:T(8,128)(2,1)S(1)} %add.86), channel_id=1, source_target_pairs={{0,4},{1,9},{2,6},{3,11},{4,0},{5,13},{6,2},{7,15},{8,12},{9,1},{1... | collective-permute-start | bytes 393224 | tf_op jit(solution)/shard_map/ppermute | solution.py:253
  15.7 0.1 copy.11
  15.9 2.9 %collective-permute-done.3 = bf16[64,1024]{1,0:T(8,128)(2,1)S(1)} collective-permute-done((bf16[64,1024]{1,0:T(8,128)(2,1)S(1)}, bf16[64,1024]{1,0:T(8,128)(2,1)S(1)}, u32[]{:S(2)}, u32[]{:S(2)}) %collective-permute-start.3) | collective-permute-done | bytes 131104 | tf_op jit(solution)/shard_map/ppermute | solution.py:253
  18.9 0.8 %collective-permute-start.4 = (bf16[64,1024]{1,0:T(8,128)(2,1)S(1)}, bf16[64,1024]{1,0:T(8,128)(2,1)S(1)}, u32[]{:S(2)}, u32[]{:S(2)}) collective-permute-start(bf16[64,1024]{1,0:T(8,128)(2,1)S(1)} %add.87), channel_id=1, source_target_pairs={{0,8},{1,3},{2,10},{3,1},{4,12},{5,7},{6,14},{7,5},{8,0},{9,11},{1... | collective-permute-start | bytes 393224 | tf_op jit(solution)/shard_map/ppermute | solution.py:253
  19.8 1.0 %copy-done.2 = bf16[1,128,1024]{2,1,0:T(8,128)(2,1)S(1)} copy-done((bf16[1,128,1024]{2,1,0:T(8,128)(2,1)S(1)}, bf16[1,128,1024]{2,1,0:T(8,128)(2,1)}, u32[]{:S(2)}) %copy-start.2) | copy-done | bytes 262168
  20.7 1.1 %copy-done.3 = bf16[1,128,3072]{2,1,0:T(8,128)(2,1)S(1)} copy-done((bf16[1,128,3072]{2,1,0:T(8,128)(2,1)S(1)}, bf16[1,128,3072]{2,1,0:T(8,128)(2,1)}, u32[]{:S(2)}) %copy-start.3) | copy-done | bytes 786456
  21.9 1.1 %copy-done.4 = bf16[128,3072]{1,0:T(8,128)(2,1)S(1)} copy-done((bf16[128,3072]{1,0:T(8,128)(2,1)S(1)}, bf16[128,3072]{1,0:T(8,128)(2,1)}, u32[]{:S(2)}) %copy-start.4) | copy-done | bytes 786456
  23.0 0.2 shard_map.77
  23.2 4.1 %collective-permute-start.5 = (bf16[64,1024]{1,0:T(8,128)(2,1)S(1)}, bf16[64,1024]{1,0:T(8,128)(2,1)S(1)}, u32[]{:S(2)}, u32[]{:S(2)}) collective-permute-start(bf16[64,1024]{1,0:T(8,128)(2,1)S(1)} %add.88.held_ref), channel_id=1, source_target_pairs={{0,1},{1,0},{2,3},{3,2},{4,5},{5,4},{6,7},{7,6},{8,9},{9,8},{10,11... | collective-permute-start | bytes 393224 | tf_op jit(solution)/shard_map/ppermute | solution.py:253
  27.4 2.1 %shard_map.79 = (f32[4,384,768]{2,1,0:T(8,128)S(1)}, f32[4,8,768]{2,1,0:T(8,128)S(1)}) custom-call(f32[2,24]{1,0:T(2,128)S(1)} %reshape.100.bias_ref, bf16[128,3072]{1,0:T(8,128)(2,1)S(1)} %get-tuple-element.18.q_ref, bf16[128,1024]{1,0:T(8,128)(2,1)S(1)} %get-tuple-element.17.own_ref, bf16[128,1024]{1,0:T(8,128)(2,1)S(1)} %collective-permute-done.on_ref, ...), custom_call_target="tpu_custom_call" | custom-call | flops 3000000000 | bytes 6000000 | tf_op jit(solution)/shard_map/pallas_call | solution.py:37
  29.5 2.9 %shard_map.80 = (f32[4,384,768]{2,1,0:T(8,128)S(1)}, bf16[4,128,768]{2,1,0:T(8,128)(2,1)S(1)}, f32[4,8,768]{2,1,0:T(8,128)S(1)}, f32[2,64,512]{2,1,0:T(8,128)S(1...) custom-call(bf16[128,3072]{1,0:T(8,128)(2,1)S(1)} %get-tuple-element.18.q_ref, ...), custom_call_target="tpu_custom_call" | custom-call | flops 3000000000 | bytes 6000000 | tf_op jit(solution)/shard_map/pallas_call | solution.py:37
  32.3 0.1 collective-permute-start.9
  32.4 1.3 %collective-permute-done.9 = bf16[2,64,512]{2,1,0:T(8,128)(2,1)S(1)} collective-permute-done((bf16[2,64,512]{2,1,0:T(8,128)(2,1)S(1)}, bf16[2,64,512]{2,1,0:T(8,128)(2,1)S(1)}, u32[]{:S(2)}, u32[]{:S(2)}) %collective-permute-start.9) | collective-permute-done | bytes 131104 | tf_op jit(solution)/shard_map/ppermute | solution.py:253
  33.9 4.1 %collective-permute-done.10 = bf16[2,64,512]{2,1,0:T(8,128)(2,1)S(1)} collective-permute-done((bf16[2,64,512]{2,1,0:T(8,128)(2,1)S(1)}, bf16[2,64,512]{2,1,0:T(8,128)(2,1)S(1)}, u32[]{:S(2)}, u32[]{:S(2)}) %collective-permute-start.10) | collective-permute-done | bytes 131104 | tf_op jit(solution)/shard_map/ppermute | solution.py:253
  38.0 2.5 %collective-permute-start.11 = (bf16[2,64,512]{2,1,0:T(8,128)(2,1)S(1)}, bf16[2,64,512]{2,1,0:T(8,128)(2,1)S(1)}, u32[]{:S(2)}, u32[]{:S(2)}) collective-permute-start(bf16[2,64,512]{2,1,0:T(8,128)(2,1)S(1)} %fusion.3), channel_id=1, source_target_pairs={{0,4},{1,9},{2,6},{3,11},{4,0},{5,13},{6,2},{7,15},{8,12},{9,1},{1... | collective-permute-start | bytes 393224 | tf_op jit(solution)/shard_map/ppermute | solution.py:253
  40.5 2.7 %collective-permute-done.11 = bf16[2,64,512]{2,1,0:T(8,128)(2,1)S(1)} collective-permute-done((bf16[2,64,512]{2,1,0:T(8,128)(2,1)S(1)}, bf16[2,64,512]{2,1,0:T(8,128)(2,1)S(1)}, u32[]{:S(2)}, u32[]{:S(2)}) %collective-permute-start.11) | collective-permute-done | bytes 131104 | tf_op jit(solution)/shard_map/ppermute | solution.py:253
  43.4 0.2 collective-permute-start.12
  43.5 1.5 %shard_map.81 = (f32[2,128,512]{2,1,0:T(8,128)S(1)}, bf16[2,128,512]{2,1,0:T(8,128)(2,1)S(1)}, bf16[2,128,512]{2,1,0:T(8,128)(2,1)S(1)}, bf16[4,384,768]{2,1,0:T(8,128)(2,1)S(1)}) custom-call(bf16[128,3072]{1,0:T(8,128)(2,1)S(1)} %get-tuple-element.18.q_ref, bf16[128,3072]{1,0:T(8,128)(2,1)S(1)} %get-tuple-element.22.do_ref, ...), custom_call_target="tpu_custom_call" | custom-call | flops 3000000000 | bytes 6000000 | tf_op jit(solution)/shard_map/pallas_call | solution.py:37
  45.0 4.7 %collective-permute-start.7 = (bf16[2,128,512]{2,1,0:T(8,128)(2,1)S(1)}, bf16[2,128,512]{2,1,0:T(8,128)(2,1)S(1)}, u32[]{:S(2)}, u32[]{:S(2)}) collective-permute-start(bf16[2,128,512]{2,1,0:T(8,128)(2,1)S(1)} %get-tuple-element.28), channel_id=1, source_target_pairs={{0,1},{1,0},{2,3},{3,2},{4,5},{5,4},{6,7},{7,6},{8,9},{9,8},{10,11... | collective-permute-start | bytes 786440 | tf_op jit(solution)/shard_map/ppermute | solution.py:253
  49.7 1.9 %collective-permute-start.8 = (bf16[2,128,512]{2,1,0:T(8,128)(2,1)S(1)}, bf16[2,128,512]{2,1,0:T(8,128)(2,1)S(1)}, u32[]{:S(2)}, u32[]{:S(2)}) collective-permute-start(bf16[2,128,512]{2,1,0:T(8,128)(2,1)S(1)} %get-tuple-element.29), channel_id=1, source_target_pairs={{1,2},{3,4},{5,6},{7,8},{9,10},{11,12},{13,14},{2,1},{4,3},{6,5},{... | collective-permute-start | bytes 786440 | tf_op jit(solution)/shard_map/ppermute | solution.py:253
  51.6 0.1 add_convert_fusion.half_ref
  51.8 1.6 %shard_map.82 = bf16[128,3072]{1,0:T(8,128)(2,1)} custom-call(bf16[128,1024]{1,0:T(8,128)(2,1)S(1)} %get-tuple-element.17.own_ref, bf16[128,1024]{1,0:T(8,128)(2,1)S(1)} %collective-permute-done.on_ref, bf16[128,1024]{1,0:T(8,128)(2,1)S(1)} %collective-permute-done.1.off_ref, bf16[64,1024]{1,0:T(8,128)(2,1)S(1)} %add.88.held_ref, ...), custom_call_target="tpu_custom_call" | custom-call | flops 2000000000 | bytes 4000000 | tf_op jit(solution)/shard_map/pallas_call | solution.py:37
  53.4 6.8 %collective-permute-done.8.r_off = bf16[2,128,512]{2,1,0:T(8,128)(2,1)S(1)} collective-permute-done((bf16[2,128,512]{2,1,0:T(8,128)(2,1)S(1)}, bf16[2,128,512]{2,1,0:T(8,128)(2,1)S(1)}, u32[]{:S(2)}, u32[]{:S(2)}) %collective-permute-start.8) | collective-permute-done | bytes 262176 | tf_op jit(solution)/shard_map/ppermute | solution.py:253
  60.2 1.4 %shard_map.83 = bf16[128,1024]{1,0:T(8,128)(2,1)} custom-call(s32[2]{0:T(128)S(1)} %get-tuple-element.32.place_ref, f32[2,128,512]{2,1,0:T(8,128)S(1)} %get-tuple-element.27.g_own, bf16[2,128,512]{2,1,0:T(8,128)(2,1)S(1)} %collective-permute-done.7.r_on, bf16[2,128,512]{2,1,0:T(8,128)(2,1)S(1)} %collective-permute-done.8.r_off, ...), custom_call_target="tpu_custom_call" | custom-call | flops 1000000 | bytes 2000 | tf_op jit(solution)/shard_map/pallas_call | solution.py:37
  (31 shorter events, 0.8 us)
Async XLA Ops:
  0.6 15.0 %copy-start = (s32[1,32,4,3]{1,2,3,0:T(4,128)S(1)}, s32[1,32,4,3]{1,2,3,0:T(4,128)}, u32[]{:S(2)}) copy-start(s32[1,32,4,3]{1,2,3,0:T(4,128)} %param.11) | copy-start | bytes 4612
  0.6 6.8 %collective-permute-start = (bf16[128,1024]{1,0:T(8,128)(2,1)}, bf16[128,1024]{1,0:T(8,128)(2,1)S(1)}, u32[]{:S(2)}, u32[]{:S(2)}) collective-permute-start(bf16[128,1024]{1,0:T(8,128)(2,1)} %bitcast.9), channel_id=1, source_target_pairs={{0,1},{1,0},{2,3},{3,2},{4,5},{5,4},{6,7},{7,6},{8,9},{9,8},{10,11... | collective-permute-start | bytes 786440 | tf_op jit(solution)/shard_map/ppermute | solution.py:253
  1.4 26.0 %collective-permute-start.1 = (bf16[128,1024]{1,0:T(8,128)(2,1)}, bf16[128,1024]{1,0:T(8,128)(2,1)S(1)}, u32[]{:S(2)}, u32[]{:S(2)}) collective-permute-start(bf16[128,1024]{1,0:T(8,128)(2,1)} %bitcast.10), channel_id=1, source_target_pairs={{1,2},{3,4},{5,6},{7,8},{9,10},{11,12},{13,14},{2,1},{4,3},{6,5},{... | collective-permute-start | bytes 786440 | tf_op jit(solution)/shard_map/ppermute | solution.py:253
  4.4 25.0 %collective-permute-start.6 = (bf16[128,3072]{1,0:T(8,128)(2,1)}, bf16[128,3072]{1,0:T(8,128)(2,1)S(1)}, u32[]{:S(2)}, u32[]{:S(2)}) collective-permute-start(bf16[128,3072]{1,0:T(8,128)(2,1)} %bitcast.15), channel_id=1, source_target_pairs={{16,0},{17,1},{18,2},{19,3},{20,4},{21,5},{22,6},{23,7},{24,8},{25... | collective-permute-start | bytes 2359304 | tf_op jit(solution)/shard_map/ppermute | solution.py:253
  7.5 1.0 %copy-start.1 = (bf16[1,128,1024]{2,1,0:T(8,128)(2,1)S(1)}, bf16[1,128,1024]{2,1,0:T(8,128)(2,1)}, u32[]{:S(2)}) copy-start(bf16[1,128,1024]{2,1,0:T(8,128)(2,1)} %param.7) | copy-start | bytes 786436
  9.0 4.2 %collective-permute-start.2 = (bf16[64,1024]{1,0:T(8,128)(2,1)S(1)}, bf16[64,1024]{1,0:T(8,128)(2,1)S(1)}, u32[]{:S(2)}, u32[]{:S(2)}) collective-permute-start(bf16[64,1024]{1,0:T(8,128)(2,1)S(1)} %shard_map.78), channel_id=1, source_target_pairs={{0,2},{1,5},{2,0},{3,7},{4,6},{5,1},{6,4},{7,3},{8,10},{9,13},{10,... | collective-permute-start | bytes 393224 | tf_op jit(solution)/shard_map/ppermute | solution.py:253
  13.2 5.6 %collective-permute-start.3 = (bf16[64,1024]{1,0:T(8,128)(2,1)S(1)}, bf16[64,1024]{1,0:T(8,128)(2,1)S(1)}, u32[]{:S(2)}, u32[]{:S(2)}) collective-permute-start(bf16[64,1024]{1,0:T(8,128)(2,1)S(1)} %add.86), channel_id=1, source_target_pairs={{0,4},{1,9},{2,6},{3,11},{4,0},{5,13},{6,2},{7,15},{8,12},{9,1},{1... | collective-permute-start | bytes 393224 | tf_op jit(solution)/shard_map/ppermute | solution.py:253
  18.9 4.3 %collective-permute-start.4 = (bf16[64,1024]{1,0:T(8,128)(2,1)S(1)}, bf16[64,1024]{1,0:T(8,128)(2,1)S(1)}, u32[]{:S(2)}, u32[]{:S(2)}) collective-permute-start(bf16[64,1024]{1,0:T(8,128)(2,1)S(1)} %add.87), channel_id=1, source_target_pairs={{0,8},{1,3},{2,10},{3,1},{4,12},{5,7},{6,14},{7,5},{8,0},{9,11},{1... | collective-permute-start | bytes 393224 | tf_op jit(solution)/shard_map/ppermute | solution.py:253
  19.8 1.0 %copy-start.2 = (bf16[1,128,1024]{2,1,0:T(8,128)(2,1)S(1)}, bf16[1,128,1024]{2,1,0:T(8,128)(2,1)}, u32[]{:S(2)}) copy-start(bf16[1,128,1024]{2,1,0:T(8,128)(2,1)} %param.7) | copy-start | bytes 786436
  20.7 1.1 %copy-start.3 = (bf16[1,128,3072]{2,1,0:T(8,128)(2,1)S(1)}, bf16[1,128,3072]{2,1,0:T(8,128)(2,1)}, u32[]{:S(2)}) copy-start(bf16[1,128,3072]{2,1,0:T(8,128)(2,1)} %param.6) | copy-start | bytes 2359300
  21.9 1.1 %copy-start.4 = (bf16[128,3072]{1,0:T(8,128)(2,1)S(1)}, bf16[128,3072]{1,0:T(8,128)(2,1)}, u32[]{:S(2)}) copy-start(bf16[128,3072]{1,0:T(8,128)(2,1)} %c_ref.1) | copy-start | bytes 2359300
  23.2 6.2 %collective-permute-start.5 = (bf16[64,1024]{1,0:T(8,128)(2,1)S(1)}, bf16[64,1024]{1,0:T(8,128)(2,1)S(1)}, u32[]{:S(2)}, u32[]{:S(2)}) collective-permute-start(bf16[64,1024]{1,0:T(8,128)(2,1)S(1)} %add.88.held_ref), channel_id=1, source_target_pairs={{0,1},{1,0},{2,3},{3,2},{4,5},{5,4},{6,7},{7,6},{8,9},{9,8},{10,11... | collective-permute-start | bytes 393224 | tf_op jit(solution)/shard_map/ppermute | solution.py:253
  32.3 1.4 %collective-permute-start.9 = (bf16[2,64,512]{2,1,0:T(8,128)(2,1)S(1)}, bf16[2,64,512]{2,1,0:T(8,128)(2,1)S(1)}, u32[]{:S(2)}, u32[]{:S(2)}) collective-permute-start(bf16[2,64,512]{2,1,0:T(8,128)(2,1)S(1)} %get-tuple-element.31), channel_id=1, source_target_pairs={{0,1},{1,0},{2,3},{3,2},{4,5},{5,4},{6,7},{7,6},{8,9},{9,8},{10,11... | collective-permute-start | bytes 393224 | tf_op jit(solution)/shard_map/ppermute | solution.py:253
  33.8 4.2 %collective-permute-start.10 = (bf16[2,64,512]{2,1,0:T(8,128)(2,1)S(1)}, bf16[2,64,512]{2,1,0:T(8,128)(2,1)S(1)}, u32[]{:S(2)}, u32[]{:S(2)}) collective-permute-start(bf16[2,64,512]{2,1,0:T(8,128)(2,1)S(1)} %fusion), channel_id=1, source_target_pairs={{0,2},{1,5},{2,0},{3,7},{4,6},{5,1},{6,4},{7,3},{8,10},{9,13},{10,... | collective-permute-start | bytes 393224 | tf_op jit(solution)/shard_map/ppermute | solution.py:253
  38.0 5.3 %collective-permute-start.11 = (bf16[2,64,512]{2,1,0:T(8,128)(2,1)S(1)}, bf16[2,64,512]{2,1,0:T(8,128)(2,1)S(1)}, u32[]{:S(2)}, u32[]{:S(2)}) collective-permute-start(bf16[2,64,512]{2,1,0:T(8,128)(2,1)S(1)} %fusion.3), channel_id=1, source_target_pairs={{0,4},{1,9},{2,6},{3,11},{4,0},{5,13},{6,2},{7,15},{8,12},{9,1},{1... | collective-permute-start | bytes 393224 | tf_op jit(solution)/shard_map/ppermute | solution.py:253
  43.4 8.3 %collective-permute-start.12 = (bf16[2,64,512]{2,1,0:T(8,128)(2,1)S(1)}, bf16[2,64,512]{2,1,0:T(8,128)(2,1)S(1)}, u32[]{:S(2)}, u32[]{:S(2)}) collective-permute-start(bf16[2,64,512]{2,1,0:T(8,128)(2,1)S(1)} %fusion.1), channel_id=1, source_target_pairs={{0,8},{1,3},{2,10},{3,1},{4,12},{5,7},{6,14},{7,5},{8,0},{9,11},{1... | collective-permute-start | bytes 393224 | tf_op jit(solution)/shard_map/ppermute | solution.py:253
  45.0 8.4 %collective-permute-start.7 = (bf16[2,128,512]{2,1,0:T(8,128)(2,1)S(1)}, bf16[2,128,512]{2,1,0:T(8,128)(2,1)S(1)}, u32[]{:S(2)}, u32[]{:S(2)}) collective-permute-start(bf16[2,128,512]{2,1,0:T(8,128)(2,1)S(1)} %get-tuple-element.28), channel_id=1, source_target_pairs={{0,1},{1,0},{2,3},{3,2},{4,5},{5,4},{6,7},{7,6},{8,9},{9,8},{10,11... | collective-permute-start | bytes 786440 | tf_op jit(solution)/shard_map/ppermute | solution.py:253
  49.7 10.5 %collective-permute-start.8 = (bf16[2,128,512]{2,1,0:T(8,128)(2,1)S(1)}, bf16[2,128,512]{2,1,0:T(8,128)(2,1)S(1)}, u32[]{:S(2)}, u32[]{:S(2)}) collective-permute-start(bf16[2,128,512]{2,1,0:T(8,128)(2,1)S(1)} %get-tuple-element.29), channel_id=1, source_target_pairs={{1,2},{3,4},{5,6},{7,8},{9,10},{11,12},{13,14},{2,1},{4,3},{6,5},{... | collective-permute-start | bytes 786440 | tf_op jit(solution)/shard_map/ppermute | solution.py:253
  51.7 8.5 %collective-permute-start.13 = (bf16[2,64,512]{2,1,0:T(8,128)(2,1)S(1)}, bf16[2,64,512]{2,1,0:T(8,128)(2,1)S(1)}, u32[]{:S(2)}, u32[]{:S(2)}) collective-permute-start(bf16[2,64,512]{2,1,0:T(8,128)(2,1)S(1)} %add_convert_fusion.half_ref), channel_id=1, source_target_pairs={{0,1},{1,0},{2,3},{3,2},{4,5},{5,4},{6,7},{7,6},{8,9},{9,8},{10,11... | collective-permute-start | bytes 393224 | tf_op jit(solution)/shard_map/ppermute | solution.py:253

commit v4 on v3

--- a/solution.py
+++ b/solution.py
@@ -125,9 +125,8 @@
             stat_ref[g, 1:2, cols] = jnp.sum(w, axis=0, keepdims=True)
 
 
-def global_kernel(
-    q_ref, shifted_ref, loss_ref, own_ref, on_ref, off_ref, held_ref, other_ref, w_ref, stat_ref,
-    dp_ref, ds_ref, out_stat_ref, keep_ref, give_ref, do_ref,
+def near_kernel(
+    shifted_ref, loss_ref, own_ref, on_ref, off_ref, w_ref, stat_ref, dp_ref, out_stat_ref, do_ref
 ):
     last = at_last_section()
 
@@ -140,15 +139,22 @@
         do_ref[...] = shifted_ref[...]
 
     for g in range(KEY_HEADS):
+        vals = stacked((own_ref, on_ref, off_ref), WIDTH + g * HEAD_SIZE)
+        dp = dot(vals, group_rows(do_ref, g), NT)
+        dp_ref[g] = dp
+        out_stat_ref[g, 0:2, :] = stat_ref[g, 0:2, :]
+        out_stat_ref[g, 2:3, :] = jnp.sum(w_ref[g] * dp, axis=0, keepdims=True)
+
+
+def global_kernel(
+    q_ref, do_ref, held_ref, other_ref, stat_ref, ds_ref, out_stat_ref, keep_ref, give_ref
+):
+    for g in range(KEY_HEADS):
         kc = g * HEAD_SIZE
-        vc = WIDTH + kc
         qg = group_rows(q_ref, g)
         dog = group_rows(do_ref, g)
         t = dot(stacked((held_ref, other_ref), kc), qg, NT) * (SCALE * LOG2E)
-        dpg = dot(stacked((held_ref, other_ref), vc), dog, NT)
-        dpl = dot(stacked((own_ref, on_ref, off_ref), vc), dog, NT)
-        dp_ref[g] = dpl
-        partial_delta = jnp.sum(w_ref[g] * dpl, axis=0, keepdims=True)
+        dp = dot(stacked((held_ref, other_ref), WIDTH + kc), dog, NT)
         m_local = stat_ref[g, 0:1, :]
         m = jnp.maximum(m_local, jnp.max(t, axis=0, keepdims=True))
         shrink = jnp.exp2(m_local - m)
@@ -157,8 +163,8 @@
         inv = 1.0 / total
         p = w * inv
         local_factor = shrink * inv
-        delta = local_factor * partial_delta + jnp.sum(p * dpg, axis=0, keepdims=True)
-        ds = (p * (dpg - delta) * SCALE).astype(BF)
+        delta = local_factor * stat_ref[g, 2:3, :] + jnp.sum(p * dp, axis=0, keepdims=True)
+        ds = (p * (dp - delta) * SCALE).astype(BF)
         ds_ref[g] = ds
         out_stat_ref[g, 0:1, :] = local_factor
         out_stat_ref[g, 1:2, :] = delta
@@ -202,11 +208,16 @@
                 )
 
 
+def place_kernel(table_ref, out_ref):
+    here = table_ref[0:1, :] == lax.axis_index("seq")
+    out_ref[...] = jnp.where(here, table_ref[1:2, :], -1)
+
+
 def finish_kernel(place_ref, g_own, r_on, r_off, half_ref, half_other_ref, out_ref):
     toks = g_own.shape[1]
     nb = toks // BLOCK_TOKENS
     core = lax.rem(lax.axis_index("seq"), 2)
-    places = (place_ref[core], place_ref[1 - core])
+    places = (place_ref[0, core], place_ref[0, 1 - core])
     for i in range(2):
         for s in range(nb):
             rows = slice(s * BLOCK_TOKENS, (s + 1) * BLOCK_TOKENS)
@@ -231,6 +242,15 @@
     return bias.reshape(nb, -1)
 
 
+def mask_rounds(bits):
+    if bits < 3:
+        return [[1 << b] for b in range(1, bits)]
+    rounds = [[2, 4, 6]] + [[1 << b] for b in range(3, bits)]
+    if bits > 3:
+        rounds[-1] = [3 << (bits - 2)]
+    return rounds
+
+
 def body(queries, packed_key_value, incoming, loss_grad, global_blocks, random_blocks):
     toks = queries.shape[1]
     nb = toks // BLOCK_TOKENS
@@ -244,10 +264,10 @@
     twin = [(i, i ^ 1) for i in range(peers)]
     side = [(i, i + 1) for i in range(1, peers - 1, 2)]
     side = side + [(j, i) for i, j in side]
-    orders = (list(range(1, bits)), list(range(2, bits)) + [1])
-    hops = [
-        [(i, i ^ (1 << orders[i % 2][r])) for i in range(peers)] for r in range(bits - 1)
-    ]
+    rounds = mask_rounds(bits)
+
+    def flipped(mask):
+        return [(i, i ^ mask) for i in range(peers)]
 
     def exchange(x, pairs, axis="seq"):
         return lax.ppermute(x, axis, pairs)
@@ -260,16 +280,17 @@
     (held,) = call(
         pick_kernel, [SMEM, HBM, VMEM],
         [shape(BLOCK_TOKENS, own.shape[1], dtype=BF)],
-        (table, own, on), 10**6, [pltpu.SemaphoreType.DMA],
+        (table, pltpu.with_memory_space_constraint(own, pltpu.HBM), on), 10**6, [pltpu.SemaphoreType.DMA],
     )
     off = exchange(own, side)
     own, q, loss_grad = call(
         load_kernel, [HBM] * 3,
         [shape(*x.shape, dtype=BF) for x in (own, q, loss_grad)],
-        (own, q, loss_grad), 10**7, [pltpu.SemaphoreType.DMA((3,))],
-    )
-    for hop in hops:
-        held = held + exchange(held, hop)
+        [pltpu.with_memory_space_constraint(x, pltpu.HBM) for x in (own, q, loss_grad)], 10**7, [pltpu.SemaphoreType.DMA((3,))],
+    )
+    for masks in rounds:
+        got = [exchange(held, flipped(m)) for m in masks]
+        held = sum(got, held)
     other = exchange(held, twin)
 
     bias = list_bias(random_blocks[0], pos, peers, nb)
@@ -279,17 +300,24 @@
         [shape(KEY_HEADS, 3 * toks, rows), shape(KEY_HEADS, 8, rows)],
         (bias, q) + near, 3 * 10**9,
     )
-    dp, ds, stats, keep, give, d_out = call(
-        global_kernel, [VMEM] * 10,
+    dp, stats, d_out = call(
+        near_kernel, [VMEM] * 7,
         [
             shape(KEY_HEADS, 3 * toks, rows),
+            shape(KEY_HEADS, 8, rows),
+            shape(*q.shape, dtype=BF),
+        ],
+        (shifted, loss_grad) + near + (w, stats), 2 * 10**9,
+    )
+    ds, stats, keep, give = call(
+        global_kernel, [VMEM] * 5,
+        [
             shape(KEY_HEADS, GLOB_ROWS, rows, dtype=BF),
             shape(KEY_HEADS, 8, rows),
             shape(2, BLOCK_TOKENS, WIDTH),
             shape(2, BLOCK_TOKENS, WIDTH, dtype=BF),
-            shape(*q.shape, dtype=BF),
         ],
-        (q, shifted, loss_grad) + near + (held, other, w, stats), 3 * 10**9,
+        (q, d_out, held, other, stats), 2 * 10**9,
     )
     total = keep + exchange(give, twin).astype(F32)
     g_own, g_on, g_off, ds_local = call(
@@ -306,11 +334,15 @@
         queries_kernel, [VMEM] * 7, [shape(*q.shape, dtype=BF)],
         near + (held, other, ds_local, ds), 2 * 10**9,
     )
-    place = jnp.where(table[0] == pos, table[1], -1)
+    (place,) = call(
+        place_kernel, [VMEM], [shape(1, GLOBAL_BLOCKS, dtype=jnp.int32)], (table,), 1000
+    )
     r_on = exchange(g_on, twin)
     r_off = exchange(g_off, side)
-    for hop in hops:
-        total = total + exchange(total.astype(BF), hop).astype(F32)
+    for masks in rounds:
+        sent = total.astype(BF)
+        got = [exchange(sent, flipped(m)) for m in masks]
+        total = sum([x.astype(F32) for x in got], total)
     half = total.astype(BF)
     half_other = exchange(half, twin)
     (out,) = call(

time: 61.9 us -> 56.4 us (0.911)
  waiting for transfers between devices: 21.8 us -> 16.6 us
  local copies, waits for them, and re-layouts: 4.45 us -> 0.28 us
  starting transfers between devices: 23.1 us -> 25.2 us
  Pallas kernels: 10.2 us -> 11.6 us
    ppermute x14 -> x16, waiting for transfers between devices: 21.8 us -> 16.6 us  [exchange(): return lax.ppermute(x, axis, pairs)]
    unnamed x10 -> x2, local copies, waits for them, and re-layouts: 4.18 us -> 0.01 us
    ppermute x14 -> x16, starting transfers between devices: 23.1 us -> 25.2 us  [exchange(): return lax.ppermute(x, axis, pairs)]
    pallas_call x7 -> x9, Pallas kernels: 10.2 us -> 11.6 us  [call(): pl.pallas_call(kernel, in_specs=ins, out_specs=[VMEM] * len(outs), out_sh...]
  transfers between devices with their start and end apart: 14 -> 16, of which waited for: 6 -> 11; matrix products, arithmetic and copies ran while one was open for 2% -> 2% of each run, Pallas kernels for 10% -> 14%
where the time goes in v4:
time: 56.4 us; the launch traced here: 55.8 us
  starting transfers between devices  25.2 us (45%)
  waiting for transfers between devices  16.6 us (29%)
  Pallas kernels  11.6 us (21%)
  other arithmetic  1.23 us (2%)
  between operations  0.78 us (1%)
    ppermute x16, starting transfers between devices, exchange(): return lax.ppermute(x, axis, pairs)  25.2 us
    ppermute x16, waiting for transfers between devices, exchange(): return lax.ppermute(x, axis, pairs)  16.6 us
    pallas_call x9, Pallas kernels, call(): pl.pallas_call(kernel, in_specs=ins, out_specs=[VMEM] * len(outs), out_sh...  11.6 us
  transfers between devices with their start and end apart: 16, of which 11 were waited for; matrix products, arithmetic and copies ran while one was open for 2% of the time, Pallas kernels for 14%

profile of v4, /device:TPU:11, one launch (start us, length us, event | category | flops | bytes accessed | tf_op | source)
XLA Modules:
  0.0 55.8 jit_solution(17071972867817515802)
XLA Ops:
  0.6 0.7 %collective-permute-start = (bf16[128,1024]{1,0:T(8,128)(2,1)}, bf16[128,1024]{1,0:T(8,128)(2,1)S(1)}, u32[]{:S(2)}, u32[]{:S(2)}) collective-permute-start(bf16[128,1024]{1,0:T(8,128)(2,1)} %bitcast.7), channel_id=1, source_target_pairs={{0,1},{1,0},{2,3},{3,2},{4,5},{5,4},{6,7},{7,6},{8,9},{9,8},{10,11... | collective-permute-start | bytes 786440 | tf_op jit(solution)/shard_map/ppermute | solution.py:273
  1.4 3.1 %collective-permute-start.1 = (bf16[128,1024]{1,0:T(8,128)(2,1)}, bf16[128,1024]{1,0:T(8,128)(2,1)S(1)}, u32[]{:S(2)}, u32[]{:S(2)}) collective-permute-start(bf16[128,1024]{1,0:T(8,128)(2,1)} %bitcast.8), channel_id=1, source_target_pairs={{1,2},{3,4},{5,6},{7,8},{9,10},{11,12},{13,14},{2,1},{4,3},{6,5},{... | collective-permute-start | bytes 786440 | tf_op jit(solution)/shard_map/ppermute | solution.py:273
  4.4 2.2 %collective-permute-start.7 = (bf16[128,3072]{1,0:T(8,128)(2,1)}, bf16[128,3072]{1,0:T(8,128)(2,1)S(1)}, u32[]{:S(2)}, u32[]{:S(2)}) collective-permute-start(bf16[128,3072]{1,0:T(8,128)(2,1)} %bitcast.13), channel_id=1, source_target_pairs={{16,0},{17,1},{18,2},{19,3},{20,4},{21,5},{22,6},{23,7},{24,8},{25... | collective-permute-start | bytes 2359304 | tf_op jit(solution)/shard_map/ppermute | solution.py:273
  6.7 0.7 %and_select_fusion.1 = (s32[1,2]{1,0:T(1,128)S(1)}, s32[1,2]{1,0:T(1,128)S(1)}) fusion(s32[1,2]{1,0:T(1,128)} %param.10), kind=kLoop, calls=%fused_computation.11 | loop fusion | flops 38 | bytes 24 | tf_op jit(solution)/shard_map/jit(floor_divide)/jit(_where)/select_n | solution.py:279
  7.8 0.6 %shard_map.78 = bf16[64,1024]{1,0:T(8,128)(2,1)S(1)} custom-call(s32[2,2]{1,0:T(2,128)S(1)} %pad_add_fusion.table_ref, bf16[128,1024]{1,0:T(8,128)(2,1)} %bitcast.9, bf16[128,1024]{1,0:T(8,128)(2,1)S(1)} %collective-permute-done.on_ref), custom_call_target="tpu_custom_call" | custom-call | flops 1000000 | bytes 2000 | tf_op jit(solution)/shard_map/pallas_call | solution.py:37
  8.4 1.3 %collective-permute-start.2 = (bf16[64,1024]{1,0:T(8,128)(2,1)S(1)}, bf16[64,1024]{1,0:T(8,128)(2,1)S(1)}, u32[]{:S(2)}, u32[]{:S(2)}) collective-permute-start(bf16[64,1024]{1,0:T(8,128)(2,1)S(1)} %shard_map.78), channel_id=1, source_target_pairs={{0,2},{1,3},{2,0},{3,1},{4,6},{5,7},{6,4},{7,5},{8,10},{9,11},{10,... | collective-permute-start | bytes 393224 | tf_op jit(solution)/shard_map/ppermute | solution.py:273
  9.9 1.2 %collective-permute-start.4 = (bf16[64,1024]{1,0:T(8,128)(2,1)S(1)}, bf16[64,1024]{1,0:T(8,128)(2,1)S(1)}, u32[]{:S(2)}, u32[]{:S(2)}) collective-permute-start(bf16[64,1024]{1,0:T(8,128)(2,1)S(1)} %shard_map.78), channel_id=1, source_target_pairs={{0,6},{1,7},{2,4},{3,5},{4,2},{5,3},{6,0},{7,1},{8,14},{9,15},{10,... | collective-permute-start | bytes 393224 | tf_op jit(solution)/shard_map/ppermute | solution.py:273
  11.2 1.5 %shard_map.77 = (bf16[128,1024]{1,0:T(8,128)(2,1)S(1)}, bf16[128,3072]{1,0:T(8,128)(2,1)S(1)}, bf16[128,3072]{1,0:T(8,128)(2,1)S(1)}) custom-call(bf16[128,1024]{1,0:T(8,128)(2,1)} %bitcast.10, bf16[128,3072]{1,0:T(8,128)(2,1)} %bitcast.11, bf16[128,3072]{1,0:T(8,128)(2,1)} %c_ref.1), custom_call_target="tpu_custom_call" | custom-call | flops 10000000 | bytes 20000 | tf_op jit(solution)/shard_map/pallas_call | solution.py:37
  12.7 1.5 %collective-permute-done.2 = bf16[64,1024]{1,0:T(8,128)(2,1)S(1)} collective-permute-done((bf16[64,1024]{1,0:T(8,128)(2,1)S(1)}, bf16[64,1024]{1,0:T(8,128)(2,1)S(1)}, u32[]{:S(2)}, u32[]{:S(2)}) %collective-permute-start.2) | collective-permute-done | bytes 131104 | tf_op jit(solution)/shard_map/ppermute | solution.py:273
  14.2 0.6 collective-permute-done.3
  14.7 1.9 %collective-permute-done.4 = bf16[64,1024]{1,0:T(8,128)(2,1)S(1)} collective-permute-done((bf16[64,1024]{1,0:T(8,128)(2,1)S(1)}, bf16[64,1024]{1,0:T(8,128)(2,1)S(1)}, u32[]{:S(2)}, u32[]{:S(2)}) %collective-permute-start.4) | collective-permute-done | bytes 131104 | tf_op jit(solution)/shard_map/ppermute | solution.py:273
  16.6 1.4 %collective-permute-start.5 = (bf16[64,1024]{1,0:T(8,128)(2,1)S(1)}, bf16[64,1024]{1,0:T(8,128)(2,1)S(1)}, u32[]{:S(2)}, u32[]{:S(2)}) collective-permute-start(bf16[64,1024]{1,0:T(8,128)(2,1)S(1)} %add_add_fusion), channel_id=1, source_target_pairs={{0,12},{1,13},{2,14},{3,15},{4,8},{5,9},{6,10},{7,11},{8,4},{9,5},... | collective-permute-start | bytes 393224 | tf_op jit(solution)/shard_map/ppermute | solution.py:273
  18.0 2.1 %shard_map.79 = (f32[4,384,768]{2,1,0:T(8,128)S(1)}, f32[4,8,768]{2,1,0:T(8,128)S(1)}) custom-call(f32[2,24]{1,0:T(2,128)S(1)} %reshape.96.bias_ref, bf16[128,3072]{1,0:T(8,128)(2,1)S(1)} %get-tuple-element.19.q_ref, bf16[128,1024]{1,0:T(8,128)(2,1)S(1)} %get-tuple-element.18.own_ref, bf16[128,1024]{1,0:T(8,128)(2,1)S(1)} %collective-permute-done.on_ref, ...), custom_call_target="tpu_custom_call" | custom-call | flops 3000000000 | bytes 6000000 | tf_op jit(solution)/shard_map/pallas_call | solution.py:37
  20.1 0.4 collective-permute-done.5
  20.6 5.2 %collective-permute-start.6 = (bf16[64,1024]{1,0:T(8,128)(2,1)S(1)}, bf16[64,1024]{1,0:T(8,128)(2,1)S(1)}, u32[]{:S(2)}, u32[]{:S(2)}) collective-permute-start(bf16[64,1024]{1,0:T(8,128)(2,1)S(1)} %add.95.held_ref), channel_id=1, source_target_pairs={{0,1},{1,0},{2,3},{3,2},{4,5},{5,4},{6,7},{7,6},{8,9},{9,8},{10,11... | collective-permute-start | bytes 393224 | tf_op jit(solution)/shard_map/ppermute | solution.py:273
  25.8 0.9 %shard_map.80 = (f32[4,384,768]{2,1,0:T(8,128)S(1)}, f32[4,8,768]{2,1,0:T(8,128)S(1)}, bf16[128,3072]{1,0:T(8,128)(2,1)S(1)}) custom-call(bf16[128,3072]{1,0:T(8,128)(2,1)S(1)} %collective-permute-done.7.shifted_ref, bf16[128,3072]{1,0:T(8,128)(2,1)S(1)} %get-tuple-element.20.loss_ref, bf16[128,1024]{1,0:T(8,128)(2,1)S(1)} %get-tuple-element.18.own_ref, ...), custom_call_target="tpu_custom_call" | custom-call | flops 2000000000 | bytes 4000000 | tf_op jit(solution)/shard_map/pallas_call | solution.py:37
  26.7 2.1 %shard_map.81 = (bf16[4,128,768]{2,1,0:T(8,128)(2,1)S(1)}, f32[4,8,768]{2,1,0:T(8,128)S(1)}, f32[2,64,512]{2,1,0:T(8,128)S(1)}, bf16[2,64,512]{2,1,0:T(8,128)(2,1)S(1)}) custom-call(bf16[128,3072]{1,0:T(8,128)(2,1)S(1)} %get-tuple-element.19.q_ref, bf16[128,3072]{1,0:T(8,128)(2,1)S(1)} %get-tuple-element.23.do_ref, bf16[64,1024]{1,0:T(8,128)(2,1)S(1)} %add.95.held_ref, ...), custom_call_target="tpu_custom_call" | custom-call | flops 2000000000 | bytes 4000000 | tf_op jit(solution)/shard_map/pallas_call | solution.py:37
  29.3 1.0 %collective-permute-done.10 = bf16[2,64,512]{2,1,0:T(8,128)(2,1)S(1)} collective-permute-done((bf16[2,64,512]{2,1,0:T(8,128)(2,1)S(1)}, bf16[2,64,512]{2,1,0:T(8,128)(2,1)S(1)}, u32[]{:S(2)}, u32[]{:S(2)}) %collective-permute-start.10) | collective-permute-done | bytes 131104 | tf_op jit(solution)/shard_map/ppermute | solution.py:273
  30.3 2.0 %collective-permute-start.11 = (bf16[2,64,512]{2,1,0:T(8,128)(2,1)S(1)}, bf16[2,64,512]{2,1,0:T(8,128)(2,1)S(1)}, u32[]{:S(2)}, u32[]{:S(2)}) collective-permute-start(bf16[2,64,512]{2,1,0:T(8,128)(2,1)S(1)} %fusion), channel_id=1, source_target_pairs={{0,2},{1,3},{2,0},{3,1},{4,6},{5,7},{6,4},{7,5},{8,10},{9,11},{10,... | collective-permute-start | bytes 393224 | tf_op jit(solution)/shard_map/ppermute | solution.py:273
  32.3 1.3 %collective-permute-start.13 = (bf16[2,64,512]{2,1,0:T(8,128)(2,1)S(1)}, bf16[2,64,512]{2,1,0:T(8,128)(2,1)S(1)}, u32[]{:S(2)}, u32[]{:S(2)}) collective-permute-start(bf16[2,64,512]{2,1,0:T(8,128)(2,1)S(1)} %fusion), channel_id=1, source_target_pairs={{0,6},{1,7},{2,4},{3,5},{4,2},{5,3},{6,0},{7,1},{8,14},{9,15},{10,... | collective-permute-start | bytes 393224 | tf_op jit(solution)/shard_map/ppermute | solution.py:273
  33.6 2.2 %collective-permute-done.11 = bf16[2,64,512]{2,1,0:T(8,128)(2,1)S(1)} collective-permute-done((bf16[2,64,512]{2,1,0:T(8,128)(2,1)S(1)}, bf16[2,64,512]{2,1,0:T(8,128)(2,1)S(1)}, u32[]{:S(2)}, u32[]{:S(2)}) %collective-permute-start.11) | collective-permute-done | bytes 131104 | tf_op jit(solution)/shard_map/ppermute | solution.py:273
  35.8 0.9 %collective-permute-done.12 = bf16[2,64,512]{2,1,0:T(8,128)(2,1)S(1)} collective-permute-done((bf16[2,64,512]{2,1,0:T(8,128)(2,1)S(1)}, bf16[2,64,512]{2,1,0:T(8,128)(2,1)S(1)}, u32[]{:S(2)}, u32[]{:S(2)}) %collective-permute-start.12) | collective-permute-done | bytes 131104 | tf_op jit(solution)/shard_map/ppermute | solution.py:273
  36.7 2.9 %collective-permute-done.13 = bf16[2,64,512]{2,1,0:T(8,128)(2,1)S(1)} collective-permute-done((bf16[2,64,512]{2,1,0:T(8,128)(2,1)S(1)}, bf16[2,64,512]{2,1,0:T(8,128)(2,1)S(1)}, u32[]{:S(2)}, u32[]{:S(2)}) %collective-permute-start.13) | collective-permute-done | bytes 131104 | tf_op jit(solution)/shard_map/ppermute | solution.py:273
  39.7 0.8 %collective-permute-start.14 = (bf16[2,64,512]{2,1,0:T(8,128)(2,1)S(1)}, bf16[2,64,512]{2,1,0:T(8,128)(2,1)S(1)}, u32[]{:S(2)}, u32[]{:S(2)}) collective-permute-start(bf16[2,64,512]{2,1,0:T(8,128)(2,1)S(1)} %fusion.1), channel_id=1, source_target_pairs={{0,12},{1,13},{2,14},{3,15},{4,8},{5,9},{6,10},{7,11},{8,4},{9,5},... | collective-permute-start | bytes 393224 | tf_op jit(solution)/shard_map/ppermute | solution.py:273
  40.5 1.5 %shard_map.82 = (f32[2,128,512]{2,1,0:T(8,128)S(1)}, bf16[2,128,512]{2,1,0:T(8,128)(2,1)S(1)}, bf16[2,128,512]{2,1,0:T(8,128)(2,1)S(1)}, bf16[4,384,768]{2,1,0:T(8,128)(2,1)S(1)}) custom-call(bf16[128,3072]{1,0:T(8,128)(2,1)S(1)} %get-tuple-element.19.q_ref, bf16[128,3072]{1,0:T(8,128)(2,1)S(1)} %get-tuple-element.23.do_ref, ...), custom_call_target="tpu_custom_call" | custom-call | flops 3000000000 | bytes 6000000 | tf_op jit(solution)/shard_map/pallas_call | solution.py:37
  42.0 1.8 %collective-permute-start.8 = (bf16[2,128,512]{2,1,0:T(8,128)(2,1)S(1)}, bf16[2,128,512]{2,1,0:T(8,128)(2,1)S(1)}, u32[]{:S(2)}, u32[]{:S(2)}) collective-permute-start(bf16[2,128,512]{2,1,0:T(8,128)(2,1)S(1)} %get-tuple-element.30), channel_id=1, source_target_pairs={{0,1},{1,0},{2,3},{3,2},{4,5},{5,4},{6,7},{7,6},{8,9},{9,8},{10,11... | collective-permute-start | bytes 786440 | tf_op jit(solution)/shard_map/ppermute | solution.py:273
  43.9 2.7 %collective-permute-start.9 = (bf16[2,128,512]{2,1,0:T(8,128)(2,1)S(1)}, bf16[2,128,512]{2,1,0:T(8,128)(2,1)S(1)}, u32[]{:S(2)}, u32[]{:S(2)}) collective-permute-start(bf16[2,128,512]{2,1,0:T(8,128)(2,1)S(1)} %get-tuple-element.31), channel_id=1, source_target_pairs={{1,2},{3,4},{5,6},{7,8},{9,10},{11,12},{13,14},{2,1},{4,3},{6,5},{... | collective-permute-start | bytes 786440 | tf_op jit(solution)/shard_map/ppermute | solution.py:273
  46.6 1.1 %collective-permute-done.14 = bf16[2,64,512]{2,1,0:T(8,128)(2,1)S(1)} collective-permute-done((bf16[2,64,512]{2,1,0:T(8,128)(2,1)S(1)}, bf16[2,64,512]{2,1,0:T(8,128)(2,1)S(1)}, u32[]{:S(2)}, u32[]{:S(2)}) %collective-permute-start.14) | collective-permute-done | bytes 131104 | tf_op jit(solution)/shard_map/ppermute | solution.py:273
  47.8 0.9 %collective-permute-start.15 = (bf16[2,64,512]{2,1,0:T(8,128)(2,1)S(1)}, bf16[2,64,512]{2,1,0:T(8,128)(2,1)S(1)}, u32[]{:S(2)}, u32[]{:S(2)}) collective-permute-start(bf16[2,64,512]{2,1,0:T(8,128)(2,1)S(1)} %add_convert_fusion.half_ref), channel_id=1, source_target_pairs={{0,1},{1,0},{2,3},{3,2},{4,5},{5,4},{6,7},{7,6},{8,9},{9,8},{10,11... | collective-permute-start | bytes 393224 | tf_op jit(solution)/shard_map/ppermute | solution.py:273
  48.6 1.6 %shard_map.83 = bf16[128,3072]{1,0:T(8,128)(2,1)} custom-call(bf16[128,1024]{1,0:T(8,128)(2,1)S(1)} %get-tuple-element.18.own_ref, bf16[128,1024]{1,0:T(8,128)(2,1)S(1)} %collective-permute-done.on_ref, bf16[128,1024]{1,0:T(8,128)(2,1)S(1)} %collective-permute-done.1.off_ref, bf16[64,1024]{1,0:T(8,128)(2,1)S(1)} %add.95.held_ref, ...), custom_call_target="tpu_custom_call" | custom-call | flops 2000000000 | bytes 4000000 | tf_op jit(solution)/shard_map/pallas_call | solution.py:37
  50.2 4.1 %collective-permute-done.9.r_off = bf16[2,128,512]{2,1,0:T(8,128)(2,1)S(1)} collective-permute-done((bf16[2,128,512]{2,1,0:T(8,128)(2,1)S(1)}, bf16[2,128,512]{2,1,0:T(8,128)(2,1)S(1)}, u32[]{:S(2)}, u32[]{:S(2)}) %collective-permute-start.9) | collective-permute-done | bytes 262176 | tf_op jit(solution)/shard_map/ppermute | solution.py:273
  54.3 1.4 %shard_map.85 = bf16[128,1024]{1,0:T(8,128)(2,1)} custom-call(s32[1,2]{1,0:T(1,128)S(1)} %shard_map.84.place_ref, f32[2,128,512]{2,1,0:T(8,128)S(1)} %get-tuple-element.29.g_own, bf16[2,128,512]{2,1,0:T(8,128)(2,1)S(1)} %collective-permute-done.8.r_on, bf16[2,128,512]{2,1,0:T(8,128)(2,1)S(1)} %collective-permute-done.9.r_off, ...), custom_call_target="tpu_custom_call" | custom-call | flops 1000000 | bytes 2000 | tf_op jit(solution)/shard_map/pallas_call | solution.py:37
  (27 shorter events, 1.6 us)
Async XLA Ops:
  0.6 6.9 %copy-start = (s32[1,32,4,3]{1,2,3,0:T(4,128)S(1)}, s32[1,32,4,3]{1,2,3,0:T(4,128)}, u32[]{:S(2)}) copy-start(s32[1,32,4,3]{1,2,3,0:T(4,128)} %param.11) | copy-start | bytes 4612
  0.6 7.2 %collective-permute-start = (bf16[128,1024]{1,0:T(8,128)(2,1)}, bf16[128,1024]{1,0:T(8,128)(2,1)S(1)}, u32[]{:S(2)}, u32[]{:S(2)}) collective-permute-start(bf16[128,1024]{1,0:T(8,128)(2,1)} %bitcast.7), channel_id=1, source_target_pairs={{0,1},{1,0},{2,3},{3,2},{4,5},{5,4},{6,7},{7,6},{8,9},{9,8},{10,11... | collective-permute-start | bytes 786440 | tf_op jit(solution)/shard_map/ppermute | solution.py:273
  1.4 16.6 %collective-permute-start.1 = (bf16[128,1024]{1,0:T(8,128)(2,1)}, bf16[128,1024]{1,0:T(8,128)(2,1)S(1)}, u32[]{:S(2)}, u32[]{:S(2)}) collective-permute-start(bf16[128,1024]{1,0:T(8,128)(2,1)} %bitcast.8), channel_id=1, source_target_pairs={{1,2},{3,4},{5,6},{7,8},{9,10},{11,12},{13,14},{2,1},{4,3},{6,5},{... | collective-permute-start | bytes 786440 | tf_op jit(solution)/shard_map/ppermute | solution.py:273
  4.4 21.3 %collective-permute-start.7 = (bf16[128,3072]{1,0:T(8,128)(2,1)}, bf16[128,3072]{1,0:T(8,128)(2,1)S(1)}, u32[]{:S(2)}, u32[]{:S(2)}) collective-permute-start(bf16[128,3072]{1,0:T(8,128)(2,1)} %bitcast.13), channel_id=1, source_target_pairs={{16,0},{17,1},{18,2},{19,3},{20,4},{21,5},{22,6},{23,7},{24,8},{25... | collective-permute-start | bytes 2359304 | tf_op jit(solution)/shard_map/ppermute | solution.py:273
  8.4 5.8 %collective-permute-start.2 = (bf16[64,1024]{1,0:T(8,128)(2,1)S(1)}, bf16[64,1024]{1,0:T(8,128)(2,1)S(1)}, u32[]{:S(2)}, u32[]{:S(2)}) collective-permute-start(bf16[64,1024]{1,0:T(8,128)(2,1)S(1)} %shard_map.78), channel_id=1, source_target_pairs={{0,2},{1,3},{2,0},{3,1},{4,6},{5,7},{6,4},{7,5},{8,10},{9,11},{10,... | collective-permute-start | bytes 393224 | tf_op jit(solution)/shard_map/ppermute | solution.py:273
  9.7 5.0 %collective-permute-start.3 = (bf16[64,1024]{1,0:T(8,128)(2,1)S(1)}, bf16[64,1024]{1,0:T(8,128)(2,1)S(1)}, u32[]{:S(2)}, u32[]{:S(2)}) collective-permute-start(bf16[64,1024]{1,0:T(8,128)(2,1)S(1)} %shard_map.78), channel_id=1, source_target_pairs={{0,4},{1,5},{2,6},{3,7},{4,0},{5,1},{6,2},{7,3},{8,12},{9,13},{10,... | collective-permute-start | bytes 393224 | tf_op jit(solution)/shard_map/ppermute | solution.py:273
  9.9 6.7 %collective-permute-start.4 = (bf16[64,1024]{1,0:T(8,128)(2,1)S(1)}, bf16[64,1024]{1,0:T(8,128)(2,1)S(1)}, u32[]{:S(2)}, u32[]{:S(2)}) collective-permute-start(bf16[64,1024]{1,0:T(8,128)(2,1)S(1)} %shard_map.78), channel_id=1, source_target_pairs={{0,6},{1,7},{2,4},{3,5},{4,2},{5,3},{6,0},{7,1},{8,14},{9,15},{10,... | collective-permute-start | bytes 393224 | tf_op jit(solution)/shard_map/ppermute | solution.py:273
  16.6 3.9 %collective-permute-start.5 = (bf16[64,1024]{1,0:T(8,128)(2,1)S(1)}, bf16[64,1024]{1,0:T(8,128)(2,1)S(1)}, u32[]{:S(2)}, u32[]{:S(2)}) collective-permute-start(bf16[64,1024]{1,0:T(8,128)(2,1)S(1)} %add_add_fusion), channel_id=1, source_target_pairs={{0,12},{1,13},{2,14},{3,15},{4,8},{5,9},{6,10},{7,11},{8,4},{9,5},... | collective-permute-start | bytes 393224 | tf_op jit(solution)/shard_map/ppermute | solution.py:273
  20.6 6.2 %collective-permute-start.6 = (bf16[64,1024]{1,0:T(8,128)(2,1)S(1)}, bf16[64,1024]{1,0:T(8,128)(2,1)S(1)}, u32[]{:S(2)}, u32[]{:S(2)}) collective-permute-start(bf16[64,1024]{1,0:T(8,128)(2,1)S(1)} %add.95.held_ref), channel_id=1, source_target_pairs={{0,1},{1,0},{2,3},{3,2},{4,5},{5,4},{6,7},{7,6},{8,9},{9,8},{10,11... | collective-permute-start | bytes 393224 | tf_op jit(solution)/shard_map/ppermute | solution.py:273
  28.9 1.4 %collective-permute-start.10 = (bf16[2,64,512]{2,1,0:T(8,128)(2,1)S(1)}, bf16[2,64,512]{2,1,0:T(8,128)(2,1)S(1)}, u32[]{:S(2)}, u32[]{:S(2)}) collective-permute-start(bf16[2,64,512]{2,1,0:T(8,128)(2,1)S(1)} %get-tuple-element.33), channel_id=1, source_target_pairs={{0,1},{1,0},{2,3},{3,2},{4,5},{5,4},{6,7},{7,6},{8,9},{9,8},{10,11... | collective-permute-start | bytes 393224 | tf_op jit(solution)/shard_map/ppermute | solution.py:273
  30.3 5.5 %collective-permute-start.11 = (bf16[2,64,512]{2,1,0:T(8,128)(2,1)S(1)}, bf16[2,64,512]{2,1,0:T(8,128)(2,1)S(1)}, u32[]{:S(2)}, u32[]{:S(2)}) collective-permute-start(bf16[2,64,512]{2,1,0:T(8,128)(2,1)S(1)} %fusion), channel_id=1, source_target_pairs={{0,2},{1,3},{2,0},{3,1},{4,6},{5,7},{6,4},{7,5},{8,10},{9,11},{10,... | collective-permute-start | bytes 393224 | tf_op jit(solution)/shard_map/ppermute | solution.py:273
  32.3 4.4 %collective-permute-start.12 = (bf16[2,64,512]{2,1,0:T(8,128)(2,1)S(1)}, bf16[2,64,512]{2,1,0:T(8,128)(2,1)S(1)}, u32[]{:S(2)}, u32[]{:S(2)}) collective-permute-start(bf16[2,64,512]{2,1,0:T(8,128)(2,1)S(1)} %fusion), channel_id=1, source_target_pairs={{0,4},{1,5},{2,6},{3,7},{4,0},{5,1},{6,2},{7,3},{8,12},{9,13},{10,... | collective-permute-start | bytes 393224 | tf_op jit(solution)/shard_map/ppermute | solution.py:273
  32.3 7.3 %collective-permute-start.13 = (bf16[2,64,512]{2,1,0:T(8,128)(2,1)S(1)}, bf16[2,64,512]{2,1,0:T(8,128)(2,1)S(1)}, u32[]{:S(2)}, u32[]{:S(2)}) collective-permute-start(bf16[2,64,512]{2,1,0:T(8,128)(2,1)S(1)} %fusion), channel_id=1, source_target_pairs={{0,6},{1,7},{2,4},{3,5},{4,2},{5,3},{6,0},{7,1},{8,14},{9,15},{10,... | collective-permute-start | bytes 393224 | tf_op jit(solution)/shard_map/ppermute | solution.py:273
  39.7 8.0 %collective-permute-start.14 = (bf16[2,64,512]{2,1,0:T(8,128)(2,1)S(1)}, bf16[2,64,512]{2,1,0:T(8,128)(2,1)S(1)}, u32[]{:S(2)}, u32[]{:S(2)}) collective-permute-start(bf16[2,64,512]{2,1,0:T(8,128)(2,1)S(1)} %fusion.1), channel_id=1, source_target_pairs={{0,12},{1,13},{2,14},{3,15},{4,8},{5,9},{6,10},{7,11},{8,4},{9,5},... | collective-permute-start | bytes 393224 | tf_op jit(solution)/shard_map/ppermute | solution.py:273
  42.0 8.2 %collective-permute-start.8 = (bf16[2,128,512]{2,1,0:T(8,128)(2,1)S(1)}, bf16[2,128,512]{2,1,0:T(8,128)(2,1)S(1)}, u32[]{:S(2)}, u32[]{:S(2)}) collective-permute-start(bf16[2,128,512]{2,1,0:T(8,128)(2,1)S(1)} %get-tuple-element.30), channel_id=1, source_target_pairs={{0,1},{1,0},{2,3},{3,2},{4,5},{5,4},{6,7},{7,6},{8,9},{9,8},{10,11... | collective-permute-start | bytes 786440 | tf_op jit(solution)/shard_map/ppermute | solution.py:273
  43.9 10.5 %collective-permute-start.9 = (bf16[2,128,512]{2,1,0:T(8,128)(2,1)S(1)}, bf16[2,128,512]{2,1,0:T(8,128)(2,1)S(1)}, u32[]{:S(2)}, u32[]{:S(2)}) collective-permute-start(bf16[2,128,512]{2,1,0:T(8,128)(2,1)S(1)} %get-tuple-element.31), channel_id=1, source_target_pairs={{1,2},{3,4},{5,6},{7,8},{9,10},{11,12},{13,14},{2,1},{4,3},{6,5},{... | collective-permute-start | bytes 786440 | tf_op jit(solution)/shard_map/ppermute | solution.py:273
  47.8 6.6 %collective-permute-start.15 = (bf16[2,64,512]{2,1,0:T(8,128)(2,1)S(1)}, bf16[2,64,512]{2,1,0:T(8,128)(2,1)S(1)}, u32[]{:S(2)}, u32[]{:S(2)}) collective-permute-start(bf16[2,64,512]{2,1,0:T(8,128)(2,1)S(1)} %add_convert_fusion.half_ref), channel_id=1, source_target_pairs={{0,1},{1,0},{2,3},{3,2},{4,5},{5,4},{6,7},{7,6},{8,9},{9,8},{10,11... | collective-permute-start | bytes 393224 | tf_op jit(solution)/shard_map/ppermute | solution.py:273

commit v5 on v4

--- a/solution.py
+++ b/solution.py
@@ -1,3 +1,4 @@
+import functools
 import math
 
 import jax
@@ -33,11 +34,12 @@
     return lax.dot_general(a, b, dims, preferred_element_type=F32)
 
 
-def call(kernel, ins, outs, args, flops, scratch=()):
+def call(kernel, ins, outs, args, flops, scratch=(), out_specs=None, aliases={}):
     return pl.pallas_call(
         kernel,
         in_specs=ins,
-        out_specs=[VMEM] * len(outs),
+        out_specs=out_specs or [VMEM] * len(outs),
+        input_output_aliases=aliases,
         out_shape=outs,
         scratch_shapes=scratch,
         compiler_params=pltpu.CompilerParams(vmem_limit_bytes=24 << 20),
@@ -67,10 +69,10 @@
     return lax.axis_index("section") == lax.axis_size("section") - 1
 
 
-def load_kernel(a_ref, b_ref, c_ref, a_out, b_out, c_out, sems):
+def load_kernel(a_ref, b_ref, a_out, b_out, sems):
     copies = [
         pltpu.make_async_copy(src, dst, sems.at[i])
-        for i, (src, dst) in enumerate(((a_ref, a_out), (b_ref, b_out), (c_ref, c_out)))
+        for i, (src, dst) in enumerate(((a_ref, a_out), (b_ref, b_out)))
     ]
     for copy in copies:
         copy.start()
@@ -78,27 +80,28 @@
         copy.wait()
 
 
-def pick_kernel(table_ref, own_ref, on_ref, out_ref, sem):
+def pick_kernel(ids_ref, own_ref, keep_ref, give_ref, own_out, ids, sems):
+    nb = own_ref.shape[0] // BLOCK_TOKENS
     pos = lax.axis_index("seq")
     core = lax.rem(pos, 2)
-    owner = table_ref[0, core]
-    row = pl.multiple_of(table_ref[1, core] * BLOCK_TOKENS, BLOCK_TOKENS)
-    mine = owner == pos
-    theirs = owner == pos + 1 - 2 * core
-
-    @pl.when(mine)
-    def _():
-        copy = pltpu.make_async_copy(own_ref.at[pl.ds(row, BLOCK_TOKENS)], out_ref, sem)
-        copy.start()
-        copy.wait()
-
-    @pl.when(theirs)
-    def _():
-        out_ref[...] = on_ref[pl.ds(row, BLOCK_TOKENS), :]
-
-    @pl.when(jnp.logical_not(mine | theirs))
-    def _():
-        out_ref[...] = jnp.zeros_like(out_ref)
+    fetch_ids = pltpu.make_async_copy(ids_ref, ids, sems.at[0])
+    fetch_own = pltpu.make_async_copy(own_ref, own_out, sems.at[1])
+    fetch_ids.start()
+    fetch_own.start()
+    fetch_ids.wait()
+    fetch_own.wait()
+    for which, out in ((core, keep_ref), (1 - core, give_ref)):
+        block = ids[0, which]
+        mine = lax.div(block, nb) == pos
+        row = pl.multiple_of(lax.rem(block, nb) * BLOCK_TOKENS, BLOCK_TOKENS)
+
+        @pl.when(mine)
+        def _(out=out, row=row):
+            out[...] = own_out[pl.ds(row, BLOCK_TOKENS), :]
+
+        @pl.when(jnp.logical_not(mine))
+        def _(out=out):
+            out[...] = jnp.zeros_like(out)
 
 
 def local_kernel(bias_ref, q_ref, own_ref, on_ref, off_ref, w_ref, stat_ref):
@@ -149,12 +152,14 @@
 def global_kernel(
     q_ref, do_ref, held_ref, other_ref, stat_ref, ds_ref, out_stat_ref, keep_ref, give_ref
 ):
-    for g in range(KEY_HEADS):
+    def scores(g):
         kc = g * HEAD_SIZE
         qg = group_rows(q_ref, g)
         dog = group_rows(do_ref, g)
         t = dot(stacked((held_ref, other_ref), kc), qg, NT) * (SCALE * LOG2E)
-        dp = dot(stacked((held_ref, other_ref), WIDTH + kc), dog, NT)
+        return qg, dog, t, dot(stacked((held_ref, other_ref), WIDTH + kc), dog, NT)
+
+    def weights(g, t, dp):
         m_local = stat_ref[g, 0:1, :]
         m = jnp.maximum(m_local, jnp.max(t, axis=0, keepdims=True))
         shrink = jnp.exp2(m_local - m)
@@ -168,10 +173,21 @@
         ds_ref[g] = ds
         out_stat_ref[g, 0:1, :] = local_factor
         out_stat_ref[g, 1:2, :] = delta
-        cols = slice(kc, kc + HEAD_SIZE)
-        for i, grad in enumerate((dot(ds, qg, NN), dot(p.astype(BF), dog, NN))):
+        return ds, p.astype(BF)
+
+    def sums(g, ds, p, qg, dog):
+        cols = slice(g * HEAD_SIZE, (g + 1) * HEAD_SIZE)
+        for i, grad in enumerate((dot(ds, qg, NN), dot(p, dog, NN))):
             keep_ref[i, :, cols] = grad[:BLOCK_TOKENS]
             give_ref[i, :, cols] = grad[BLOCK_TOKENS:].astype(BF)
+
+    first = scores(0)
+    for g in range(KEY_HEADS):
+        qg, dog, t, dp = first
+        if g + 1 < KEY_HEADS:
+            first = scores(g + 1)
+        ds, p = weights(g, t, dp)
+        sums(g, ds, p, qg, dog)
 
 
 def local_ds(w_ref, dp_ref, stat_ref, g):
@@ -208,23 +224,40 @@
                 )
 
 
-def place_kernel(table_ref, out_ref):
-    here = table_ref[0:1, :] == lax.axis_index("seq")
-    out_ref[...] = jnp.where(here, table_ref[1:2, :], -1)
-
-
-def finish_kernel(place_ref, g_own, r_on, r_off, half_ref, half_other_ref, out_ref):
+def place_kernel(nb, ids_ref, out_ref):
+    slot = ids_ref[...] - lax.axis_index("seq") * nb
+    out_ref[...] = jnp.where((slot >= 0) & (slot < nb), slot, -1)
+
+
+def merge_kernel(place_ref, g_own, r_on, r_off, half_ref, base_ref, out_ref, rows_ref, sems):
     toks = g_own.shape[1]
-    nb = toks // BLOCK_TOKENS
-    core = lax.rem(lax.axis_index("seq"), 2)
-    places = (place_ref[0, core], place_ref[0, 1 - core])
-    for i in range(2):
-        for s in range(nb):
-            rows = slice(s * BLOCK_TOKENS, (s + 1) * BLOCK_TOKENS)
+    place = place_ref[0, lax.rem(lax.axis_index("seq"), 2)]
+    copies = []
+    for s in range(toks // BLOCK_TOKENS):
+        rows = slice(s * BLOCK_TOKENS, (s + 1) * BLOCK_TOKENS)
+        for i in range(2):
             total = g_own[i, rows] + r_on[i, rows].astype(F32) + r_off[i, rows].astype(F32)
-            for place, ref in zip(places, (half_ref, half_other_ref)):
-                total = total + jnp.where(place == s, ref[i].astype(F32), 0.0)
-            out_ref[rows, i * WIDTH : (i + 1) * WIDTH] = total.astype(BF)
+            total = total + jnp.where(place == s, half_ref[i].astype(F32), 0.0)
+            base_ref[i, rows] = total
+            rows_ref[rows, i * WIDTH : (i + 1) * WIDTH] = total.astype(BF)
+        copies.append(pltpu.make_async_copy(rows_ref.at[rows], out_ref.at[rows], sems.at[s]))
+        copies[-1].start()
+    for copy in copies:
+        copy.wait()
+
+
+def finish_kernel(place_ref, base_ref, half_ref, in_ref, out_ref, rows_ref, sem):
+    place = place_ref[0, 1 - lax.rem(lax.axis_index("seq"), 2)]
+
+    @pl.when(place >= 0)
+    def _():
+        rows = pl.ds(pl.multiple_of(place * BLOCK_TOKENS, BLOCK_TOKENS), BLOCK_TOKENS)
+        for i in range(2):
+            total = base_ref[i, rows, :] + half_ref[i].astype(F32)
+            rows_ref[:, i * WIDTH : (i + 1) * WIDTH] = total.astype(BF)
+        copy = pltpu.make_async_copy(rows_ref, out_ref.at[rows], sem)
+        copy.start()
+        copy.wait()
 
 
 def list_bias(random_table, pos, peers, nb):
@@ -274,19 +307,21 @@
 
     q = queries[0]
     own = packed_key_value[0]
-    on = exchange(own, twin)
     shifted = exchange(incoming[0], [(i, i - 1) for i in range(1, sections)], "section")
-    table = jnp.concatenate([global_blocks // nb, global_blocks % nb], 0)
-    (held,) = call(
-        pick_kernel, [SMEM, HBM, VMEM],
-        [shape(BLOCK_TOKENS, own.shape[1], dtype=BF)],
-        (table, pltpu.with_memory_space_constraint(own, pltpu.HBM), on), 10**6, [pltpu.SemaphoreType.DMA],
-    )
-    off = exchange(own, side)
-    own, q, loss_grad = call(
-        load_kernel, [HBM] * 3,
-        [shape(*x.shape, dtype=BF) for x in (own, q, loss_grad)],
-        [pltpu.with_memory_space_constraint(x, pltpu.HBM) for x in (own, q, loss_grad)], 10**7, [pltpu.SemaphoreType.DMA((3,))],
+    held, give, own_near = call(
+        pick_kernel, [HBM] * 2,
+        [shape(BLOCK_TOKENS, own.shape[1], dtype=BF)] * 2 + [shape(*own.shape, dtype=BF)],
+        [pltpu.with_memory_space_constraint(x, pltpu.HBM) for x in (global_blocks, own)], 10**6,
+        [pltpu.SMEM((1, GLOBAL_BLOCKS), jnp.int32), pltpu.SemaphoreType.DMA((2,))],
+    )
+    held = held + exchange(give, twin)
+    on = exchange(own_near, twin)
+    off = exchange(own_near, side)
+    own = own_near
+    q, loss_grad = call(
+        load_kernel, [HBM] * 2, [shape(*x.shape, dtype=BF) for x in (q, loss_grad)],
+        [pltpu.with_memory_space_constraint(x, pltpu.HBM) for x in (q, loss_grad)], 10**7,
+        [pltpu.SemaphoreType.DMA((2,))],
     )
     for masks in rounds:
         got = [exchange(held, flipped(m)) for m in masks]
@@ -335,7 +370,8 @@
         near + (held, other, ds_local, ds), 2 * 10**9,
     )
     (place,) = call(
-        place_kernel, [VMEM], [shape(1, GLOBAL_BLOCKS, dtype=jnp.int32)], (table,), 1000
+        functools.partial(place_kernel, nb), [VMEM],
+        [shape(1, GLOBAL_BLOCKS, dtype=jnp.int32)], (global_blocks,), 1000,
     )
     r_on = exchange(g_on, twin)
     r_off = exchange(g_off, side)
@@ -345,9 +381,16 @@
         total = sum([x.astype(F32) for x in got], total)
     half = total.astype(BF)
     half_other = exchange(half, twin)
+    base, out = call(
+        merge_kernel, [SMEM] + [VMEM] * 4,
+        [shape(2, toks, WIDTH), shape(*own.shape, dtype=BF)],
+        (place, g_own, r_on, r_off, half), 10**6,
+        [pltpu.VMEM(own.shape, BF), pltpu.SemaphoreType.DMA((nb,))], [VMEM, HBM],
+    )
     (out,) = call(
-        finish_kernel, [SMEM] + [VMEM] * 5, [shape(*own.shape, dtype=BF)],
-        (place, g_own, r_on, r_off, half, half_other), 10**6,
+        finish_kernel, [SMEM, VMEM, VMEM, HBM], [shape(*own.shape, dtype=BF)],
+        (place, base, half_other, out), 10**6,
+        [pltpu.VMEM((BLOCK_TOKENS, own.shape[1]), BF), pltpu.SemaphoreType.DMA], [HBM], {3: 0},
     )
     return (dq[None], out[None])
 

time: 56.4 us -> 59.6 us (1.057)
  waiting for transfers between devices: 16.6 us -> 18.3 us
  Pallas kernels: 11.6 us -> 12.8 us
  starting transfers between devices: 25.2 us -> 26 us
  other arithmetic: 1.23 us -> 0.57 us
    ppermute x16 -> x17, waiting for transfers between devices: 16.6 us -> 18.3 us  [exchange(): return lax.ppermute(x, axis, pairs)]
    pallas_call x9 -> x10, Pallas kernels: 11.6 us -> 12.8 us  [call(): pl.pallas_call(kernel, in_specs=ins, out_specs=out_specs or [VMEM] * len(...]
    ppermute x16 -> x17, starting transfers between devices: 25.2 us -> 26 us  [exchange(): return lax.ppermute(x, axis, pairs)]
    select_n x1 -> x0, other arithmetic: 0.67 us -> none  [body(): table = jnp.concatenate([global_blocks // nb, global_blocks % nb], 0)]
  transfers between devices with their start and end apart: 16 -> 17, of which waited for: 11 -> 11; matrix products, arithmetic and copies ran while one was open for 2% -> 1% of each run, Pallas kernels for 14% -> 15%
where the time goes in v5:
time: 59.6 us; the launch traced here: 58.7 us
  starting transfers between devices  26 us (44%)
  waiting for transfers between devices  18.3 us (31%)
  Pallas kernels  12.8 us (21%)
  between operations  0.77 us (1%)
    ppermute x17, starting transfers between devices, exchange(): return lax.ppermute(x, axis, pairs)  26 us
    ppermute x17, waiting for transfers between devices, exchange(): return lax.ppermute(x, axis, pairs)  18.3 us
    pallas_call x10, Pallas kernels, call(): pl.pallas_call(kernel, in_specs=ins, out_specs=out_specs or [VMEM] * len(...  12.8 us
  transfers between devices with their start and end apart: 17, of which 11 were waited for; matrix products, arithmetic and copies ran while one was open for 1% of the time, Pallas kernels for 15%

profile of v5, /device:TPU:11, one launch (start us, length us, event | category | flops | bytes accessed | tf_op | source)
XLA Modules:
  0.0 58.7 jit_solution(15093581907408561492)
XLA Ops:
  0.6 1.0 %shard_map.77 = (bf16[64,1024]{1,0:T(8,128)(2,1)S(1)}, bf16[64,1024]{1,0:T(8,128)(2,1)S(1)}, bf16[128,1024]{1,0:T(8,128)(2,1)S(1)}) custom-call(s32[1,2]{1,0:T(1,128)} %ids_ref.3, bf16[128,1024]{1,0:T(8,128)(2,1)} %bitcast.8), custom_call_target="tpu_custom_call" | custom-call | flops 1000000 | bytes 2000 | tf_op jit(solution)/shard_map/pallas_call | solution.py:38
  1.6 0.7 %collective-permute-start = (bf16[128,1024]{1,0:T(8,128)(2,1)S(1)}, bf16[128,1024]{1,0:T(8,128)(2,1)S(1)}, u32[]{:S(2)}, u32[]{:S(2)}) collective-permute-start(bf16[128,1024]{1,0:T(8,128)(2,1)S(1)} %get-tuple-element.22.own_ref), channel_id=1, source_target_pairs={{0,1},{1,0},{2,3},{3,2},{4,5},{5,4},{6,7},{7,6},{8,9},{9,8},{10,11... | collective-permute-start | bytes 786440 | tf_op jit(solution)/shard_map/ppermute | solution.py:306
  2.4 3.0 %collective-permute-start.1 = (bf16[128,1024]{1,0:T(8,128)(2,1)S(1)}, bf16[128,1024]{1,0:T(8,128)(2,1)S(1)}, u32[]{:S(2)}, u32[]{:S(2)}) collective-permute-start(bf16[128,1024]{1,0:T(8,128)(2,1)S(1)} %get-tuple-element.22.own_ref), channel_id=1, source_target_pairs={{1,2},{3,4},{5,6},{7,8},{9,10},{11,12},{13,14},{2,1},{4,3},{6,5},{... | collective-permute-start | bytes 786440 | tf_op jit(solution)/shard_map/ppermute | solution.py:306
  5.4 2.2 %collective-permute-start.8 = (bf16[128,3072]{1,0:T(8,128)(2,1)}, bf16[128,3072]{1,0:T(8,128)(2,1)S(1)}, u32[]{:S(2)}, u32[]{:S(2)}) collective-permute-start(bf16[128,3072]{1,0:T(8,128)(2,1)} %bitcast.10), channel_id=1, source_target_pairs={{16,0},{17,1},{18,2},{19,3},{20,4},{21,5},{22,6},{23,7},{24,8},{25... | collective-permute-start | bytes 2359304 | tf_op jit(solution)/shard_map/ppermute | solution.py:306
  7.7 0.7 %collective-permute-start.2 = (bf16[64,1024]{1,0:T(8,128)(2,1)S(1)}, bf16[64,1024]{1,0:T(8,128)(2,1)S(1)}, u32[]{:S(2)}, u32[]{:S(2)}) collective-permute-start(bf16[64,1024]{1,0:T(8,128)(2,1)S(1)} %get-tuple-element.24), channel_id=1, source_target_pairs={{0,1},{1,0},{2,3},{3,2},{4,5},{5,4},{6,7},{7,6},{8,9},{9,8},{10,11... | collective-permute-start | bytes 393224 | tf_op jit(solution)/shard_map/ppermute | solution.py:306
  8.5 0.8 %collective-permute-done.2 = bf16[64,1024]{1,0:T(8,128)(2,1)S(1)} collective-permute-done((bf16[64,1024]{1,0:T(8,128)(2,1)S(1)}, bf16[64,1024]{1,0:T(8,128)(2,1)S(1)}, u32[]{:S(2)}, u32[]{:S(2)}) %collective-permute-start.2) | collective-permute-done | bytes 131104 | tf_op jit(solution)/shard_map/ppermute | solution.py:306
  9.4 1.0 %collective-permute-start.3 = (bf16[64,1024]{1,0:T(8,128)(2,1)S(1)}, bf16[64,1024]{1,0:T(8,128)(2,1)S(1)}, u32[]{:S(2)}, u32[]{:S(2)}) collective-permute-start(bf16[64,1024]{1,0:T(8,128)(2,1)S(1)} %add.87), channel_id=1, source_target_pairs={{0,2},{1,3},{2,0},{3,1},{4,6},{5,7},{6,4},{7,5},{8,10},{9,11},{10,... | collective-permute-start | bytes 393224 | tf_op jit(solution)/shard_map/ppermute | solution.py:306
  10.9 4.1 %collective-permute-done.3 = bf16[64,1024]{1,0:T(8,128)(2,1)S(1)} collective-permute-done((bf16[64,1024]{1,0:T(8,128)(2,1)S(1)}, bf16[64,1024]{1,0:T(8,128)(2,1)S(1)}, u32[]{:S(2)}, u32[]{:S(2)}) %collective-permute-start.3) | collective-permute-done | bytes 131104 | tf_op jit(solution)/shard_map/ppermute | solution.py:306
  15.0 1.5 %collective-permute-start.5 = (bf16[64,1024]{1,0:T(8,128)(2,1)S(1)}, bf16[64,1024]{1,0:T(8,128)(2,1)S(1)}, u32[]{:S(2)}, u32[]{:S(2)}) collective-permute-start(bf16[64,1024]{1,0:T(8,128)(2,1)S(1)} %add.87), channel_id=1, source_target_pairs={{0,6},{1,7},{2,4},{3,5},{4,2},{5,3},{6,0},{7,1},{8,14},{9,15},{10,... | collective-permute-start | bytes 393224 | tf_op jit(solution)/shard_map/ppermute | solution.py:306
  16.5 1.4 %shard_map.78 = (bf16[128,3072]{1,0:T(8,128)(2,1)S(1)}, bf16[128,3072]{1,0:T(8,128)(2,1)S(1)}) custom-call(bf16[128,3072]{1,0:T(8,128)(2,1)} %bitcast.7, bf16[128,3072]{1,0:T(8,128)(2,1)} %b_ref.1), custom_call_target="tpu_custom_call" | custom-call | flops 10000000 | bytes 20000 | tf_op jit(solution)/shard_map/pallas_call | solution.py:38
  17.9 1.8 %collective-permute-done.5 = bf16[64,1024]{1,0:T(8,128)(2,1)S(1)} collective-permute-done((bf16[64,1024]{1,0:T(8,128)(2,1)S(1)}, bf16[64,1024]{1,0:T(8,128)(2,1)S(1)}, u32[]{:S(2)}, u32[]{:S(2)}) %collective-permute-start.5) | collective-permute-done | bytes 131104 | tf_op jit(solution)/shard_map/ppermute | solution.py:306
  19.7 1.4 %collective-permute-start.6 = (bf16[64,1024]{1,0:T(8,128)(2,1)S(1)}, bf16[64,1024]{1,0:T(8,128)(2,1)S(1)}, u32[]{:S(2)}, u32[]{:S(2)}) collective-permute-start(bf16[64,1024]{1,0:T(8,128)(2,1)S(1)} %add_add_fusion), channel_id=1, source_target_pairs={{0,12},{1,13},{2,14},{3,15},{4,8},{5,9},{6,10},{7,11},{8,4},{9,5},... | collective-permute-start | bytes 393224 | tf_op jit(solution)/shard_map/ppermute | solution.py:306
  21.1 2.1 %shard_map.79 = (f32[4,384,768]{2,1,0:T(8,128)S(1)}, f32[4,8,768]{2,1,0:T(8,128)S(1)}) custom-call(f32[2,24]{1,0:T(2,128)S(1)} %reshape.96.bias_ref, bf16[128,3072]{1,0:T(8,128)(2,1)S(1)} %get-tuple-element.25.q_ref, bf16[128,1024]{1,0:T(8,128)(2,1)S(1)} %get-tuple-element.22.own_ref, bf16[128,1024]{1,0:T(8,128)(2,1)S(1)} %collective-permute-done.on_ref, ...), custom_call_target="tpu_custom_call" | custom-call | flops 3000000000 | bytes 6000000 | tf_op jit(solution)/shard_map/pallas_call | solution.py:38
  23.7 5.7 %collective-permute-start.7 = (bf16[64,1024]{1,0:T(8,128)(2,1)S(1)}, bf16[64,1024]{1,0:T(8,128)(2,1)S(1)}, u32[]{:S(2)}, u32[]{:S(2)}) collective-permute-start(bf16[64,1024]{1,0:T(8,128)(2,1)S(1)} %add.91.held_ref), channel_id=1, source_target_pairs={{0,1},{1,0},{2,3},{3,2},{4,5},{5,4},{6,7},{7,6},{8,9},{9,8},{10,11... | collective-permute-start | bytes 393224 | tf_op jit(solution)/shard_map/ppermute | solution.py:306
  29.4 0.9 %shard_map.80 = (f32[4,384,768]{2,1,0:T(8,128)S(1)}, f32[4,8,768]{2,1,0:T(8,128)S(1)}, bf16[128,3072]{1,0:T(8,128)(2,1)S(1)}) custom-call(bf16[128,3072]{1,0:T(8,128)(2,1)S(1)} %collective-permute-done.8.shifted_ref, bf16[128,3072]{1,0:T(8,128)(2,1)S(1)} %get-tuple-element.26.loss_ref, bf16[128,1024]{1,0:T(8,128)(2,1)S(1)} %get-tuple-element.22.own_ref, ...), custom_call_target="tpu_custom_call" | custom-call | flops 2000000000 | bytes 4000000 | tf_op jit(solution)/shard_map/pallas_call | solution.py:38
  30.4 1.8 %shard_map.81 = (bf16[4,128,768]{2,1,0:T(8,128)(2,1)S(1)}, f32[4,8,768]{2,1,0:T(8,128)S(1)}, f32[2,64,512]{2,1,0:T(8,128)S(1)}, bf16[2,64,512]{2,1,0:T(8,128)(2,1)S(1)}) custom-call(bf16[128,3072]{1,0:T(8,128)(2,1)S(1)} %get-tuple-element.25.q_ref, bf16[128,3072]{1,0:T(8,128)(2,1)S(1)} %get-tuple-element.29.do_ref, bf16[64,1024]{1,0:T(8,128)(2,1)S(1)} %add.91.held_ref, ...), custom_call_target="tpu_custom_call" | custom-call | flops 2000000000 | bytes 4000000 | tf_op jit(solution)/shard_map/pallas_call | solution.py:38
  32.1 0.4 collective-permute-start.11
  32.6 1.0 %collective-permute-done.11 = bf16[2,64,512]{2,1,0:T(8,128)(2,1)S(1)} collective-permute-done((bf16[2,64,512]{2,1,0:T(8,128)(2,1)S(1)}, bf16[2,64,512]{2,1,0:T(8,128)(2,1)S(1)}, u32[]{:S(2)}, u32[]{:S(2)}) %collective-permute-start.11) | collective-permute-done | bytes 131104 | tf_op jit(solution)/shard_map/ppermute | solution.py:306
  33.6 1.8 %collective-permute-start.12 = (bf16[2,64,512]{2,1,0:T(8,128)(2,1)S(1)}, bf16[2,64,512]{2,1,0:T(8,128)(2,1)S(1)}, u32[]{:S(2)}, u32[]{:S(2)}) collective-permute-start(bf16[2,64,512]{2,1,0:T(8,128)(2,1)S(1)} %fusion), channel_id=1, source_target_pairs={{0,2},{1,3},{2,0},{3,1},{4,6},{5,7},{6,4},{7,5},{8,10},{9,11},{10,... | collective-permute-start | bytes 393224 | tf_op jit(solution)/shard_map/ppermute | solution.py:306
  35.3 1.3 %collective-permute-start.14 = (bf16[2,64,512]{2,1,0:T(8,128)(2,1)S(1)}, bf16[2,64,512]{2,1,0:T(8,128)(2,1)S(1)}, u32[]{:S(2)}, u32[]{:S(2)}) collective-permute-start(bf16[2,64,512]{2,1,0:T(8,128)(2,1)S(1)} %fusion), channel_id=1, source_target_pairs={{0,6},{1,7},{2,4},{3,5},{4,2},{5,3},{6,0},{7,1},{8,14},{9,15},{10,... | collective-permute-start | bytes 393224 | tf_op jit(solution)/shard_map/ppermute | solution.py:306
  36.6 2.2 %collective-permute-done.12 = bf16[2,64,512]{2,1,0:T(8,128)(2,1)S(1)} collective-permute-done((bf16[2,64,512]{2,1,0:T(8,128)(2,1)S(1)}, bf16[2,64,512]{2,1,0:T(8,128)(2,1)S(1)}, u32[]{:S(2)}, u32[]{:S(2)}) %collective-permute-start.12) | collective-permute-done | bytes 131104 | tf_op jit(solution)/shard_map/ppermute | solution.py:306
  38.8 0.9 %collective-permute-done.13 = bf16[2,64,512]{2,1,0:T(8,128)(2,1)S(1)} collective-permute-done((bf16[2,64,512]{2,1,0:T(8,128)(2,1)S(1)}, bf16[2,64,512]{2,1,0:T(8,128)(2,1)S(1)}, u32[]{:S(2)}, u32[]{:S(2)}) %collective-permute-start.13) | collective-permute-done | bytes 131104 | tf_op jit(solution)/shard_map/ppermute | solution.py:306
  39.8 2.9 %collective-permute-done.14 = bf16[2,64,512]{2,1,0:T(8,128)(2,1)S(1)} collective-permute-done((bf16[2,64,512]{2,1,0:T(8,128)(2,1)S(1)}, bf16[2,64,512]{2,1,0:T(8,128)(2,1)S(1)}, u32[]{:S(2)}, u32[]{:S(2)}) %collective-permute-start.14) | collective-permute-done | bytes 131104 | tf_op jit(solution)/shard_map/ppermute | solution.py:306
  42.7 0.7 %collective-permute-start.15 = (bf16[2,64,512]{2,1,0:T(8,128)(2,1)S(1)}, bf16[2,64,512]{2,1,0:T(8,128)(2,1)S(1)}, u32[]{:S(2)}, u32[]{:S(2)}) collective-permute-start(bf16[2,64,512]{2,1,0:T(8,128)(2,1)S(1)} %fusion.1), channel_id=1, source_target_pairs={{0,12},{1,13},{2,14},{3,15},{4,8},{5,9},{6,10},{7,11},{8,4},{9,5},... | collective-permute-start | bytes 393224 | tf_op jit(solution)/shard_map/ppermute | solution.py:306
  43.5 1.5 %shard_map.82 = (f32[2,128,512]{2,1,0:T(8,128)S(1)}, bf16[2,128,512]{2,1,0:T(8,128)(2,1)S(1)}, bf16[2,128,512]{2,1,0:T(8,128)(2,1)S(1)}, bf16[4,384,768]{2,1,0:T(8,128)(2,1)S(1)}) custom-call(bf16[128,3072]{1,0:T(8,128)(2,1)S(1)} %get-tuple-element.25.q_ref, bf16[128,3072]{1,0:T(8,128)(2,1)S(1)} %get-tuple-element.29.do_ref, ...), custom_call_target="tpu_custom_call" | custom-call | flops 3000000000 | bytes 6000000 | tf_op jit(solution)/shard_map/pallas_call | solution.py:38
  44.9 4.3 %collective-permute-start.10 = (bf16[2,128,512]{2,1,0:T(8,128)(2,1)S(1)}, bf16[2,128,512]{2,1,0:T(8,128)(2,1)S(1)}, u32[]{:S(2)}, u32[]{:S(2)}) collective-permute-start(bf16[2,128,512]{2,1,0:T(8,128)(2,1)S(1)} %get-tuple-element.37), channel_id=1, source_target_pairs={{1,2},{3,4},{5,6},{7,8},{9,10},{11,12},{13,14},{2,1},{4,3},{6,5},{... | collective-permute-start | bytes 786440 | tf_op jit(solution)/shard_map/ppermute | solution.py:306
  49.5 1.2 %collective-permute-done.15 = bf16[2,64,512]{2,1,0:T(8,128)(2,1)S(1)} collective-permute-done((bf16[2,64,512]{2,1,0:T(8,128)(2,1)S(1)}, bf16[2,64,512]{2,1,0:T(8,128)(2,1)S(1)}, u32[]{:S(2)}, u32[]{:S(2)}) %collective-permute-start.15) | collective-permute-done | bytes 131104 | tf_op jit(solution)/shard_map/ppermute | solution.py:306
  50.8 0.9 %collective-permute-start.16 = (bf16[2,64,512]{2,1,0:T(8,128)(2,1)S(1)}, bf16[2,64,512]{2,1,0:T(8,128)(2,1)S(1)}, u32[]{:S(2)}, u32[]{:S(2)}) collective-permute-start(bf16[2,64,512]{2,1,0:T(8,128)(2,1)S(1)} %add_convert_fusion.half_ref), channel_id=1, source_target_pairs={{0,1},{1,0},{2,3},{3,2},{4,5},{5,4},{6,7},{7,6},{8,9},{9,8},{10,11... | collective-permute-start | bytes 393224 | tf_op jit(solution)/shard_map/ppermute | solution.py:306
  51.7 1.6 %shard_map.83 = bf16[128,3072]{1,0:T(8,128)(2,1)} custom-call(bf16[128,1024]{1,0:T(8,128)(2,1)S(1)} %get-tuple-element.22.own_ref, bf16[128,1024]{1,0:T(8,128)(2,1)S(1)} %collective-permute-done.on_ref, bf16[128,1024]{1,0:T(8,128)(2,1)S(1)} %collective-permute-done.1.off_ref, bf16[64,1024]{1,0:T(8,128)(2,1)S(1)} %add.91.held_ref, ...), custom_call_target="tpu_custom_call" | custom-call | flops 2000000000 | bytes 4000000 | tf_op jit(solution)/shard_map/pallas_call | solution.py:38
  53.3 2.8 %collective-permute-done.10.r_off = bf16[2,128,512]{2,1,0:T(8,128)(2,1)S(1)} collective-permute-done((bf16[2,128,512]{2,1,0:T(8,128)(2,1)S(1)}, bf16[2,128,512]{2,1,0:T(8,128)(2,1)S(1)}, u32[]{:S(2)}, u32[]{:S(2)}) %collective-permute-start.10) | collective-permute-done | bytes 262176 | tf_op jit(solution)/shard_map/ppermute | solution.py:306
  56.1 1.3 %shard_map.85 = (f32[2,128,512]{2,1,0:T(8,128)S(1)}, bf16[128,1024]{1,0:T(8,128)(2,1)}) custom-call(s32[1,2]{1,0:T(1,128)S(1)} %shard_map.84.place_ref, f32[2,128,512]{2,1,0:T(8,128)S(1)} %get-tuple-element.35.g_own, bf16[2,128,512]{2,1,0:T(8,128)(2,1)S(1)} %collective-permute-done.9.r_on, bf16[2,128,512]{2,1,0:T(8,128)(2,1)S(1)} %collective-permute-done.10.r_off, ...), custom_call_target="tpu_custom_call" | custom-call | flops 1000000 | bytes 2000 | tf_op jit(solution)/shard_map/pallas_call | solution.py:38
  57.5 1.2 %shard_map.86 = bf16[128,1024]{1,0:T(8,128)(2,1)} custom-call(s32[1,2]{1,0:T(1,128)S(1)} %shard_map.84.place_ref, f32[2,128,512]{2,1,0:T(8,128)S(1)} %get-tuple-element.40.base_ref, bf16[2,64,512]{2,1,0:T(8,128)(2,1)S(1)} %collective-permute-done.16.half_ref, bf16[128,1024]{1,0:T(8,128)(2,1)} %get-tuple-element.41.in_ref), custom_call_target="tpu_custom_call", output_to_operand_aliasing={{}: (3, {})} | custom-call | flops 1000000 | bytes 2000 | tf_op jit(solution)/shard_map/pallas_call | solution.py:38
  (31 shorter events, 1.8 us)
Async XLA Ops:
  0.6 9.8 %copy-start = (s32[1,32,4,3]{1,2,3,0:T(4,128)S(1)}, s32[1,32,4,3]{1,2,3,0:T(4,128)}, u32[]{:S(2)}) copy-start(s32[1,32,4,3]{1,2,3,0:T(4,128)} %param.11) | copy-start | bytes 4612
  1.6 19.4 %collective-permute-start = (bf16[128,1024]{1,0:T(8,128)(2,1)S(1)}, bf16[128,1024]{1,0:T(8,128)(2,1)S(1)}, u32[]{:S(2)}, u32[]{:S(2)}) collective-permute-start(bf16[128,1024]{1,0:T(8,128)(2,1)S(1)} %get-tuple-element.22.own_ref), channel_id=1, source_target_pairs={{0,1},{1,0},{2,3},{3,2},{4,5},{5,4},{6,7},{7,6},{8,9},{9,8},{10,11... | collective-permute-start | bytes 786440 | tf_op jit(solution)/shard_map/ppermute | solution.py:306
  2.4 18.7 %collective-permute-start.1 = (bf16[128,1024]{1,0:T(8,128)(2,1)S(1)}, bf16[128,1024]{1,0:T(8,128)(2,1)S(1)}, u32[]{:S(2)}, u32[]{:S(2)}) collective-permute-start(bf16[128,1024]{1,0:T(8,128)(2,1)S(1)} %get-tuple-element.22.own_ref), channel_id=1, source_target_pairs={{1,2},{3,4},{5,6},{7,8},{9,10},{11,12},{13,14},{2,1},{4,3},{6,5},{... | collective-permute-start | bytes 786440 | tf_op jit(solution)/shard_map/ppermute | solution.py:306
  5.4 23.9 %collective-permute-start.8 = (bf16[128,3072]{1,0:T(8,128)(2,1)}, bf16[128,3072]{1,0:T(8,128)(2,1)S(1)}, u32[]{:S(2)}, u32[]{:S(2)}) collective-permute-start(bf16[128,3072]{1,0:T(8,128)(2,1)} %bitcast.10), channel_id=1, source_target_pairs={{16,0},{17,1},{18,2},{19,3},{20,4},{21,5},{22,6},{23,7},{24,8},{25... | collective-permute-start | bytes 2359304 | tf_op jit(solution)/shard_map/ppermute | solution.py:306
  7.7 1.7 %collective-permute-start.2 = (bf16[64,1024]{1,0:T(8,128)(2,1)S(1)}, bf16[64,1024]{1,0:T(8,128)(2,1)S(1)}, u32[]{:S(2)}, u32[]{:S(2)}) collective-permute-start(bf16[64,1024]{1,0:T(8,128)(2,1)S(1)} %get-tuple-element.24), channel_id=1, source_target_pairs={{0,1},{1,0},{2,3},{3,2},{4,5},{5,4},{6,7},{7,6},{8,9},{9,8},{10,11... | collective-permute-start | bytes 393224 | tf_op jit(solution)/shard_map/ppermute | solution.py:306
  9.4 5.6 %collective-permute-start.3 = (bf16[64,1024]{1,0:T(8,128)(2,1)S(1)}, bf16[64,1024]{1,0:T(8,128)(2,1)S(1)}, u32[]{:S(2)}, u32[]{:S(2)}) collective-permute-start(bf16[64,1024]{1,0:T(8,128)(2,1)S(1)} %add.87), channel_id=1, source_target_pairs={{0,2},{1,3},{2,0},{3,1},{4,6},{5,7},{6,4},{7,5},{8,10},{9,11},{10,... | collective-permute-start | bytes 393224 | tf_op jit(solution)/shard_map/ppermute | solution.py:306
  10.7 7.2 %collective-permute-start.4 = (bf16[64,1024]{1,0:T(8,128)(2,1)S(1)}, bf16[64,1024]{1,0:T(8,128)(2,1)S(1)}, u32[]{:S(2)}, u32[]{:S(2)}) collective-permute-start(bf16[64,1024]{1,0:T(8,128)(2,1)S(1)} %add.87), channel_id=1, source_target_pairs={{0,4},{1,5},{2,6},{3,7},{4,0},{5,1},{6,2},{7,3},{8,12},{9,13},{10,... | collective-permute-start | bytes 393224 | tf_op jit(solution)/shard_map/ppermute | solution.py:306
  15.0 4.7 %collective-permute-start.5 = (bf16[64,1024]{1,0:T(8,128)(2,1)S(1)}, bf16[64,1024]{1,0:T(8,128)(2,1)S(1)}, u32[]{:S(2)}, u32[]{:S(2)}) collective-permute-start(bf16[64,1024]{1,0:T(8,128)(2,1)S(1)} %add.87), channel_id=1, source_target_pairs={{0,6},{1,7},{2,4},{3,5},{4,2},{5,3},{6,0},{7,1},{8,14},{9,15},{10,... | collective-permute-start | bytes 393224 | tf_op jit(solution)/shard_map/ppermute | solution.py:306
  19.7 3.9 %collective-permute-start.6 = (bf16[64,1024]{1,0:T(8,128)(2,1)S(1)}, bf16[64,1024]{1,0:T(8,128)(2,1)S(1)}, u32[]{:S(2)}, u32[]{:S(2)}) collective-permute-start(bf16[64,1024]{1,0:T(8,128)(2,1)S(1)} %add_add_fusion), channel_id=1, source_target_pairs={{0,12},{1,13},{2,14},{3,15},{4,8},{5,9},{6,10},{7,11},{8,4},{9,5},... | collective-permute-start | bytes 393224 | tf_op jit(solution)/shard_map/ppermute | solution.py:306
  23.7 6.7 %collective-permute-start.7 = (bf16[64,1024]{1,0:T(8,128)(2,1)S(1)}, bf16[64,1024]{1,0:T(8,128)(2,1)S(1)}, u32[]{:S(2)}, u32[]{:S(2)}) collective-permute-start(bf16[64,1024]{1,0:T(8,128)(2,1)S(1)} %add.91.held_ref), channel_id=1, source_target_pairs={{0,1},{1,0},{2,3},{3,2},{4,5},{5,4},{6,7},{7,6},{8,9},{9,8},{10,11... | collective-permute-start | bytes 393224 | tf_op jit(solution)/shard_map/ppermute | solution.py:306
  30.2 6.4 %copy-start.1 = (s32[1,2]{1,0:T(1,128)S(1)}, s32[1,2]{1,0:T(1,128)}, u32[]{:S(2)}) copy-start(s32[1,2]{1,0:T(1,128)} %ids_ref.3) | copy-start | bytes 28
  32.1 1.4 %collective-permute-start.11 = (bf16[2,64,512]{2,1,0:T(8,128)(2,1)S(1)}, bf16[2,64,512]{2,1,0:T(8,128)(2,1)S(1)}, u32[]{:S(2)}, u32[]{:S(2)}) collective-permute-start(bf16[2,64,512]{2,1,0:T(8,128)(2,1)S(1)} %get-tuple-element.39), channel_id=1, source_target_pairs={{0,1},{1,0},{2,3},{3,2},{4,5},{5,4},{6,7},{7,6},{8,9},{9,8},{10,11... | collective-permute-start | bytes 393224 | tf_op jit(solution)/shard_map/ppermute | solution.py:306
  33.6 5.2 %collective-permute-start.12 = (bf16[2,64,512]{2,1,0:T(8,128)(2,1)S(1)}, bf16[2,64,512]{2,1,0:T(8,128)(2,1)S(1)}, u32[]{:S(2)}, u32[]{:S(2)}) collective-permute-start(bf16[2,64,512]{2,1,0:T(8,128)(2,1)S(1)} %fusion), channel_id=1, source_target_pairs={{0,2},{1,3},{2,0},{3,1},{4,6},{5,7},{6,4},{7,5},{8,10},{9,11},{10,... | collective-permute-start | bytes 393224 | tf_op jit(solution)/shard_map/ppermute | solution.py:306
  35.3 4.4 %collective-permute-start.13 = (bf16[2,64,512]{2,1,0:T(8,128)(2,1)S(1)}, bf16[2,64,512]{2,1,0:T(8,128)(2,1)S(1)}, u32[]{:S(2)}, u32[]{:S(2)}) collective-permute-start(bf16[2,64,512]{2,1,0:T(8,128)(2,1)S(1)} %fusion), channel_id=1, source_target_pairs={{0,4},{1,5},{2,6},{3,7},{4,0},{5,1},{6,2},{7,3},{8,12},{9,13},{10,... | collective-permute-start | bytes 393224 | tf_op jit(solution)/shard_map/ppermute | solution.py:306
  35.3 7.3 %collective-permute-start.14 = (bf16[2,64,512]{2,1,0:T(8,128)(2,1)S(1)}, bf16[2,64,512]{2,1,0:T(8,128)(2,1)S(1)}, u32[]{:S(2)}, u32[]{:S(2)}) collective-permute-start(bf16[2,64,512]{2,1,0:T(8,128)(2,1)S(1)} %fusion), channel_id=1, source_target_pairs={{0,6},{1,7},{2,4},{3,5},{4,2},{5,3},{6,0},{7,1},{8,14},{9,15},{10,... | collective-permute-start | bytes 393224 | tf_op jit(solution)/shard_map/ppermute | solution.py:306
  42.7 8.0 %collective-permute-start.15 = (bf16[2,64,512]{2,1,0:T(8,128)(2,1)S(1)}, bf16[2,64,512]{2,1,0:T(8,128)(2,1)S(1)}, u32[]{:S(2)}, u32[]{:S(2)}) collective-permute-start(bf16[2,64,512]{2,1,0:T(8,128)(2,1)S(1)} %fusion.1), channel_id=1, source_target_pairs={{0,12},{1,13},{2,14},{3,15},{4,8},{5,9},{6,10},{7,11},{8,4},{9,5},... | collective-permute-start | bytes 393224 | tf_op jit(solution)/shard_map/ppermute | solution.py:306
  44.9 11.2 %collective-permute-start.10 = (bf16[2,128,512]{2,1,0:T(8,128)(2,1)S(1)}, bf16[2,128,512]{2,1,0:T(8,128)(2,1)S(1)}, u32[]{:S(2)}, u32[]{:S(2)}) collective-permute-start(bf16[2,128,512]{2,1,0:T(8,128)(2,1)S(1)} %get-tuple-element.37), channel_id=1, source_target_pairs={{1,2},{3,4},{5,6},{7,8},{9,10},{11,12},{13,14},{2,1},{4,3},{6,5},{... | collective-permute-start | bytes 786440 | tf_op jit(solution)/shard_map/ppermute | solution.py:306
  49.3 6.9 %collective-permute-start.9 = (bf16[2,128,512]{2,1,0:T(8,128)(2,1)S(1)}, bf16[2,128,512]{2,1,0:T(8,128)(2,1)S(1)}, u32[]{:S(2)}, u32[]{:S(2)}) collective-permute-start(bf16[2,128,512]{2,1,0:T(8,128)(2,1)S(1)} %get-tuple-element.36), channel_id=1, source_target_pairs={{0,1},{1,0},{2,3},{3,2},{4,5},{5,4},{6,7},{7,6},{8,9},{9,8},{10,11... | collective-permute-start | bytes 786440 | tf_op jit(solution)/shard_map/ppermute | solution.py:306
  50.8 6.7 %collective-permute-start.16 = (bf16[2,64,512]{2,1,0:T(8,128)(2,1)S(1)}, bf16[2,64,512]{2,1,0:T(8,128)(2,1)S(1)}, u32[]{:S(2)}, u32[]{:S(2)}) collective-permute-start(bf16[2,64,512]{2,1,0:T(8,128)(2,1)S(1)} %add_convert_fusion.half_ref), channel_id=1, source_target_pairs={{0,1},{1,0},{2,3},{3,2},{4,5},{5,4},{6,7},{7,6},{8,9},{9,8},{10,11... | collective-permute-start | bytes 393224 | tf_op jit(solution)/shard_map/ppermute | solution.py:306

commit v6 on v5

--- a/solution.py
+++ b/solution.py
@@ -104,23 +104,22 @@
             out[...] = jnp.zeros_like(out)
 
 
-def local_kernel(bias_ref, q_ref, own_ref, on_ref, off_ref, w_ref, stat_ref):
-    toks = q_ref.shape[0]
-    nb = toks // BLOCK_TOKENS
-    ncand = 3 * nb
+def listed_scores(s, bias_ref, e, first):
+    cols = slice(e * ROWS_E, (e + 1) * ROWS_E)
+    parts = [
+        s[j * BLOCK_TOKENS : (j + 1) * BLOCK_TOKENS, cols] * (SCALE * LOG2E)
+        + bias_ref[e, first + j]
+        for j in range(s.shape[0] // BLOCK_TOKENS)
+    ]
+    return cols, jnp.concatenate(parts, 0)
+
+
+def local_kernel(bias_ref, q_ref, own_ref, on_ref, w_ref, stat_ref):
+    nb = q_ref.shape[0] // BLOCK_TOKENS
     for g in range(KEY_HEADS):
-        keys = stacked((own_ref, on_ref, off_ref), g * HEAD_SIZE)
-        s = dot(keys, group_rows(q_ref, g), NT)
+        s = dot(stacked((own_ref, on_ref), g * HEAD_SIZE), group_rows(q_ref, g), NT)
         for e in range(nb):
-            cols = slice(e * ROWS_E, (e + 1) * ROWS_E)
-            t = jnp.concatenate(
-                [
-                    s[j * BLOCK_TOKENS : (j + 1) * BLOCK_TOKENS, cols] * (SCALE * LOG2E)
-                    + bias_ref[e, g * ncand + j]
-                    for j in range(ncand)
-                ],
-                0,
-            )
+            cols, t = listed_scores(s, bias_ref, e, g * 3 * nb)
             m = jnp.max(t, axis=0, keepdims=True)
             w = jnp.exp2(t - m)
             w_ref[g, :, cols] = w
@@ -128,8 +127,27 @@
             stat_ref[g, 1:2, cols] = jnp.sum(w, axis=0, keepdims=True)
 
 
+def far_kernel(bias_ref, q_ref, off_ref, stat_ref, w_ref, out_stat_ref):
+    nb = q_ref.shape[0] // BLOCK_TOKENS
+    for g in range(KEY_HEADS):
+        s = dot(off_ref[:, g * HEAD_SIZE : (g + 1) * HEAD_SIZE], group_rows(q_ref, g), NT)
+        for e in range(nb):
+            cols, t = listed_scores(s, bias_ref, e, g * 3 * nb + 2 * nb)
+            m_near = stat_ref[g, 0:1, cols]
+            m = jnp.maximum(m_near, jnp.max(t, axis=0, keepdims=True))
+            w = jnp.exp2(t - m)
+            w_ref[g, :, cols] = w
+            shrink = jnp.exp2(m_near - m)
+            out_stat_ref[g, 0:1, cols] = m
+            out_stat_ref[g, 1:2, cols] = shrink * stat_ref[g, 1:2, cols] + jnp.sum(
+                w, axis=0, keepdims=True
+            )
+            out_stat_ref[g, 2:3, cols] = shrink
+
+
 def near_kernel(
-    shifted_ref, loss_ref, own_ref, on_ref, off_ref, w_ref, stat_ref, dp_ref, out_stat_ref, do_ref
+    shifted_ref, loss_ref, own_ref, on_ref, off_ref, w_ref, w_off_ref, stat_ref,
+    dp_ref, dp_off_ref, out_stat_ref, do_ref,
 ):
     last = at_last_section()
 
@@ -142,11 +160,16 @@
         do_ref[...] = shifted_ref[...]
 
     for g in range(KEY_HEADS):
-        vals = stacked((own_ref, on_ref, off_ref), WIDTH + g * HEAD_SIZE)
-        dp = dot(vals, group_rows(do_ref, g), NT)
+        vc = WIDTH + g * HEAD_SIZE
+        dog = group_rows(do_ref, g)
+        dp = dot(stacked((own_ref, on_ref), vc), dog, NT)
+        dp_off = dot(off_ref[:, vc : vc + HEAD_SIZE], dog, NT)
         dp_ref[g] = dp
-        out_stat_ref[g, 0:2, :] = stat_ref[g, 0:2, :]
-        out_stat_ref[g, 2:3, :] = jnp.sum(w_ref[g] * dp, axis=0, keepdims=True)
+        dp_off_ref[g] = dp_off
+        out_stat_ref[g, 0:3, :] = stat_ref[g, 0:3, :]
+        out_stat_ref[g, 3:4, :] = stat_ref[g, 2:3, :] * jnp.sum(
+            w_ref[g] * dp, axis=0, keepdims=True
+        ) + jnp.sum(w_off_ref[g] * dp_off, axis=0, keepdims=True)
 
 
 def global_kernel(
@@ -168,10 +191,11 @@
         inv = 1.0 / total
         p = w * inv
         local_factor = shrink * inv
-        delta = local_factor * stat_ref[g, 2:3, :] + jnp.sum(p * dp, axis=0, keepdims=True)
+        delta = local_factor * stat_ref[g, 3:4, :] + jnp.sum(p * dp, axis=0, keepdims=True)
         ds = (p * (dp - delta) * SCALE).astype(BF)
         ds_ref[g] = ds
-        out_stat_ref[g, 0:1, :] = local_factor
+        out_stat_ref[g, 0:1, :] = local_factor * stat_ref[g, 2:3, :]
+        out_stat_ref[g, 2:3, :] = local_factor
         out_stat_ref[g, 1:2, :] = delta
         return ds, p.astype(BF)
 
@@ -181,28 +205,28 @@
             keep_ref[i, :, cols] = grad[:BLOCK_TOKENS]
             give_ref[i, :, cols] = grad[BLOCK_TOKENS:].astype(BF)
 
-    first = scores(0)
-    for g in range(KEY_HEADS):
-        qg, dog, t, dp = first
-        if g + 1 < KEY_HEADS:
-            first = scores(g + 1)
+    staged = [scores(g) for g in range(KEY_HEADS)]
+    for g, (qg, dog, t, dp) in enumerate(staged):
         ds, p = weights(g, t, dp)
         sums(g, ds, p, qg, dog)
 
 
-def local_ds(w_ref, dp_ref, stat_ref, g):
-    p = w_ref[g] * stat_ref[g, 0:1, :]
-    return p, (p * (dp_ref[g] - stat_ref[g, 1:2, :]) * SCALE).astype(BF)
-
-
-def pairs_kernel(q_ref, do_ref, w_ref, dp_ref, stat_ref, g_own, g_on, g_off, ds_ref):
+def pairs_kernel(
+    q_ref, do_ref, w_ref, w_off_ref, dp_ref, dp_off_ref, stat_ref, g_own, g_on, g_off, ds_ref
+):
     toks = q_ref.shape[0]
     for g in range(KEY_HEADS):
-        p, ds = local_ds(w_ref, dp_ref, stat_ref, g)
+        delta = stat_ref[g, 1:2, :]
+        ps, dss = [], []
+        for factor, w, dp in ((0, w_ref, dp_ref), (2, w_off_ref, dp_off_ref)):
+            p = w[g] * stat_ref[g, factor : factor + 1, :]
+            ps.append(p.astype(BF))
+            dss.append((p * (dp[g] - delta) * SCALE).astype(BF))
+        p = jnp.concatenate(ps, 0)
+        ds = jnp.concatenate(dss, 0)
         ds_ref[g] = ds
         cols = slice(g * HEAD_SIZE, (g + 1) * HEAD_SIZE)
-        grads = (dot(ds, group_rows(q_ref, g), NN), dot(p.astype(BF), group_rows(do_ref, g), NN))
-        for i, grad in enumerate(grads):
+        for i, grad in enumerate((dot(ds, group_rows(q_ref, g), NN), dot(p, group_rows(do_ref, g), NN))):
             g_own[i, :, cols] = grad[:toks]
             g_on[i, :, cols] = grad[toks : 2 * toks].astype(BF)
             g_off[i, :, cols] = grad[2 * toks :].astype(BF)
@@ -331,18 +355,24 @@
     bias = list_bias(random_blocks[0], pos, peers, nb)
     near = (own, on, off)
     w, stats = call(
-        local_kernel, [SMEM] + [VMEM] * 4,
-        [shape(KEY_HEADS, 3 * toks, rows), shape(KEY_HEADS, 8, rows)],
-        (bias, q) + near, 3 * 10**9,
-    )
-    dp, stats, d_out = call(
-        near_kernel, [VMEM] * 7,
+        local_kernel, [SMEM] + [VMEM] * 3,
+        [shape(KEY_HEADS, 2 * toks, rows), shape(KEY_HEADS, 8, rows)],
+        (bias, q, own, on), 2 * 10**9,
+    )
+    w_off, stats = call(
+        far_kernel, [SMEM] + [VMEM] * 3,
+        [shape(KEY_HEADS, toks, rows), shape(KEY_HEADS, 8, rows)],
+        (bias, q, off, stats), 10**9,
+    )
+    dp, dp_off, stats, d_out = call(
+        near_kernel, [VMEM] * 8,
         [
-            shape(KEY_HEADS, 3 * toks, rows),
+            shape(KEY_HEADS, 2 * toks, rows),
+            shape(KEY_HEADS, toks, rows),
             shape(KEY_HEADS, 8, rows),
             shape(*q.shape, dtype=BF),
         ],
-        (shifted, loss_grad) + near + (w, stats), 2 * 10**9,
+        (shifted, loss_grad) + near + (w, w_off, stats), 2 * 10**9,
     )
     ds, stats, keep, give = call(
         global_kernel, [VMEM] * 5,
@@ -356,14 +386,14 @@
     )
     total = keep + exchange(give, twin).astype(F32)
     g_own, g_on, g_off, ds_local = call(
-        pairs_kernel, [VMEM] * 5,
+        pairs_kernel, [VMEM] * 7,
         [
             shape(2, toks, WIDTH),
             shape(2, toks, WIDTH, dtype=BF),
             shape(2, toks, WIDTH, dtype=BF),
             shape(KEY_HEADS, 3 * toks, rows, dtype=BF),
         ],
-        (q, d_out, w, dp, stats), 3 * 10**9,
+        (q, d_out, w, w_off, dp, dp_off, stats), 3 * 10**9,
     )
     (dq,) = call(
         queries_kernel, [VMEM] * 7, [shape(*q.shape, dtype=BF)],

time: 59.6 us -> 55.4 us (0.930); the launches traced: 58.7 us -> 55.2 us
  waiting for transfers between devices: 18.3 us -> 15.5 us
  starting transfers between devices: 26 us -> 24.7 us
    ppermute x17, waiting for transfers between devices: 18.3 us -> 15.5 us  [exchange(): return lax.ppermute(x, axis, pairs)]
    ppermute x17, starting transfers between devices: 26 us -> 24.7 us  [exchange(): return lax.ppermute(x, axis, pairs)]
    pallas_call x10 -> x11, Pallas kernels: 12.8 us -> 13.3 us  [call(): pl.pallas_call(kernel, in_specs=ins, out_specs=out_specs or [VMEM] * len(...]
  transfers between devices with their start and end apart: 17 -> 17, of which waited for: 11 -> 10; matrix products, arithmetic and copies ran while one was open for 1% -> 1% of each run, Pallas kernels for 15% -> 17%
where the time goes in v6:
time: 55.4 us; the launch traced here: 55.2 us
  starting transfers between devices  24.7 us (45%)
  waiting for transfers between devices  15.5 us (28%)
  Pallas kernels  13.3 us (24%)
  between operations  0.8 us (1%)
  other arithmetic  0.59 us (1%)
    ppermute x17, starting transfers between devices, exchange(): return lax.ppermute(x, axis, pairs)  24.7 us
    ppermute x17, waiting for transfers between devices, exchange(): return lax.ppermute(x, axis, pairs)  15.5 us
    pallas_call x11, Pallas kernels, call(): pl.pallas_call(kernel, in_specs=ins, out_specs=out_specs or [VMEM] * len(...  13.3 us
  transfers between devices with their start and end apart: 17, of which 10 were waited for; matrix products, arithmetic and copies ran while one was open for 1% of the time, Pallas kernels for 17%

profile of v6, /device:TPU:11, one launch (start us, length us, event | category | flops | bytes accessed | tf_op | source)
XLA Modules:
  0.0 55.2 jit_solution(9692445992968927803)
XLA Ops:
  0.6 1.0 %shard_map.77 = (bf16[64,1024]{1,0:T(8,128)(2,1)S(1)}, bf16[64,1024]{1,0:T(8,128)(2,1)S(1)}, bf16[128,1024]{1,0:T(8,128)(2,1)S(1)}) custom-call(s32[1,2]{1,0:T(1,128)} %ids_ref.3, bf16[128,1024]{1,0:T(8,128)(2,1)} %bitcast.8), custom_call_target="tpu_custom_call" | custom-call | flops 1000000 | bytes 2000 | tf_op jit(solution)/shard_map/pallas_call | solution.py:38
  1.6 0.7 %collective-permute-start = (bf16[128,1024]{1,0:T(8,128)(2,1)S(1)}, bf16[128,1024]{1,0:T(8,128)(2,1)S(1)}, u32[]{:S(2)}, u32[]{:S(2)}) collective-permute-start(bf16[128,1024]{1,0:T(8,128)(2,1)S(1)} %get-tuple-element.25.own_ref), channel_id=1, source_target_pairs={{0,1},{1,0},{2,3},{3,2},{4,5},{5,4},{6,7},{7,6},{8,9},{9,8},{10,11... | collective-permute-start | bytes 786440 | tf_op jit(solution)/shard_map/ppermute | solution.py:330
  2.4 2.2 %collective-permute-start.8 = (bf16[128,3072]{1,0:T(8,128)(2,1)}, bf16[128,3072]{1,0:T(8,128)(2,1)S(1)}, u32[]{:S(2)}, u32[]{:S(2)}) collective-permute-start(bf16[128,3072]{1,0:T(8,128)(2,1)} %bitcast.10), channel_id=1, source_target_pairs={{16,0},{17,1},{18,2},{19,3},{20,4},{21,5},{22,6},{23,7},{24,8},{25... | collective-permute-start | bytes 2359304 | tf_op jit(solution)/shard_map/ppermute | solution.py:330
  4.6 0.4 collective-permute-start.2
  5.4 0.6 %collective-permute-done.2 = bf16[64,1024]{1,0:T(8,128)(2,1)S(1)} collective-permute-done((bf16[64,1024]{1,0:T(8,128)(2,1)S(1)}, bf16[64,1024]{1,0:T(8,128)(2,1)S(1)}, u32[]{:S(2)}, u32[]{:S(2)}) %collective-permute-start.2) | collective-permute-done | bytes 131104 | tf_op jit(solution)/shard_map/ppermute | solution.py:330
  6.0 1.3 %collective-permute-start.3 = (bf16[64,1024]{1,0:T(8,128)(2,1)S(1)}, bf16[64,1024]{1,0:T(8,128)(2,1)S(1)}, u32[]{:S(2)}, u32[]{:S(2)}) collective-permute-start(bf16[64,1024]{1,0:T(8,128)(2,1)S(1)} %add.87), channel_id=1, source_target_pairs={{0,2},{1,3},{2,0},{3,1},{4,6},{5,7},{6,4},{7,5},{8,10},{9,11},{10,... | collective-permute-start | bytes 393224 | tf_op jit(solution)/shard_map/ppermute | solution.py:330
  7.5 1.2 %collective-permute-start.5 = (bf16[64,1024]{1,0:T(8,128)(2,1)S(1)}, bf16[64,1024]{1,0:T(8,128)(2,1)S(1)}, u32[]{:S(2)}, u32[]{:S(2)}) collective-permute-start(bf16[64,1024]{1,0:T(8,128)(2,1)S(1)} %add.87), channel_id=1, source_target_pairs={{0,6},{1,7},{2,4},{3,5},{4,2},{5,3},{6,0},{7,1},{8,14},{9,15},{10,... | collective-permute-start | bytes 393224 | tf_op jit(solution)/shard_map/ppermute | solution.py:330
  8.9 1.4 %shard_map.78 = (bf16[128,3072]{1,0:T(8,128)(2,1)S(1)}, bf16[128,3072]{1,0:T(8,128)(2,1)S(1)}) custom-call(bf16[128,3072]{1,0:T(8,128)(2,1)} %bitcast.7, bf16[128,3072]{1,0:T(8,128)(2,1)} %b_ref.1), custom_call_target="tpu_custom_call" | custom-call | flops 10000000 | bytes 20000 | tf_op jit(solution)/shard_map/pallas_call | solution.py:38
  10.3 0.6 %collective-permute-done.3 = bf16[64,1024]{1,0:T(8,128)(2,1)S(1)} collective-permute-done((bf16[64,1024]{1,0:T(8,128)(2,1)S(1)}, bf16[64,1024]{1,0:T(8,128)(2,1)S(1)}, u32[]{:S(2)}, u32[]{:S(2)}) %collective-permute-start.3) | collective-permute-done | bytes 131104 | tf_op jit(solution)/shard_map/ppermute | solution.py:330
  10.9 4.2 %collective-permute-start.1 = (bf16[128,1024]{1,0:T(8,128)(2,1)S(1)}, bf16[128,1024]{1,0:T(8,128)(2,1)S(1)}, u32[]{:S(2)}, u32[]{:S(2)}) collective-permute-start(bf16[128,1024]{1,0:T(8,128)(2,1)S(1)} %get-tuple-element.25.own_ref), channel_id=1, source_target_pairs={{1,2},{3,4},{5,6},{7,8},{9,10},{11,12},{13,14},{2,1},{4,3},{6,5},{... | collective-permute-start | bytes 786440 | tf_op jit(solution)/shard_map/ppermute | solution.py:330
  15.1 1.4 %collective-permute-start.6 = (bf16[64,1024]{1,0:T(8,128)(2,1)S(1)}, bf16[64,1024]{1,0:T(8,128)(2,1)S(1)}, u32[]{:S(2)}, u32[]{:S(2)}) collective-permute-start(bf16[64,1024]{1,0:T(8,128)(2,1)S(1)} %add_add_fusion), channel_id=1, source_target_pairs={{0,12},{1,13},{2,14},{3,15},{4,8},{5,9},{6,10},{7,11},{8,4},{9,5},... | collective-permute-start | bytes 393224 | tf_op jit(solution)/shard_map/ppermute | solution.py:330
  16.5 1.6 %shard_map.79 = (f32[4,256,768]{2,1,0:T(8,128)S(1)}, f32[4,8,768]{2,1,0:T(8,128)S(1)}) custom-call(f32[2,24]{1,0:T(2,128)S(1)} %reshape.96.bias_ref, bf16[128,3072]{1,0:T(8,128)(2,1)S(1)} %get-tuple-element.28.q_ref, bf16[128,1024]{1,0:T(8,128)(2,1)S(1)} %get-tuple-element.25.own_ref, bf16[128,1024]{1,0:T(8,128)(2,1)S(1)} %collective-permute-done.on_ref), custom_call_target="tpu_custom_call" | custom-call | flops 2000000000 | bytes 4000000 | tf_op jit(solution)/shard_map/pallas_call | solution.py:38
  18.1 3.8 %collective-permute-done.1.off_ref = bf16[128,1024]{1,0:T(8,128)(2,1)S(1)} collective-permute-done((bf16[128,1024]{1,0:T(8,128)(2,1)S(1)}, bf16[128,1024]{1,0:T(8,128)(2,1)S(1)}, u32[]{:S(2)}, u32[]{:S(2)}) %collective-permute-start.1) | collective-permute-done | bytes 262176 | tf_op jit(solution)/shard_map/ppermute | solution.py:330
  21.9 1.2 %shard_map.80 = (f32[4,128,768]{2,1,0:T(8,128)S(1)}, f32[4,8,768]{2,1,0:T(8,128)S(1)}) custom-call(f32[2,24]{1,0:T(2,128)S(1)} %reshape.96.bias_ref, bf16[128,3072]{1,0:T(8,128)(2,1)S(1)} %get-tuple-element.28.q_ref, bf16[128,1024]{1,0:T(8,128)(2,1)S(1)} %collective-permute-done.1.off_ref, f32[4,8,768]{2,1,0:T(8,128)S(1)} %get-tuple-element.31.stat_ref), custom_call_target="tpu_custom_call" | custom-call | flops 1000000000 | bytes 2000000 | tf_op jit(solution)/shard_map/pallas_call | solution.py:38
  23.1 2.8 %collective-permute-start.7 = (bf16[64,1024]{1,0:T(8,128)(2,1)S(1)}, bf16[64,1024]{1,0:T(8,128)(2,1)S(1)}, u32[]{:S(2)}, u32[]{:S(2)}) collective-permute-start(bf16[64,1024]{1,0:T(8,128)(2,1)S(1)} %add.91.held_ref), channel_id=1, source_target_pairs={{0,1},{1,0},{2,3},{3,2},{4,5},{5,4},{6,7},{7,6},{8,9},{9,8},{10,11... | collective-permute-start | bytes 393224 | tf_op jit(solution)/shard_map/ppermute | solution.py:330
  25.9 0.9 %shard_map.81 = (f32[4,256,768]{2,1,0:T(8,128)S(1)}, f32[4,128,768]{2,1,0:T(8,128)S(1)}, f32[4,8,768]{2,1,0:T(8,128)S(1)}, bf16[128,3072]{1,0:T(8,128)(2,1)S(1)}) custom-call(bf16[128,3072]{1,0:T(8,128)(2,1)S(1)} %collective-permute-done.8.shifted_ref, bf16[128,3072]{1,0:T(8,128)(2,1)S(1)} %get-tuple-element.29.loss_ref, ...), custom_call_target="tpu_custom_call" | custom-call | flops 2000000000 | bytes 4000000 | tf_op jit(solution)/shard_map/pallas_call | solution.py:38
  26.9 1.6 %shard_map.82 = (bf16[4,128,768]{2,1,0:T(8,128)(2,1)S(1)}, f32[4,8,768]{2,1,0:T(8,128)S(1)}, f32[2,64,512]{2,1,0:T(8,128)S(1)}, bf16[2,64,512]{2,1,0:T(8,128)(2,1)S(1)}) custom-call(bf16[128,3072]{1,0:T(8,128)(2,1)S(1)} %get-tuple-element.28.q_ref, bf16[128,3072]{1,0:T(8,128)(2,1)S(1)} %get-tuple-element.34.do_ref, bf16[64,1024]{1,0:T(8,128)(2,1)S(1)} %add.91.held_ref, ...), custom_call_target="tpu_custom_call" | custom-call | flops 2000000000 | bytes 4000000 | tf_op jit(solution)/shard_map/pallas_call | solution.py:38
  28.5 0.4 collective-permute-start.11
  29.0 1.0 %collective-permute-done.11 = bf16[2,64,512]{2,1,0:T(8,128)(2,1)S(1)} collective-permute-done((bf16[2,64,512]{2,1,0:T(8,128)(2,1)S(1)}, bf16[2,64,512]{2,1,0:T(8,128)(2,1)S(1)}, u32[]{:S(2)}, u32[]{:S(2)}) %collective-permute-start.11) | collective-permute-done | bytes 131104 | tf_op jit(solution)/shard_map/ppermute | solution.py:330
  30.0 0.7 %collective-permute-start.12 = (bf16[2,64,512]{2,1,0:T(8,128)(2,1)S(1)}, bf16[2,64,512]{2,1,0:T(8,128)(2,1)S(1)}, u32[]{:S(2)}, u32[]{:S(2)}) collective-permute-start(bf16[2,64,512]{2,1,0:T(8,128)(2,1)S(1)} %fusion), channel_id=1, source_target_pairs={{0,2},{1,3},{2,0},{3,1},{4,6},{5,7},{6,4},{7,5},{8,10},{9,11},{10,... | collective-permute-start | bytes 393224 | tf_op jit(solution)/shard_map/ppermute | solution.py:330
  30.7 2.0 %collective-permute-start.14 = (bf16[2,64,512]{2,1,0:T(8,128)(2,1)S(1)}, bf16[2,64,512]{2,1,0:T(8,128)(2,1)S(1)}, u32[]{:S(2)}, u32[]{:S(2)}) collective-permute-start(bf16[2,64,512]{2,1,0:T(8,128)(2,1)S(1)} %fusion), channel_id=1, source_target_pairs={{0,6},{1,7},{2,4},{3,5},{4,2},{5,3},{6,0},{7,1},{8,14},{9,15},{10,... | collective-permute-start | bytes 393224 | tf_op jit(solution)/shard_map/ppermute | solution.py:330
  32.7 2.0 %collective-permute-done.12 = bf16[2,64,512]{2,1,0:T(8,128)(2,1)S(1)} collective-permute-done((bf16[2,64,512]{2,1,0:T(8,128)(2,1)S(1)}, bf16[2,64,512]{2,1,0:T(8,128)(2,1)S(1)}, u32[]{:S(2)}, u32[]{:S(2)}) %collective-permute-start.12) | collective-permute-done | bytes 131104 | tf_op jit(solution)/shard_map/ppermute | solution.py:330
  34.7 0.6 %collective-permute-done.13 = bf16[2,64,512]{2,1,0:T(8,128)(2,1)S(1)} collective-permute-done((bf16[2,64,512]{2,1,0:T(8,128)(2,1)S(1)}, bf16[2,64,512]{2,1,0:T(8,128)(2,1)S(1)}, u32[]{:S(2)}, u32[]{:S(2)}) %collective-permute-start.13) | collective-permute-done | bytes 131104 | tf_op jit(solution)/shard_map/ppermute | solution.py:330
  35.3 3.1 %collective-permute-done.14 = bf16[2,64,512]{2,1,0:T(8,128)(2,1)S(1)} collective-permute-done((bf16[2,64,512]{2,1,0:T(8,128)(2,1)S(1)}, bf16[2,64,512]{2,1,0:T(8,128)(2,1)S(1)}, u32[]{:S(2)}, u32[]{:S(2)}) %collective-permute-start.14) | collective-permute-done | bytes 131104 | tf_op jit(solution)/shard_map/ppermute | solution.py:330
  38.5 1.0 %collective-permute-start.15 = (bf16[2,64,512]{2,1,0:T(8,128)(2,1)S(1)}, bf16[2,64,512]{2,1,0:T(8,128)(2,1)S(1)}, u32[]{:S(2)}, u32[]{:S(2)}) collective-permute-start(bf16[2,64,512]{2,1,0:T(8,128)(2,1)S(1)} %fusion.1), channel_id=1, source_target_pairs={{0,12},{1,13},{2,14},{3,15},{4,8},{5,9},{6,10},{7,11},{8,4},{9,5},... | collective-permute-start | bytes 393224 | tf_op jit(solution)/shard_map/ppermute | solution.py:330
  39.5 1.5 %shard_map.83 = (f32[2,128,512]{2,1,0:T(8,128)S(1)}, bf16[2,128,512]{2,1,0:T(8,128)(2,1)S(1)}, bf16[2,128,512]{2,1,0:T(8,128)(2,1)S(1)}, bf16[4,384,768]{2,1,0:T(8,128)(2,1)S(1)}) custom-call(bf16[128,3072]{1,0:T(8,128)(2,1)S(1)} %get-tuple-element.28.q_ref, bf16[128,3072]{1,0:T(8,128)(2,1)S(1)} %get-tuple-element.34.do_ref, ...), custom_call_target="tpu_custom_call" | custom-call | flops 3000000000 | bytes 6000000 | tf_op jit(solution)/shard_map/pallas_call | solution.py:38
  41.0 4.7 %collective-permute-start.10 = (bf16[2,128,512]{2,1,0:T(8,128)(2,1)S(1)}, bf16[2,128,512]{2,1,0:T(8,128)(2,1)S(1)}, u32[]{:S(2)}, u32[]{:S(2)}) collective-permute-start(bf16[2,128,512]{2,1,0:T(8,128)(2,1)S(1)} %get-tuple-element.43), channel_id=1, source_target_pairs={{1,2},{3,4},{5,6},{7,8},{9,10},{11,12},{13,14},{2,1},{4,3},{6,5},{... | collective-permute-start | bytes 786440 | tf_op jit(solution)/shard_map/ppermute | solution.py:330
  46.0 1.5 %collective-permute-start.16 = (bf16[2,64,512]{2,1,0:T(8,128)(2,1)S(1)}, bf16[2,64,512]{2,1,0:T(8,128)(2,1)S(1)}, u32[]{:S(2)}, u32[]{:S(2)}) collective-permute-start(bf16[2,64,512]{2,1,0:T(8,128)(2,1)S(1)} %add_convert_fusion.half_ref), channel_id=1, source_target_pairs={{0,1},{1,0},{2,3},{3,2},{4,5},{5,4},{6,7},{7,6},{8,9},{9,8},{10,11... | collective-permute-start | bytes 393224 | tf_op jit(solution)/shard_map/ppermute | solution.py:330
  47.5 1.6 %shard_map.84 = bf16[128,3072]{1,0:T(8,128)(2,1)} custom-call(bf16[128,1024]{1,0:T(8,128)(2,1)S(1)} %get-tuple-element.25.own_ref, bf16[128,1024]{1,0:T(8,128)(2,1)S(1)} %collective-permute-done.on_ref, bf16[128,1024]{1,0:T(8,128)(2,1)S(1)} %collective-permute-done.1.off_ref, bf16[64,1024]{1,0:T(8,128)(2,1)S(1)} %add.91.held_ref, ...), custom_call_target="tpu_custom_call" | custom-call | flops 2000000000 | bytes 4000000 | tf_op jit(solution)/shard_map/pallas_call | solution.py:38
  49.1 3.5 %collective-permute-done.10.r_off = bf16[2,128,512]{2,1,0:T(8,128)(2,1)S(1)} collective-permute-done((bf16[2,128,512]{2,1,0:T(8,128)(2,1)S(1)}, bf16[2,128,512]{2,1,0:T(8,128)(2,1)S(1)}, u32[]{:S(2)}, u32[]{:S(2)}) %collective-permute-start.10) | collective-permute-done | bytes 262176 | tf_op jit(solution)/shard_map/ppermute | solution.py:330
  52.6 1.3 %shard_map.86 = (f32[2,128,512]{2,1,0:T(8,128)S(1)}, bf16[128,1024]{1,0:T(8,128)(2,1)}) custom-call(s32[1,2]{1,0:T(1,128)S(1)} %shard_map.85.place_ref, f32[2,128,512]{2,1,0:T(8,128)S(1)} %get-tuple-element.41.g_own, bf16[2,128,512]{2,1,0:T(8,128)(2,1)S(1)} %collective-permute-done.9.r_on, bf16[2,128,512]{2,1,0:T(8,128)(2,1)S(1)} %collective-permute-done.10.r_off, ...), custom_call_target="tpu_custom_call" | custom-call | flops 1000000 | bytes 2000 | tf_op jit(solution)/shard_map/pallas_call | solution.py:38
  53.9 1.2 %shard_map.87 = bf16[128,1024]{1,0:T(8,128)(2,1)} custom-call(s32[1,2]{1,0:T(1,128)S(1)} %shard_map.85.place_ref, f32[2,128,512]{2,1,0:T(8,128)S(1)} %get-tuple-element.46.base_ref, bf16[2,64,512]{2,1,0:T(8,128)(2,1)S(1)} %collective-permute-done.16.half_ref, bf16[128,1024]{1,0:T(8,128)(2,1)} %get-tuple-element.47.in_ref), custom_call_target="tpu_custom_call", output_to_operand_aliasing={{}: (3, {})} | custom-call | flops 1000000 | bytes 2000 | tf_op jit(solution)/shard_map/pallas_call | solution.py:38
  (32 shorter events, 1.4 us)
Async XLA Ops:
  0.6 4.5 %copy-start = (s32[1,32,4,3]{1,2,3,0:T(4,128)S(1)}, s32[1,32,4,3]{1,2,3,0:T(4,128)}, u32[]{:S(2)}) copy-start(s32[1,32,4,3]{1,2,3,0:T(4,128)} %param.11) | copy-start | bytes 4612
  1.6 14.8 %collective-permute-start = (bf16[128,1024]{1,0:T(8,128)(2,1)S(1)}, bf16[128,1024]{1,0:T(8,128)(2,1)S(1)}, u32[]{:S(2)}, u32[]{:S(2)}) collective-permute-start(bf16[128,1024]{1,0:T(8,128)(2,1)S(1)} %get-tuple-element.25.own_ref), channel_id=1, source_target_pairs={{0,1},{1,0},{2,3},{3,2},{4,5},{5,4},{6,7},{7,6},{8,9},{9,8},{10,11... | collective-permute-start | bytes 786440 | tf_op jit(solution)/shard_map/ppermute | solution.py:330
  2.4 23.5 %collective-permute-start.8 = (bf16[128,3072]{1,0:T(8,128)(2,1)}, bf16[128,3072]{1,0:T(8,128)(2,1)S(1)}, u32[]{:S(2)}, u32[]{:S(2)}) collective-permute-start(bf16[128,3072]{1,0:T(8,128)(2,1)} %bitcast.10), channel_id=1, source_target_pairs={{16,0},{17,1},{18,2},{19,3},{20,4},{21,5},{22,6},{23,7},{24,8},{25... | collective-permute-start | bytes 2359304 | tf_op jit(solution)/shard_map/ppermute | solution.py:330
  4.6 1.4 %collective-permute-start.2 = (bf16[64,1024]{1,0:T(8,128)(2,1)S(1)}, bf16[64,1024]{1,0:T(8,128)(2,1)S(1)}, u32[]{:S(2)}, u32[]{:S(2)}) collective-permute-start(bf16[64,1024]{1,0:T(8,128)(2,1)S(1)} %get-tuple-element.27), channel_id=1, source_target_pairs={{0,1},{1,0},{2,3},{3,2},{4,5},{5,4},{6,7},{7,6},{8,9},{9,8},{10,11... | collective-permute-start | bytes 393224 | tf_op jit(solution)/shard_map/ppermute | solution.py:330
  6.0 4.8 %collective-permute-start.3 = (bf16[64,1024]{1,0:T(8,128)(2,1)S(1)}, bf16[64,1024]{1,0:T(8,128)(2,1)S(1)}, u32[]{:S(2)}, u32[]{:S(2)}) collective-permute-start(bf16[64,1024]{1,0:T(8,128)(2,1)S(1)} %add.87), channel_id=1, source_target_pairs={{0,2},{1,3},{2,0},{3,1},{4,6},{5,7},{6,4},{7,5},{8,10},{9,11},{10,... | collective-permute-start | bytes 393224 | tf_op jit(solution)/shard_map/ppermute | solution.py:330
  7.3 7.7 %collective-permute-start.4 = (bf16[64,1024]{1,0:T(8,128)(2,1)S(1)}, bf16[64,1024]{1,0:T(8,128)(2,1)S(1)}, u32[]{:S(2)}, u32[]{:S(2)}) collective-permute-start(bf16[64,1024]{1,0:T(8,128)(2,1)S(1)} %add.87), channel_id=1, source_target_pairs={{0,4},{1,5},{2,6},{3,7},{4,0},{5,1},{6,2},{7,3},{8,12},{9,13},{10,... | collective-permute-start | bytes 393224 | tf_op jit(solution)/shard_map/ppermute | solution.py:330
  7.5 7.5 %collective-permute-start.5 = (bf16[64,1024]{1,0:T(8,128)(2,1)S(1)}, bf16[64,1024]{1,0:T(8,128)(2,1)S(1)}, u32[]{:S(2)}, u32[]{:S(2)}) collective-permute-start(bf16[64,1024]{1,0:T(8,128)(2,1)S(1)} %add.87), channel_id=1, source_target_pairs={{0,6},{1,7},{2,4},{3,5},{4,2},{5,3},{6,0},{7,1},{8,14},{9,15},{10,... | collective-permute-start | bytes 393224 | tf_op jit(solution)/shard_map/ppermute | solution.py:330
  10.9 11.0 %collective-permute-start.1 = (bf16[128,1024]{1,0:T(8,128)(2,1)S(1)}, bf16[128,1024]{1,0:T(8,128)(2,1)S(1)}, u32[]{:S(2)}, u32[]{:S(2)}) collective-permute-start(bf16[128,1024]{1,0:T(8,128)(2,1)S(1)} %get-tuple-element.25.own_ref), channel_id=1, source_target_pairs={{1,2},{3,4},{5,6},{7,8},{9,10},{11,12},{13,14},{2,1},{4,3},{6,5},{... | collective-permute-start | bytes 786440 | tf_op jit(solution)/shard_map/ppermute | solution.py:330
  15.1 8.0 %collective-permute-start.6 = (bf16[64,1024]{1,0:T(8,128)(2,1)S(1)}, bf16[64,1024]{1,0:T(8,128)(2,1)S(1)}, u32[]{:S(2)}, u32[]{:S(2)}) collective-permute-start(bf16[64,1024]{1,0:T(8,128)(2,1)S(1)} %add_add_fusion), channel_id=1, source_target_pairs={{0,12},{1,13},{2,14},{3,15},{4,8},{5,9},{6,10},{7,11},{8,4},{9,5},... | collective-permute-start | bytes 393224 | tf_op jit(solution)/shard_map/ppermute | solution.py:330
  23.1 3.8 %collective-permute-start.7 = (bf16[64,1024]{1,0:T(8,128)(2,1)S(1)}, bf16[64,1024]{1,0:T(8,128)(2,1)S(1)}, u32[]{:S(2)}, u32[]{:S(2)}) collective-permute-start(bf16[64,1024]{1,0:T(8,128)(2,1)S(1)} %add.91.held_ref), channel_id=1, source_target_pairs={{0,1},{1,0},{2,3},{3,2},{4,5},{5,4},{6,7},{7,6},{8,9},{9,8},{10,11... | collective-permute-start | bytes 393224 | tf_op jit(solution)/shard_map/ppermute | solution.py:330
  26.9 5.8 %copy-start.1 = (s32[1,2]{1,0:T(1,128)S(1)}, s32[1,2]{1,0:T(1,128)}, u32[]{:S(2)}) copy-start(s32[1,2]{1,0:T(1,128)} %ids_ref.3) | copy-start | bytes 28
  28.5 1.4 %collective-permute-start.11 = (bf16[2,64,512]{2,1,0:T(8,128)(2,1)S(1)}, bf16[2,64,512]{2,1,0:T(8,128)(2,1)S(1)}, u32[]{:S(2)}, u32[]{:S(2)}) collective-permute-start(bf16[2,64,512]{2,1,0:T(8,128)(2,1)S(1)} %get-tuple-element.45), channel_id=1, source_target_pairs={{0,1},{1,0},{2,3},{3,2},{4,5},{5,4},{6,7},{7,6},{8,9},{9,8},{10,11... | collective-permute-start | bytes 393224 | tf_op jit(solution)/shard_map/ppermute | solution.py:330
  30.0 4.8 %collective-permute-start.12 = (bf16[2,64,512]{2,1,0:T(8,128)(2,1)S(1)}, bf16[2,64,512]{2,1,0:T(8,128)(2,1)S(1)}, u32[]{:S(2)}, u32[]{:S(2)}) collective-permute-start(bf16[2,64,512]{2,1,0:T(8,128)(2,1)S(1)} %fusion), channel_id=1, source_target_pairs={{0,2},{1,3},{2,0},{3,1},{4,6},{5,7},{6,4},{7,5},{8,10},{9,11},{10,... | collective-permute-start | bytes 393224 | tf_op jit(solution)/shard_map/ppermute | solution.py:330
  30.7 4.6 %collective-permute-start.13 = (bf16[2,64,512]{2,1,0:T(8,128)(2,1)S(1)}, bf16[2,64,512]{2,1,0:T(8,128)(2,1)S(1)}, u32[]{:S(2)}, u32[]{:S(2)}) collective-permute-start(bf16[2,64,512]{2,1,0:T(8,128)(2,1)S(1)} %fusion), channel_id=1, source_target_pairs={{0,4},{1,5},{2,6},{3,7},{4,0},{5,1},{6,2},{7,3},{8,12},{9,13},{10,... | collective-permute-start | bytes 393224 | tf_op jit(solution)/shard_map/ppermute | solution.py:330
  30.7 7.8 %collective-permute-start.14 = (bf16[2,64,512]{2,1,0:T(8,128)(2,1)S(1)}, bf16[2,64,512]{2,1,0:T(8,128)(2,1)S(1)}, u32[]{:S(2)}, u32[]{:S(2)}) collective-permute-start(bf16[2,64,512]{2,1,0:T(8,128)(2,1)S(1)} %fusion), channel_id=1, source_target_pairs={{0,6},{1,7},{2,4},{3,5},{4,2},{5,3},{6,0},{7,1},{8,14},{9,15},{10,... | collective-permute-start | bytes 393224 | tf_op jit(solution)/shard_map/ppermute | solution.py:330
  38.5 7.4 %collective-permute-start.15 = (bf16[2,64,512]{2,1,0:T(8,128)(2,1)S(1)}, bf16[2,64,512]{2,1,0:T(8,128)(2,1)S(1)}, u32[]{:S(2)}, u32[]{:S(2)}) collective-permute-start(bf16[2,64,512]{2,1,0:T(8,128)(2,1)S(1)} %fusion.1), channel_id=1, source_target_pairs={{0,12},{1,13},{2,14},{3,15},{4,8},{5,9},{6,10},{7,11},{8,4},{9,5},... | collective-permute-start | bytes 393224 | tf_op jit(solution)/shard_map/ppermute | solution.py:330
  41.0 11.5 %collective-permute-start.10 = (bf16[2,128,512]{2,1,0:T(8,128)(2,1)S(1)}, bf16[2,128,512]{2,1,0:T(8,128)(2,1)S(1)}, u32[]{:S(2)}, u32[]{:S(2)}) collective-permute-start(bf16[2,128,512]{2,1,0:T(8,128)(2,1)S(1)} %get-tuple-element.43), channel_id=1, source_target_pairs={{1,2},{3,4},{5,6},{7,8},{9,10},{11,12},{13,14},{2,1},{4,3},{6,5},{... | collective-permute-start | bytes 786440 | tf_op jit(solution)/shard_map/ppermute | solution.py:330
  45.7 6.9 %collective-permute-start.9 = (bf16[2,128,512]{2,1,0:T(8,128)(2,1)S(1)}, bf16[2,128,512]{2,1,0:T(8,128)(2,1)S(1)}, u32[]{:S(2)}, u32[]{:S(2)}) collective-permute-start(bf16[2,128,512]{2,1,0:T(8,128)(2,1)S(1)} %get-tuple-element.42), channel_id=1, source_target_pairs={{0,1},{1,0},{2,3},{3,2},{4,5},{5,4},{6,7},{7,6},{8,9},{9,8},{10,11... | collective-permute-start | bytes 786440 | tf_op jit(solution)/shard_map/ppermute | solution.py:330
  46.0 7.9 %collective-permute-start.16 = (bf16[2,64,512]{2,1,0:T(8,128)(2,1)S(1)}, bf16[2,64,512]{2,1,0:T(8,128)(2,1)S(1)}, u32[]{:S(2)}, u32[]{:S(2)}) collective-permute-start(bf16[2,64,512]{2,1,0:T(8,128)(2,1)S(1)} %add_convert_fusion.half_ref), channel_id=1, source_target_pairs={{0,1},{1,0},{2,3},{3,2},{4,5},{5,4},{6,7},{7,6},{8,9},{9,8},{10,11... | collective-permute-start | bytes 393224 | tf_op jit(solution)/shard_map/ppermute | solution.py:330

commit v7 on v6

--- a/solution.py
+++ b/solution.py
@@ -88,20 +88,17 @@
     fetch_own = pltpu.make_async_copy(own_ref, own_out, sems.at[1])
     fetch_ids.start()
     fetch_own.start()
+    keep_ref[...] = jnp.zeros_like(keep_ref)
+    give_ref[...] = jnp.zeros_like(give_ref)
     fetch_ids.wait()
     fetch_own.wait()
     for which, out in ((core, keep_ref), (1 - core, give_ref)):
         block = ids[0, which]
-        mine = lax.div(block, nb) == pos
         row = pl.multiple_of(lax.rem(block, nb) * BLOCK_TOKENS, BLOCK_TOKENS)
 
-        @pl.when(mine)
+        @pl.when(lax.div(block, nb) == pos)
         def _(out=out, row=row):
             out[...] = own_out[pl.ds(row, BLOCK_TOKENS), :]
-
-        @pl.when(jnp.logical_not(mine))
-        def _(out=out):
-            out[...] = jnp.zeros_like(out)
 
 
 def listed_scores(s, bias_ref, e, first):

time: 55.4 us -> 55.3 us (level)
  no operation moved by 1% of the time
where the time goes in v7:
time: 55.3 us; the launch traced here: 55.1 us
  starting transfers between devices  24.7 us (45%)
  waiting for transfers between devices  15.5 us (28%)
  Pallas kernels  13.3 us (24%)
  between operations  0.8 us (1%)
  other arithmetic  0.59 us (1%)
    ppermute x17, starting transfers between devices, exchange(): return lax.ppermute(x, axis, pairs)  24.7 us
    ppermute x17, waiting for transfers between devices, exchange(): return lax.ppermute(x, axis, pairs)  15.5 us
    pallas_call x11, Pallas kernels, call(): pl.pallas_call(kernel, in_specs=ins, out_specs=out_specs or [VMEM] * len(...  13.3 us
  transfers between devices with their start and end apart: 17, of which 10 were waited for; matrix products, arithmetic and copies ran while one was open for 1% of the time, Pallas kernels for 17%

profile of v7, /device:TPU:11, one launch (start us, length us, event | category | flops | bytes accessed | tf_op | source)
XLA Modules:
  0.0 55.1 jit_solution(5154377869812688917)
XLA Ops:
  0.6 1.0 %shard_map.77 = (bf16[64,1024]{1,0:T(8,128)(2,1)S(1)}, bf16[64,1024]{1,0:T(8,128)(2,1)S(1)}, bf16[128,1024]{1,0:T(8,128)(2,1)S(1)}) custom-call(s32[1,2]{1,0:T(1,128)} %ids_ref.3, bf16[128,1024]{1,0:T(8,128)(2,1)} %bitcast.8), custom_call_target="tpu_custom_call" | custom-call | flops 1000000 | bytes 2000 | tf_op jit(solution)/shard_map/pallas_call | solution.py:38
  1.6 0.7 %collective-permute-start = (bf16[128,1024]{1,0:T(8,128)(2,1)S(1)}, bf16[128,1024]{1,0:T(8,128)(2,1)S(1)}, u32[]{:S(2)}, u32[]{:S(2)}) collective-permute-start(bf16[128,1024]{1,0:T(8,128)(2,1)S(1)} %get-tuple-element.25.own_ref), channel_id=1, source_target_pairs={{0,1},{1,0},{2,3},{3,2},{4,5},{5,4},{6,7},{7,6},{8,9},{9,8},{10,11... | collective-permute-start | bytes 786440 | tf_op jit(solution)/shard_map/ppermute | solution.py:327
  2.4 2.2 %collective-permute-start.8 = (bf16[128,3072]{1,0:T(8,128)(2,1)}, bf16[128,3072]{1,0:T(8,128)(2,1)S(1)}, u32[]{:S(2)}, u32[]{:S(2)}) collective-permute-start(bf16[128,3072]{1,0:T(8,128)(2,1)} %bitcast.10), channel_id=1, source_target_pairs={{16,0},{17,1},{18,2},{19,3},{20,4},{21,5},{22,6},{23,7},{24,8},{25... | collective-permute-start | bytes 2359304 | tf_op jit(solution)/shard_map/ppermute | solution.py:327
  4.6 0.4 collective-permute-start.2
  5.4 0.6 %collective-permute-done.2 = bf16[64,1024]{1,0:T(8,128)(2,1)S(1)} collective-permute-done((bf16[64,1024]{1,0:T(8,128)(2,1)S(1)}, bf16[64,1024]{1,0:T(8,128)(2,1)S(1)}, u32[]{:S(2)}, u32[]{:S(2)}) %collective-permute-start.2) | collective-permute-done | bytes 131104 | tf_op jit(solution)/shard_map/ppermute | solution.py:327
  6.0 1.3 %collective-permute-start.3 = (bf16[64,1024]{1,0:T(8,128)(2,1)S(1)}, bf16[64,1024]{1,0:T(8,128)(2,1)S(1)}, u32[]{:S(2)}, u32[]{:S(2)}) collective-permute-start(bf16[64,1024]{1,0:T(8,128)(2,1)S(1)} %add.87), channel_id=1, source_target_pairs={{0,2},{1,3},{2,0},{3,1},{4,6},{5,7},{6,4},{7,5},{8,10},{9,11},{10,... | collective-permute-start | bytes 393224 | tf_op jit(solution)/shard_map/ppermute | solution.py:327
  7.5 1.2 %collective-permute-start.5 = (bf16[64,1024]{1,0:T(8,128)(2,1)S(1)}, bf16[64,1024]{1,0:T(8,128)(2,1)S(1)}, u32[]{:S(2)}, u32[]{:S(2)}) collective-permute-start(bf16[64,1024]{1,0:T(8,128)(2,1)S(1)} %add.87), channel_id=1, source_target_pairs={{0,6},{1,7},{2,4},{3,5},{4,2},{5,3},{6,0},{7,1},{8,14},{9,15},{10,... | collective-permute-start | bytes 393224 | tf_op jit(solution)/shard_map/ppermute | solution.py:327
  8.8 1.4 %shard_map.78 = (bf16[128,3072]{1,0:T(8,128)(2,1)S(1)}, bf16[128,3072]{1,0:T(8,128)(2,1)S(1)}) custom-call(bf16[128,3072]{1,0:T(8,128)(2,1)} %bitcast.7, bf16[128,3072]{1,0:T(8,128)(2,1)} %b_ref.1), custom_call_target="tpu_custom_call" | custom-call | flops 10000000 | bytes 20000 | tf_op jit(solution)/shard_map/pallas_call | solution.py:38
  10.2 0.6 %collective-permute-done.3 = bf16[64,1024]{1,0:T(8,128)(2,1)S(1)} collective-permute-done((bf16[64,1024]{1,0:T(8,128)(2,1)S(1)}, bf16[64,1024]{1,0:T(8,128)(2,1)S(1)}, u32[]{:S(2)}, u32[]{:S(2)}) %collective-permute-start.3) | collective-permute-done | bytes 131104 | tf_op jit(solution)/shard_map/ppermute | solution.py:327
  10.8 4.2 %collective-permute-start.1 = (bf16[128,1024]{1,0:T(8,128)(2,1)S(1)}, bf16[128,1024]{1,0:T(8,128)(2,1)S(1)}, u32[]{:S(2)}, u32[]{:S(2)}) collective-permute-start(bf16[128,1024]{1,0:T(8,128)(2,1)S(1)} %get-tuple-element.25.own_ref), channel_id=1, source_target_pairs={{1,2},{3,4},{5,6},{7,8},{9,10},{11,12},{13,14},{2,1},{4,3},{6,5},{... | collective-permute-start | bytes 786440 | tf_op jit(solution)/shard_map/ppermute | solution.py:327
  15.1 1.4 %collective-permute-start.6 = (bf16[64,1024]{1,0:T(8,128)(2,1)S(1)}, bf16[64,1024]{1,0:T(8,128)(2,1)S(1)}, u32[]{:S(2)}, u32[]{:S(2)}) collective-permute-start(bf16[64,1024]{1,0:T(8,128)(2,1)S(1)} %add_add_fusion), channel_id=1, source_target_pairs={{0,12},{1,13},{2,14},{3,15},{4,8},{5,9},{6,10},{7,11},{8,4},{9,5},... | collective-permute-start | bytes 393224 | tf_op jit(solution)/shard_map/ppermute | solution.py:327
  16.5 1.6 %shard_map.79 = (f32[4,256,768]{2,1,0:T(8,128)S(1)}, f32[4,8,768]{2,1,0:T(8,128)S(1)}) custom-call(f32[2,24]{1,0:T(2,128)S(1)} %reshape.96.bias_ref, bf16[128,3072]{1,0:T(8,128)(2,1)S(1)} %get-tuple-element.28.q_ref, bf16[128,1024]{1,0:T(8,128)(2,1)S(1)} %get-tuple-element.25.own_ref, bf16[128,1024]{1,0:T(8,128)(2,1)S(1)} %collective-permute-done.on_ref), custom_call_target="tpu_custom_call" | custom-call | flops 2000000000 | bytes 4000000 | tf_op jit(solution)/shard_map/pallas_call | solution.py:38
  18.1 3.8 %collective-permute-done.1.off_ref = bf16[128,1024]{1,0:T(8,128)(2,1)S(1)} collective-permute-done((bf16[128,1024]{1,0:T(8,128)(2,1)S(1)}, bf16[128,1024]{1,0:T(8,128)(2,1)S(1)}, u32[]{:S(2)}, u32[]{:S(2)}) %collective-permute-start.1) | collective-permute-done | bytes 262176 | tf_op jit(solution)/shard_map/ppermute | solution.py:327
  21.9 1.2 %shard_map.80 = (f32[4,128,768]{2,1,0:T(8,128)S(1)}, f32[4,8,768]{2,1,0:T(8,128)S(1)}) custom-call(f32[2,24]{1,0:T(2,128)S(1)} %reshape.96.bias_ref, bf16[128,3072]{1,0:T(8,128)(2,1)S(1)} %get-tuple-element.28.q_ref, bf16[128,1024]{1,0:T(8,128)(2,1)S(1)} %collective-permute-done.1.off_ref, f32[4,8,768]{2,1,0:T(8,128)S(1)} %get-tuple-element.31.stat_ref), custom_call_target="tpu_custom_call" | custom-call | flops 1000000000 | bytes 2000000 | tf_op jit(solution)/shard_map/pallas_call | solution.py:38
  23.1 2.8 %collective-permute-start.7 = (bf16[64,1024]{1,0:T(8,128)(2,1)S(1)}, bf16[64,1024]{1,0:T(8,128)(2,1)S(1)}, u32[]{:S(2)}, u32[]{:S(2)}) collective-permute-start(bf16[64,1024]{1,0:T(8,128)(2,1)S(1)} %add.91.held_ref), channel_id=1, source_target_pairs={{0,1},{1,0},{2,3},{3,2},{4,5},{5,4},{6,7},{7,6},{8,9},{9,8},{10,11... | collective-permute-start | bytes 393224 | tf_op jit(solution)/shard_map/ppermute | solution.py:327
  25.9 0.9 %shard_map.81 = (f32[4,256,768]{2,1,0:T(8,128)S(1)}, f32[4,128,768]{2,1,0:T(8,128)S(1)}, f32[4,8,768]{2,1,0:T(8,128)S(1)}, bf16[128,3072]{1,0:T(8,128)(2,1)S(1)}) custom-call(bf16[128,3072]{1,0:T(8,128)(2,1)S(1)} %collective-permute-done.8.shifted_ref, bf16[128,3072]{1,0:T(8,128)(2,1)S(1)} %get-tuple-element.29.loss_ref, ...), custom_call_target="tpu_custom_call" | custom-call | flops 2000000000 | bytes 4000000 | tf_op jit(solution)/shard_map/pallas_call | solution.py:38
  26.9 1.6 %shard_map.82 = (bf16[4,128,768]{2,1,0:T(8,128)(2,1)S(1)}, f32[4,8,768]{2,1,0:T(8,128)S(1)}, f32[2,64,512]{2,1,0:T(8,128)S(1)}, bf16[2,64,512]{2,1,0:T(8,128)(2,1)S(1)}) custom-call(bf16[128,3072]{1,0:T(8,128)(2,1)S(1)} %get-tuple-element.28.q_ref, bf16[128,3072]{1,0:T(8,128)(2,1)S(1)} %get-tuple-element.34.do_ref, bf16[64,1024]{1,0:T(8,128)(2,1)S(1)} %add.91.held_ref, ...), custom_call_target="tpu_custom_call" | custom-call | flops 2000000000 | bytes 4000000 | tf_op jit(solution)/shard_map/pallas_call | solution.py:38
  28.5 0.4 collective-permute-start.11
  28.9 1.0 %collective-permute-done.11 = bf16[2,64,512]{2,1,0:T(8,128)(2,1)S(1)} collective-permute-done((bf16[2,64,512]{2,1,0:T(8,128)(2,1)S(1)}, bf16[2,64,512]{2,1,0:T(8,128)(2,1)S(1)}, u32[]{:S(2)}, u32[]{:S(2)}) %collective-permute-start.11) | collective-permute-done | bytes 131104 | tf_op jit(solution)/shard_map/ppermute | solution.py:327
  30.0 0.7 %collective-permute-start.12 = (bf16[2,64,512]{2,1,0:T(8,128)(2,1)S(1)}, bf16[2,64,512]{2,1,0:T(8,128)(2,1)S(1)}, u32[]{:S(2)}, u32[]{:S(2)}) collective-permute-start(bf16[2,64,512]{2,1,0:T(8,128)(2,1)S(1)} %fusion), channel_id=1, source_target_pairs={{0,2},{1,3},{2,0},{3,1},{4,6},{5,7},{6,4},{7,5},{8,10},{9,11},{10,... | collective-permute-start | bytes 393224 | tf_op jit(solution)/shard_map/ppermute | solution.py:327
  30.7 2.0 %collective-permute-start.14 = (bf16[2,64,512]{2,1,0:T(8,128)(2,1)S(1)}, bf16[2,64,512]{2,1,0:T(8,128)(2,1)S(1)}, u32[]{:S(2)}, u32[]{:S(2)}) collective-permute-start(bf16[2,64,512]{2,1,0:T(8,128)(2,1)S(1)} %fusion), channel_id=1, source_target_pairs={{0,6},{1,7},{2,4},{3,5},{4,2},{5,3},{6,0},{7,1},{8,14},{9,15},{10,... | collective-permute-start | bytes 393224 | tf_op jit(solution)/shard_map/ppermute | solution.py:327
  32.7 2.0 %collective-permute-done.12 = bf16[2,64,512]{2,1,0:T(8,128)(2,1)S(1)} collective-permute-done((bf16[2,64,512]{2,1,0:T(8,128)(2,1)S(1)}, bf16[2,64,512]{2,1,0:T(8,128)(2,1)S(1)}, u32[]{:S(2)}, u32[]{:S(2)}) %collective-permute-start.12) | collective-permute-done | bytes 131104 | tf_op jit(solution)/shard_map/ppermute | solution.py:327
  34.7 0.6 %collective-permute-done.13 = bf16[2,64,512]{2,1,0:T(8,128)(2,1)S(1)} collective-permute-done((bf16[2,64,512]{2,1,0:T(8,128)(2,1)S(1)}, bf16[2,64,512]{2,1,0:T(8,128)(2,1)S(1)}, u32[]{:S(2)}, u32[]{:S(2)}) %collective-permute-start.13) | collective-permute-done | bytes 131104 | tf_op jit(solution)/shard_map/ppermute | solution.py:327
  35.3 3.2 %collective-permute-done.14 = bf16[2,64,512]{2,1,0:T(8,128)(2,1)S(1)} collective-permute-done((bf16[2,64,512]{2,1,0:T(8,128)(2,1)S(1)}, bf16[2,64,512]{2,1,0:T(8,128)(2,1)S(1)}, u32[]{:S(2)}, u32[]{:S(2)}) %collective-permute-start.14) | collective-permute-done | bytes 131104 | tf_op jit(solution)/shard_map/ppermute | solution.py:327
  38.5 1.0 %collective-permute-start.15 = (bf16[2,64,512]{2,1,0:T(8,128)(2,1)S(1)}, bf16[2,64,512]{2,1,0:T(8,128)(2,1)S(1)}, u32[]{:S(2)}, u32[]{:S(2)}) collective-permute-start(bf16[2,64,512]{2,1,0:T(8,128)(2,1)S(1)} %fusion.1), channel_id=1, source_target_pairs={{0,12},{1,13},{2,14},{3,15},{4,8},{5,9},{6,10},{7,11},{8,4},{9,5},... | collective-permute-start | bytes 393224 | tf_op jit(solution)/shard_map/ppermute | solution.py:327
  39.5 1.5 %shard_map.83 = (f32[2,128,512]{2,1,0:T(8,128)S(1)}, bf16[2,128,512]{2,1,0:T(8,128)(2,1)S(1)}, bf16[2,128,512]{2,1,0:T(8,128)(2,1)S(1)}, bf16[4,384,768]{2,1,0:T(8,128)(2,1)S(1)}) custom-call(bf16[128,3072]{1,0:T(8,128)(2,1)S(1)} %get-tuple-element.28.q_ref, bf16[128,3072]{1,0:T(8,128)(2,1)S(1)} %get-tuple-element.34.do_ref, ...), custom_call_target="tpu_custom_call" | custom-call | flops 3000000000 | bytes 6000000 | tf_op jit(solution)/shard_map/pallas_call | solution.py:38
  41.0 4.7 %collective-permute-start.10 = (bf16[2,128,512]{2,1,0:T(8,128)(2,1)S(1)}, bf16[2,128,512]{2,1,0:T(8,128)(2,1)S(1)}, u32[]{:S(2)}, u32[]{:S(2)}) collective-permute-start(bf16[2,128,512]{2,1,0:T(8,128)(2,1)S(1)} %get-tuple-element.43), channel_id=1, source_target_pairs={{1,2},{3,4},{5,6},{7,8},{9,10},{11,12},{13,14},{2,1},{4,3},{6,5},{... | collective-permute-start | bytes 786440 | tf_op jit(solution)/shard_map/ppermute | solution.py:327
  46.0 1.5 %collective-permute-start.16 = (bf16[2,64,512]{2,1,0:T(8,128)(2,1)S(1)}, bf16[2,64,512]{2,1,0:T(8,128)(2,1)S(1)}, u32[]{:S(2)}, u32[]{:S(2)}) collective-permute-start(bf16[2,64,512]{2,1,0:T(8,128)(2,1)S(1)} %add_convert_fusion.half_ref), channel_id=1, source_target_pairs={{0,1},{1,0},{2,3},{3,2},{4,5},{5,4},{6,7},{7,6},{8,9},{9,8},{10,11... | collective-permute-start | bytes 393224 | tf_op jit(solution)/shard_map/ppermute | solution.py:327
  47.5 1.6 %shard_map.84 = bf16[128,3072]{1,0:T(8,128)(2,1)} custom-call(bf16[128,1024]{1,0:T(8,128)(2,1)S(1)} %get-tuple-element.25.own_ref, bf16[128,1024]{1,0:T(8,128)(2,1)S(1)} %collective-permute-done.on_ref, bf16[128,1024]{1,0:T(8,128)(2,1)S(1)} %collective-permute-done.1.off_ref, bf16[64,1024]{1,0:T(8,128)(2,1)S(1)} %add.91.held_ref, ...), custom_call_target="tpu_custom_call" | custom-call | flops 2000000000 | bytes 4000000 | tf_op jit(solution)/shard_map/pallas_call | solution.py:38
  49.1 3.5 %collective-permute-done.10.r_off = bf16[2,128,512]{2,1,0:T(8,128)(2,1)S(1)} collective-permute-done((bf16[2,128,512]{2,1,0:T(8,128)(2,1)S(1)}, bf16[2,128,512]{2,1,0:T(8,128)(2,1)S(1)}, u32[]{:S(2)}, u32[]{:S(2)}) %collective-permute-start.10) | collective-permute-done | bytes 262176 | tf_op jit(solution)/shard_map/ppermute | solution.py:327
  52.5 1.3 %shard_map.86 = (f32[2,128,512]{2,1,0:T(8,128)S(1)}, bf16[128,1024]{1,0:T(8,128)(2,1)}) custom-call(s32[1,2]{1,0:T(1,128)S(1)} %shard_map.85.place_ref, f32[2,128,512]{2,1,0:T(8,128)S(1)} %get-tuple-element.41.g_own, bf16[2,128,512]{2,1,0:T(8,128)(2,1)S(1)} %collective-permute-done.9.r_on, bf16[2,128,512]{2,1,0:T(8,128)(2,1)S(1)} %collective-permute-done.10.r_off, ...), custom_call_target="tpu_custom_call" | custom-call | flops 1000000 | bytes 2000 | tf_op jit(solution)/shard_map/pallas_call | solution.py:38
  53.9 1.2 %shard_map.87 = bf16[128,1024]{1,0:T(8,128)(2,1)} custom-call(s32[1,2]{1,0:T(1,128)S(1)} %shard_map.85.place_ref, f32[2,128,512]{2,1,0:T(8,128)S(1)} %get-tuple-element.46.base_ref, bf16[2,64,512]{2,1,0:T(8,128)(2,1)S(1)} %collective-permute-done.16.half_ref, bf16[128,1024]{1,0:T(8,128)(2,1)} %get-tuple-element.47.in_ref), custom_call_target="tpu_custom_call", output_to_operand_aliasing={{}: (3, {})} | custom-call | flops 1000000 | bytes 2000 | tf_op jit(solution)/shard_map/pallas_call | solution.py:38
  (32 shorter events, 1.4 us)
Async XLA Ops:
  0.6 4.5 %copy-start = (s32[1,32,4,3]{1,2,3,0:T(4,128)S(1)}, s32[1,32,4,3]{1,2,3,0:T(4,128)}, u32[]{:S(2)}) copy-start(s32[1,32,4,3]{1,2,3,0:T(4,128)} %param.11) | copy-start | bytes 4612
  1.6 14.8 %collective-permute-start = (bf16[128,1024]{1,0:T(8,128)(2,1)S(1)}, bf16[128,1024]{1,0:T(8,128)(2,1)S(1)}, u32[]{:S(2)}, u32[]{:S(2)}) collective-permute-start(bf16[128,1024]{1,0:T(8,128)(2,1)S(1)} %get-tuple-element.25.own_ref), channel_id=1, source_target_pairs={{0,1},{1,0},{2,3},{3,2},{4,5},{5,4},{6,7},{7,6},{8,9},{9,8},{10,11... | collective-permute-start | bytes 786440 | tf_op jit(solution)/shard_map/ppermute | solution.py:327
  2.4 23.5 %collective-permute-start.8 = (bf16[128,3072]{1,0:T(8,128)(2,1)}, bf16[128,3072]{1,0:T(8,128)(2,1)S(1)}, u32[]{:S(2)}, u32[]{:S(2)}) collective-permute-start(bf16[128,3072]{1,0:T(8,128)(2,1)} %bitcast.10), channel_id=1, source_target_pairs={{16,0},{17,1},{18,2},{19,3},{20,4},{21,5},{22,6},{23,7},{24,8},{25... | collective-permute-start | bytes 2359304 | tf_op jit(solution)/shard_map/ppermute | solution.py:327
  4.6 1.4 %collective-permute-start.2 = (bf16[64,1024]{1,0:T(8,128)(2,1)S(1)}, bf16[64,1024]{1,0:T(8,128)(2,1)S(1)}, u32[]{:S(2)}, u32[]{:S(2)}) collective-permute-start(bf16[64,1024]{1,0:T(8,128)(2,1)S(1)} %get-tuple-element.27), channel_id=1, source_target_pairs={{0,1},{1,0},{2,3},{3,2},{4,5},{5,4},{6,7},{7,6},{8,9},{9,8},{10,11... | collective-permute-start | bytes 393224 | tf_op jit(solution)/shard_map/ppermute | solution.py:327
  6.0 4.8 %collective-permute-start.3 = (bf16[64,1024]{1,0:T(8,128)(2,1)S(1)}, bf16[64,1024]{1,0:T(8,128)(2,1)S(1)}, u32[]{:S(2)}, u32[]{:S(2)}) collective-permute-start(bf16[64,1024]{1,0:T(8,128)(2,1)S(1)} %add.87), channel_id=1, source_target_pairs={{0,2},{1,3},{2,0},{3,1},{4,6},{5,7},{6,4},{7,5},{8,10},{9,11},{10,... | collective-permute-start | bytes 393224 | tf_op jit(solution)/shard_map/ppermute | solution.py:327
  7.3 7.7 %collective-permute-start.4 = (bf16[64,1024]{1,0:T(8,128)(2,1)S(1)}, bf16[64,1024]{1,0:T(8,128)(2,1)S(1)}, u32[]{:S(2)}, u32[]{:S(2)}) collective-permute-start(bf16[64,1024]{1,0:T(8,128)(2,1)S(1)} %add.87), channel_id=1, source_target_pairs={{0,4},{1,5},{2,6},{3,7},{4,0},{5,1},{6,2},{7,3},{8,12},{9,13},{10,... | collective-permute-start | bytes 393224 | tf_op jit(solution)/shard_map/ppermute | solution.py:327
  7.5 7.5 %collective-permute-start.5 = (bf16[64,1024]{1,0:T(8,128)(2,1)S(1)}, bf16[64,1024]{1,0:T(8,128)(2,1)S(1)}, u32[]{:S(2)}, u32[]{:S(2)}) collective-permute-start(bf16[64,1024]{1,0:T(8,128)(2,1)S(1)} %add.87), channel_id=1, source_target_pairs={{0,6},{1,7},{2,4},{3,5},{4,2},{5,3},{6,0},{7,1},{8,14},{9,15},{10,... | collective-permute-start | bytes 393224 | tf_op jit(solution)/shard_map/ppermute | solution.py:327
  10.8 11.0 %collective-permute-start.1 = (bf16[128,1024]{1,0:T(8,128)(2,1)S(1)}, bf16[128,1024]{1,0:T(8,128)(2,1)S(1)}, u32[]{:S(2)}, u32[]{:S(2)}) collective-permute-start(bf16[128,1024]{1,0:T(8,128)(2,1)S(1)} %get-tuple-element.25.own_ref), channel_id=1, source_target_pairs={{1,2},{3,4},{5,6},{7,8},{9,10},{11,12},{13,14},{2,1},{4,3},{6,5},{... | collective-permute-start | bytes 786440 | tf_op jit(solution)/shard_map/ppermute | solution.py:327
  15.1 8.0 %collective-permute-start.6 = (bf16[64,1024]{1,0:T(8,128)(2,1)S(1)}, bf16[64,1024]{1,0:T(8,128)(2,1)S(1)}, u32[]{:S(2)}, u32[]{:S(2)}) collective-permute-start(bf16[64,1024]{1,0:T(8,128)(2,1)S(1)} %add_add_fusion), channel_id=1, source_target_pairs={{0,12},{1,13},{2,14},{3,15},{4,8},{5,9},{6,10},{7,11},{8,4},{9,5},... | collective-permute-start | bytes 393224 | tf_op jit(solution)/shard_map/ppermute | solution.py:327
  23.1 3.8 %collective-permute-start.7 = (bf16[64,1024]{1,0:T(8,128)(2,1)S(1)}, bf16[64,1024]{1,0:T(8,128)(2,1)S(1)}, u32[]{:S(2)}, u32[]{:S(2)}) collective-permute-start(bf16[64,1024]{1,0:T(8,128)(2,1)S(1)} %add.91.held_ref), channel_id=1, source_target_pairs={{0,1},{1,0},{2,3},{3,2},{4,5},{5,4},{6,7},{7,6},{8,9},{9,8},{10,11... | collective-permute-start | bytes 393224 | tf_op jit(solution)/shard_map/ppermute | solution.py:327
  26.9 5.8 %copy-start.1 = (s32[1,2]{1,0:T(1,128)S(1)}, s32[1,2]{1,0:T(1,128)}, u32[]{:S(2)}) copy-start(s32[1,2]{1,0:T(1,128)} %ids_ref.3) | copy-start | bytes 28
  28.5 1.4 %collective-permute-start.11 = (bf16[2,64,512]{2,1,0:T(8,128)(2,1)S(1)}, bf16[2,64,512]{2,1,0:T(8,128)(2,1)S(1)}, u32[]{:S(2)}, u32[]{:S(2)}) collective-permute-start(bf16[2,64,512]{2,1,0:T(8,128)(2,1)S(1)} %get-tuple-element.45), channel_id=1, source_target_pairs={{0,1},{1,0},{2,3},{3,2},{4,5},{5,4},{6,7},{7,6},{8,9},{9,8},{10,11... | collective-permute-start | bytes 393224 | tf_op jit(solution)/shard_map/ppermute | solution.py:327
  30.0 4.8 %collective-permute-start.12 = (bf16[2,64,512]{2,1,0:T(8,128)(2,1)S(1)}, bf16[2,64,512]{2,1,0:T(8,128)(2,1)S(1)}, u32[]{:S(2)}, u32[]{:S(2)}) collective-permute-start(bf16[2,64,512]{2,1,0:T(8,128)(2,1)S(1)} %fusion), channel_id=1, source_target_pairs={{0,2},{1,3},{2,0},{3,1},{4,6},{5,7},{6,4},{7,5},{8,10},{9,11},{10,... | collective-permute-start | bytes 393224 | tf_op jit(solution)/shard_map/ppermute | solution.py:327
  30.6 4.6 %collective-permute-start.13 = (bf16[2,64,512]{2,1,0:T(8,128)(2,1)S(1)}, bf16[2,64,512]{2,1,0:T(8,128)(2,1)S(1)}, u32[]{:S(2)}, u32[]{:S(2)}) collective-permute-start(bf16[2,64,512]{2,1,0:T(8,128)(2,1)S(1)} %fusion), channel_id=1, source_target_pairs={{0,4},{1,5},{2,6},{3,7},{4,0},{5,1},{6,2},{7,3},{8,12},{9,13},{10,... | collective-permute-start | bytes 393224 | tf_op jit(solution)/shard_map/ppermute | solution.py:327
  30.7 7.8 %collective-permute-start.14 = (bf16[2,64,512]{2,1,0:T(8,128)(2,1)S(1)}, bf16[2,64,512]{2,1,0:T(8,128)(2,1)S(1)}, u32[]{:S(2)}, u32[]{:S(2)}) collective-permute-start(bf16[2,64,512]{2,1,0:T(8,128)(2,1)S(1)} %fusion), channel_id=1, source_target_pairs={{0,6},{1,7},{2,4},{3,5},{4,2},{5,3},{6,0},{7,1},{8,14},{9,15},{10,... | collective-permute-start | bytes 393224 | tf_op jit(solution)/shard_map/ppermute | solution.py:327
  38.5 7.4 %collective-permute-start.15 = (bf16[2,64,512]{2,1,0:T(8,128)(2,1)S(1)}, bf16[2,64,512]{2,1,0:T(8,128)(2,1)S(1)}, u32[]{:S(2)}, u32[]{:S(2)}) collective-permute-start(bf16[2,64,512]{2,1,0:T(8,128)(2,1)S(1)} %fusion.1), channel_id=1, source_target_pairs={{0,12},{1,13},{2,14},{3,15},{4,8},{5,9},{6,10},{7,11},{8,4},{9,5},... | collective-permute-start | bytes 393224 | tf_op jit(solution)/shard_map/ppermute | solution.py:327
  41.0 11.5 %collective-permute-start.10 = (bf16[2,128,512]{2,1,0:T(8,128)(2,1)S(1)}, bf16[2,128,512]{2,1,0:T(8,128)(2,1)S(1)}, u32[]{:S(2)}, u32[]{:S(2)}) collective-permute-start(bf16[2,128,512]{2,1,0:T(8,128)(2,1)S(1)} %get-tuple-element.43), channel_id=1, source_target_pairs={{1,2},{3,4},{5,6},{7,8},{9,10},{11,12},{13,14},{2,1},{4,3},{6,5},{... | collective-permute-start | bytes 786440 | tf_op jit(solution)/shard_map/ppermute | solution.py:327
  45.7 6.9 %collective-permute-start.9 = (bf16[2,128,512]{2,1,0:T(8,128)(2,1)S(1)}, bf16[2,128,512]{2,1,0:T(8,128)(2,1)S(1)}, u32[]{:S(2)}, u32[]{:S(2)}) collective-permute-start(bf16[2,128,512]{2,1,0:T(8,128)(2,1)S(1)} %get-tuple-element.42), channel_id=1, source_target_pairs={{0,1},{1,0},{2,3},{3,2},{4,5},{5,4},{6,7},{7,6},{8,9},{9,8},{10,11... | collective-permute-start | bytes 786440 | tf_op jit(solution)/shard_map/ppermute | solution.py:327
  46.0 7.9 %collective-permute-start.16 = (bf16[2,64,512]{2,1,0:T(8,128)(2,1)S(1)}, bf16[2,64,512]{2,1,0:T(8,128)(2,1)S(1)}, u32[]{:S(2)}, u32[]{:S(2)}) collective-permute-start(bf16[2,64,512]{2,1,0:T(8,128)(2,1)S(1)} %add_convert_fusion.half_ref), channel_id=1, source_target_pairs={{0,1},{1,0},{2,3},{3,2},{4,5},{5,4},{6,7},{7,6},{8,9},{9,8},{10,11... | collective-permute-start | bytes 393224 | tf_op jit(solution)/shard_map/ppermute | solution.py:327
